TPU v7x, 32 devices: a whole 2x2x4 slice. The times are simulated.
32 devices in a mesh: brick: 8 (over z, x), sub: 4 (over y, core).
Axes of the slice: x: 2, y: 2, z: 4, core: 2. Of those that a mesh axis runs over, the one named last changes fastest.
Arguments:
- psi: bfloat16 [128, 48, 2304], P(('brick', 'sub')), may hold values from -6 to 6
- potential: bfloat16 [128, 48, 2304], P(('brick', 'sub')), may hold values from -5 to 5
- offsets: int32 [128], P(('brick', 'sub')), may hold values from 0 to 255, as said below
- kernel: bfloat16 [128, 100], P(('brick', 'sub')), may hold values from -0.8984375 to 0.8984375
- multipliers: bfloat16 [128, 100], P(('brick', 'sub')), may hold values from -0.8984375 to 0.8984375
- pattern: int32 [128, 25], P(('brick', 'sub')), may hold values 0 or 1
Outputs:
- gradient: bfloat16 [128, 48, 2304], P(('brick', 'sub'))
- margin_band: float32 [128, 100], P(('brick', 'sub'))
- hamiltonian_band: float32 [128, 100], P(('brick', 'sub'))
Inputs may be any that keep to these rules, and one draw needn't show every extreme that they name: offsets[a] = (8 * (a // 4) + 8 / 2 - 48 / 2 + u) mod 256 with an integer u from -24 to 24; both ends are taken by some function.
All inputs are finite; a program needn't handle non-finite values. No bound on the sum of `pattern` on one device may be relied on, other than what follows from the above.
Results may differ from a plain program's by a relative error of at most 0.0059.
Values may be sent and summed in bfloat16 or wider, within the bound.
No kernel may reach another device: no remote copies, remote signals or barrier semaphores. Data moves between devices by JAX's collectives and lax.ppermute only.
A program may use at most 128 MiB of HBM per device.

v0:
```python
import math

import jax
import jax.numpy as jnp
from jax import lax
from jax.sharding import PartitionSpec as P

Q = 8
K = 6


filter_reach = 14


def shifted(block, axis, distance):
    devices = range(lax.axis_size(axis))
    route = [((i - distance) % len(devices), i) for i in devices]
    return lax.ppermute(block, axis, route)


def kinetic_matrix(edge_len):
    positions = jnp.arange(edge_len, dtype=jnp.int32)
    offset_gap = positions[:, None] - positions[None, :]
    distance = jnp.abs(offset_gap).astype(jnp.float32)
    parity_sign = 1.0 - 2.0 * (jnp.abs(offset_gap) % 2).astype(jnp.float32)
    off_diag = parity_sign / jnp.maximum(distance, 1.0) ** 2
    entries = jnp.where(offset_gap == 0, math.pi**2 / 6.0, off_diag)
    entries = jnp.where(jnp.abs(offset_gap) <= filter_reach, entries, 0.0)
    return entries.astype(jnp.bfloat16)


def cross_matrix(kinetic, edge_len):
    kin_float = kinetic.astype(jnp.float32)
    identity = jnp.eye(edge_len, dtype=jnp.float32)
    return (jnp.kron(kin_float, identity) + jnp.kron(identity, kin_float)).astype(jnp.bfloat16)


def apply_hamiltonian(psi, potential):
    fn_count, edge_len, plane_len = psi.shape
    kinetic = kinetic_matrix(edge_len)
    first_pass = jnp.einsum("wx,fxq->fwq", kinetic, psi, preferred_element_type=jnp.float32)
    cross = cross_matrix(kinetic, edge_len)
    second_pass = jnp.dot(
        psi.reshape(fn_count * edge_len, plane_len), cross, preferred_element_type=jnp.float32
    )
    summed = first_pass + second_pass.reshape(fn_count, edge_len, plane_len)
    result = summed + potential.astype(jnp.float32) * psi.astype(jnp.float32)
    return result.astype(jnp.bfloat16)


def embed(functions, region_start, window_len):

    def place(function, start_at):
        zeros_block = jnp.zeros((window_len, function.shape[1]), function.dtype)
        return lax.dynamic_update_slice_in_dim(zeros_block, function, start_at, 0)

    return jax.vmap(place)(functions, region_start)


def extract(window, region_start, edge_len):

    def take(planes, start_at):
        return lax.dynamic_slice_in_dim(planes, start_at, edge_len, 0)

    return jax.vmap(take)(window, region_start)


def dense_kernel(band_rows, group_count, band_reach, fn_count):
    dense_rows = []
    for slot_group in range(group_count):
        padded = jnp.pad(
            band_rows[slot_group], ((0, 0), (group_count * fn_count, group_count * fn_count))
        )
        first_col = (group_count + band_reach - slot_group) * fn_count
        dense_rows.append(padded[:, first_col : first_col + group_count * fn_count])
    return jnp.concatenate(dense_rows, axis=0)


def band_from_dense(dense, group_count, band_reach, fn_count):
    padded = jnp.pad(dense, ((0, 0), (band_reach * fn_count, band_reach * fn_count)))
    band_width = (2 * band_reach + 1) * fn_count
    pieces = []
    for slot_group in range(group_count):
        first_col = slot_group * fn_count
        pieces.append(padded[first_col : first_col + fn_count, first_col : first_col + band_width])
    return jnp.stack(pieces)


def grid_work(phi, hphi, kernel_rows, multi_rows, group_count, band_reach, fn_count, edge_len):
    volume_scale = 1.0 / float(edge_len**3)
    contract = (((1,), (1,)), ((), ()))
    margin = lax.dot_general(phi, phi, contract, preferred_element_type=jnp.float32) * volume_scale
    energy = lax.dot_general(phi, hphi, contract, preferred_element_type=jnp.float32) * volume_scale
    mixed = jnp.concatenate(
        [
            dense_kernel(kernel_rows, group_count, band_reach, fn_count),
            -dense_kernel(multi_rows, group_count, band_reach, fn_count),
        ],
        axis=1,
    )
    stacked = jnp.concatenate([hphi, phi], axis=0)
    grad = jnp.dot(mixed, stacked, preferred_element_type=jnp.float32).astype(jnp.bfloat16)
    margin_rows = band_from_dense(margin, group_count, band_reach, fn_count).astype(jnp.bfloat16)
    energy_rows = band_from_dense(energy, group_count, band_reach, fn_count).astype(jnp.bfloat16)
    return (grad, margin_rows, energy_rows)


def shards(psi, potential, offsets, kernel, multipliers, pattern):
    fn_count, edge_len, plane_len = psi.shape
    sub_count = lax.axis_size("sub")
    brick_count = lax.axis_size("brick")
    total_planes = Q * sub_count * brick_count
    band_reach = 2 * K
    band_width = kernel.shape[1]
    hpsi = apply_hamiltonian(psi, potential)
    spread = jnp.repeat(pattern, fn_count, axis=1).astype(jnp.bfloat16)
    kernel_eff = kernel * spread
    multi_eff = multipliers * spread
    margin_sum = jnp.zeros((fn_count, band_width), jnp.float32)
    energy_sum = jnp.zeros((fn_count, band_width), jnp.float32)
    my_rank = lax.axis_index("brick") * sub_count + lax.axis_index("sub")
    group_count = 2 * K + 1
    window_len = group_count * Q
    region_start = jnp.mod(offsets - (my_rank - K) * Q, total_planes)
    window_psi = embed(psi, region_start, window_len)
    window_hpsi = embed(hpsi, region_start, window_len)
    arrived = [None] * group_count
    for offset in range(-K, K + 1):
        first_plane = (offset + K) * Q
        payload = (
            window_psi[:, first_plane : first_plane + Q],
            window_hpsi[:, first_plane : first_plane + Q],
            kernel_eff,
            multi_eff,
        )
        if offset != 0:
            payload = shifted(
                (payload[0], payload[1], payload[2], payload[3]), ("brick", "sub"), offset
            )
        arrived[K - offset] = payload
    phi = jnp.concatenate([arrival[0] for arrival in arrived], axis=0).reshape(
        group_count * fn_count, Q * plane_len
    )
    hphi = jnp.concatenate([arrival[1] for arrival in arrived], axis=0).reshape(
        group_count * fn_count, Q * plane_len
    )
    kernel_rows = jnp.stack([arrival[2] for arrival in arrived])
    multi_rows = jnp.stack([arrival[3] for arrival in arrived])
    grad, margin_rows, energy_rows = grid_work(
        phi, hphi, kernel_rows, multi_rows, group_count, band_reach, fn_count, edge_len
    )
    grad = grad.reshape(group_count, fn_count, Q, plane_len)
    window = [None] * group_count
    for offset in range(-K, K + 1):
        slot_group = K - offset
        payload = (grad[slot_group], margin_rows[slot_group], energy_rows[slot_group])
        if offset != 0:
            payload = shifted((payload[0], payload[1], payload[2]), ("brick", "sub"), -offset)
        window[offset + K] = payload[0]
        margin_sum = margin_sum + payload[1].astype(jnp.float32)
        energy_sum = energy_sum + payload[2].astype(jnp.float32)
    gradient = extract(jnp.concatenate(window, axis=1), region_start, edge_len)
    return (gradient, margin_sum, energy_sum)


def solution(mesh):
    in_specs = (
        P(("brick", "sub"), None, None),
        P(("brick", "sub"), None, None),
        P(("brick", "sub")),
        P(("brick", "sub"), None),
        P(("brick", "sub"), None),
        P(("brick", "sub"), None),
    )
    out_specs = (
        P(("brick", "sub"), None, None),
        P(("brick", "sub"), None),
        P(("brick", "sub"), None),
    )
    return jax.shard_map(shards, mesh=mesh, in_specs=in_specs, out_specs=out_specs, check_vma=False)
```

profile of v0, /device:TPU:0, one launch (start us, length us, event | category | flops | bytes accessed | tf_op | source)
XLA Modules:
  0.0 338.1 jit_solution(2958094522870864891)
XLA Ops:
  2.3 3.9 %collective-permute-start.12 = (bf16[4,100]{1,0:T(4,128)(2,1)S(1)}, bf16[4,100]{1,0:T(4,128)(2,1)S(1)}, u32[]{:S(2)}, u32[]{:S(2)}) collective-permute-start(bf16[4,100]{1,0:T(4,128)(2,1)S(1)} %get-tuple-element.129), channel_id=1, source_target_pairs={{26,0},{27,1},{28,2},{29,3},{30,4},{31,5},{0,6},{1,7},{2,8},{3,9},... | collective-permute-start | bytes 2408 | tf_op jit(solution)/shard_map/ppermute | solution.py:18
  14.0 31.2 %while.3 = (s32[]{:T(128)}, bf16[4,104,2304]{2,1,0:T(8,128)(2,1)S(1)}, s32[4,3]{1,0:T(4,128)S(1)}, bf16[4,48,2304]{2,1,0:T(8,128)(2,1)S(1)}, s32[]{:T(128)}, /*index=5*/s32[3]{0:T(128)S(1)}, s32[]{:T(128)}) while((s32[]{:T(128)}, bf16[4,104,2304]{2,1,0:T(8,128)(2,1)S(1)}, s32[4,3]{1,0:T(4,128)S(1)}, bf16[4,48,2304]{2,1,0:T(8,128)(2,1)S(1)}, ...), condition=%wide.while_cond.1, body=%wide.while_body.1.sunk | while | flops 110611 | bytes 1106091 | solution.py:55
  14.6 2.7 and_reduce_fusion.5
  19.2 2.5 dynamic-update-slice.33
  22.4 2.7 and_reduce_fusion.5
  30.1 2.7 and_reduce_fusion.5
  34.8 2.5 dynamic-update-slice.33
  37.9 2.7 and_reduce_fusion.5
  42.6 2.5 dynamic-update-slice.33
  45.3 5.3 %collective-permute-start.18 = (bf16[4,100]{1,0:T(4,128)(2,1)S(1)}, bf16[4,100]{1,0:T(4,128)(2,1)S(1)}, u32[]{:S(2)}, u32[]{:S(2)}) collective-permute-start(bf16[4,100]{1,0:T(4,128)(2,1)S(1)} %get-tuple-element.129), channel_id=1, source_target_pairs={{1,0},{2,1},{3,2},{4,3},{5,4},{6,5},{7,6},{8,7},{9,8},{10,9},{11,1... | collective-permute-start | bytes 2408 | tf_op jit(solution)/shard_map/ppermute | solution.py:18
  51.3 10.2 %add_convert_fusion = bf16[48,48,48,48]{3,2,1,0:T(8,128)(2,1)} fusion(f32[48,48]{1,0:T(8,128)S(1)} %fusion.27, f32[48,48]{1,0:T(8,128)S(1)} %fusion.22), kind=kLoop, calls=%fused_computation.7 | loop fusion | flops 21233664 | bytes 10635264 | tf_op jit(solution)/shard_map/convert_element_type | solution.py:35
  61.5 38.7 %convert_element_type.212 = bf16[2304,2304]{1,0:T(8,128)(2,1)} reshape(bf16[48,48,48,48]{3,2,1,0:T(8,128)(2,1)} %add_convert_fusion) | data formatting | bytes 21233664 | tf_op jit(solution)/shard_map/convert_element_type | solution.py:35
  105.3 6.2 %fusion.47 = f32[2304,192]{0,1:T(8,128)S(1)} fusion(bf16[192,2304]{1,0:T(8,128)(2,1)S(1)} %bitcast.92, bf16[2304,2304]{1,0:T(8,128)(2,1)} %convert_element_type.212), kind=kOutput, calls=%fused_computation.110 | convolution fusion | flops 2038431744 | bytes 13271040 | tf_op jit(solution)/shard_map/dot_general | solution.py:43
  120.8 5.4 %collective-permute-start.6 = (bf16[4,100]{1,0:T(4,128)(2,1)S(1)}, bf16[4,100]{1,0:T(4,128)(2,1)S(1)}, u32[]{:S(2)}, u32[]{:S(2)}) collective-permute-start(bf16[4,100]{1,0:T(4,128)(2,1)S(1)} %get-tuple-element.128), channel_id=1, source_target_pairs={{1,0},{2,1},{3,2},{4,3},{5,4},{6,5},{7,6},{8,7},{9,8},{10,9},{11,1... | collective-permute-start | bytes 2408 | tf_op jit(solution)/shard_map/ppermute | solution.py:18
  129.7 3.0 collective-permute-start.11
  137.7 34.6 %while.2 = (s32[]{:T(128)}, bf16[4,104,2304]{2,1,0:T(8,128)(2,1)S(1)}, s32[4,3]{1,0:T(4,128)S(1)}, bf16[4,48,2304]{2,1,0:T(8,128)(2,1)}, s32[]{:T(128)}, /*index=5*/s32[3]{0:T(128)S(1)}, s32[]{:T(128)}) while((s32[]{:T(128)}, bf16[4,104,2304]{2,1,0:T(8,128)(2,1)S(1)}, s32[4,3]{1,0:T(4,128)S(1)}, bf16[4,48,2304]{2,1,0:T(8,128)(2,1)}, s32[]{:T(128)}, ...), condition=%wide.while_cond, body=%wide.while_body.sunk | while | flops 110611 | bytes 1106091 | solution.py:55
  138.4 2.6 and_reduce_fusion.4
  141.0 2.9 dynamic-slice_select_fusion.4
  147.1 2.6 and_reduce_fusion.4
  149.7 2.9 dynamic-slice_select_fusion.4
  155.7 2.6 and_reduce_fusion.4
  158.3 2.9 dynamic-slice_select_fusion.4
  164.4 2.6 and_reduce_fusion.4
  167.0 2.9 dynamic-slice_select_fusion.4
  173.2 3.0 collective-permute-start.40
  176.2 5.4 %collective-permute-start.42 = (bf16[4,8,2304]{2,0,1:T(4,128)(2,1)S(1)}, bf16[4,8,2304]{2,0,1:T(4,128)(2,1)S(1)}, u32[]{:S(2)}, u32[]{:S(2)}) collective-permute-start(bf16[4,8,2304]{2,0,1:T(4,128)(2,1)S(1)} %copy-done.12), channel_id=1, source_target_pairs={{1,0},{2,1},{3,2},{4,3},{5,4},{6,5},{7,6},{8,7},{9,8},{10,9},{11,1... | collective-permute-start | bytes 442376 | tf_op jit(solution)/shard_map/ppermute | solution.py:18
  185.8 2.7 collective-permute-start.47
  195.3 2.7 collective-permute-done.46
  201.2 4.2 %collective-permute-start.28 = (bf16[4,8,2304]{2,0,1:T(4,128)(2,1)}, bf16[4,8,2304]{2,0,1:T(4,128)(2,1)}, u32[]{:S(2)}, u32[]{:S(2)}) collective-permute-start(bf16[4,8,2304]{2,0,1:T(4,128)(2,1)} %get-tuple-element.86), channel_id=1, source_target_pairs={{30,0},{31,1},{0,2},{1,3},{2,4},{3,5},{4,6},{5,7},{6,8},{7,9},{8,1... | collective-permute-start | bytes 442376 | tf_op jit(solution)/shard_map/ppermute | solution.py:18
  205.5 5.3 %collective-permute-start.30 = (bf16[4,8,2304]{2,0,1:T(4,128)(2,1)}, bf16[4,8,2304]{2,0,1:T(4,128)(2,1)}, u32[]{:S(2)}, u32[]{:S(2)}) collective-permute-start(bf16[4,8,2304]{2,0,1:T(4,128)(2,1)} %get-tuple-element.83), channel_id=1, source_target_pairs={{1,0},{2,1},{3,2},{4,3},{5,4},{6,5},{7,6},{8,7},{9,8},{10,9},{11,1... | collective-permute-start | bytes 442376 | tf_op jit(solution)/shard_map/ppermute | solution.py:18
  212.9 4.2 %concatenate.26 = bf16[52,52]{1,0:T(8,128)(2,1)} concatenate(bf16[4,52]{1,0:T(4,128)(2,1)S(1)} %slice.364, bf16[4,52]{1,0:T(4,128)(2,1)S(1)} %slice.365, bf16[4,52]{1,0:T(4,128)(2,1)S(1)} %slice.366, bf16[4,52]{1,0:T(4,128)(2,1)S(1)} %slice.367, bf16[4,52]{1,0:T(4,128)(2,1)S(1)} %slice.368, bf16[4,52]{1,0:T(4,128)(2,1)S(1)} %slice.369, bf16[4,52]{1,0:T(4,128)(2,1)S(1)} %slice.370, ...), dimensions={0} | concatenate | bytes 10816 | tf_op jit(solution)/shard_map/concatenate | solution.py:76
  217.1 6.3 %concatenate.31 = bf16[52,8,2304]{2,0,1:T(8,128)(2,1)S(1)} concatenate(bf16[4,8,2304]{2,0,1:T(4,128)(2,1)S(1)} %collective-permute-done.36, bf16[4,8,2304]{2,0,1:T(4,128)(2,1)S(1)} %collective-permute-done.37, bf16[4,8,2304]{2,0,1:T(4,128)(2,1)S(1)} %collective-permute-done.38, bf16[4,8,2304]{2,0,1:T(4,128)(2,1)S(1)} %collective-permute-done.39, ...), dimensions={0} | concatenate | bytes 3833856 | tf_op jit(solution)/shard_map/concatenate | solution.py:141
  223.6 3.1 collective-permute-start.33
  231.2 3.2 collective-permute-done.33
  234.4 3.2 collective-permute-done.34
  237.5 2.6 collective-permute-done.35
  240.1 13.2 %concatenate.30 = bf16[52,8,2304]{2,0,1:T(8,128)(2,1)} concatenate(bf16[4,8,2304]{2,0,1:T(4,128)(2,1)S(1)} %collective-permute-done.24, bf16[4,8,2304]{2,0,1:T(4,128)(2,1)S(1)} %copy-done.4, bf16[4,8,2304]{2,0,1:T(4,128)(2,1)} %collective-permute-done.26, bf16[4,8,2304]{2,0,1:T(4,128)(2,1)} %collective-permute-done.27, bf16[4,8,2304]{2,0,1:T(4,128)(2,1)} %collective-permute-done.28, ...), dimensions={0} | concatenate | bytes 3833856 | tf_op jit(solution)/shard_map/concatenate | solution.py:144
  258.4 5.3 %collective-permute-start.75 = (bf16[4,100]{1,0:T(4,128)(2,1)S(1)}, bf16[4,100]{1,0:T(4,128)(2,1)S(1)}, u32[]{:S(2)}, u32[]{:S(2)}) collective-permute-start(bf16[4,100]{1,0:T(4,128)(2,1)S(1)} %get-tuple-element.112), channel_id=1, source_target_pairs={{29,0},{30,1},{31,2},{0,3},{1,4},{2,5},{3,6},{4,7},{5,8},{6,9},{7,... | collective-permute-start | bytes 2408 | tf_op jit(solution)/shard_map/ppermute | solution.py:18
  266.0 5.2 %collective-permute-start.78 = (bf16[4,100]{1,0:T(4,128)(2,1)S(1)}, bf16[4,100]{1,0:T(4,128)(2,1)S(1)}, u32[]{:S(2)}, u32[]{:S(2)}) collective-permute-start(bf16[4,100]{1,0:T(4,128)(2,1)S(1)} %get-tuple-element.109), channel_id=1, source_target_pairs={{1,0},{2,1},{3,2},{4,3},{5,4},{6,5},{7,6},{8,7},{9,8},{10,9},{11,1... | collective-permute-start | bytes 2408 | tf_op jit(solution)/shard_map/ppermute | solution.py:18
  274.4 2.9 collective-permute-start.83
  282.5 2.6 collective-permute-start.63
  286.8 5.4 %collective-permute-start.66 = (bf16[4,100]{1,0:T(4,128)(2,1)S(1)}, bf16[4,100]{1,0:T(4,128)(2,1)S(1)}, u32[]{:S(2)}, u32[]{:S(2)}) collective-permute-start(bf16[4,100]{1,0:T(4,128)(2,1)S(1)} %get-tuple-element.121), channel_id=1, source_target_pairs={{1,0},{2,1},{3,2},{4,3},{5,4},{6,5},{7,6},{8,7},{9,8},{10,9},{11,1... | collective-permute-start | bytes 2408 | tf_op jit(solution)/shard_map/ppermute | solution.py:18
  294.5 3.5 %collective-permute-start.71 = (bf16[4,100]{1,0:T(4,128)(2,1)S(1)}, bf16[4,100]{1,0:T(4,128)(2,1)S(1)}, u32[]{:S(2)}, u32[]{:S(2)}) collective-permute-start(bf16[4,100]{1,0:T(4,128)(2,1)S(1)} %get-tuple-element.127), channel_id=1, source_target_pairs={{6,0},{7,1},{8,2},{9,3},{10,4},{11,5},{12,6},{13,7},{14,8},{15,9},... | collective-permute-start | bytes 2408 | tf_op jit(solution)/shard_map/ppermute | solution.py:18
  301.2 2.6 collective-permute-start.51
  307.0 5.4 %collective-permute-start.54 = (bf16[4,8,2304]{2,0,1:T(4,128)(2,1)S(1)}, bf16[4,8,2304]{2,0,1:T(4,128)(2,1)S(1)}, u32[]{:S(2)}, u32[]{:S(2)}) collective-permute-start(bf16[4,8,2304]{2,0,1:T(4,128)(2,1)S(1)} %bitcast.100), channel_id=1, source_target_pairs={{1,0},{2,1},{3,2},{4,3},{5,4},{6,5},{7,6},{8,7},{9,8},{10,9},{11,1... | collective-permute-start | bytes 442376 | tf_op jit(solution)/shard_map/ppermute | solution.py:18
  315.0 4.7 %collective-permute-done.52 = bf16[4,8,2304]{2,0,1:T(4,128)(2,1)S(1)} collective-permute-done((bf16[4,8,2304]{2,0,1:T(4,128)(2,1)S(1)}, bf16[4,8,2304]{2,0,1:T(4,128)(2,1)S(1)}, u32[]{:S(2)}, u32[]{:S(2)}) %collective-permute-start.52) | collective-permute-done | bytes 147488 | tf_op jit(solution)/shard_map/ppermute | solution.py:18
  328.9 3.5 %collective-permute-done.59 = bf16[4,8,2304]{2,0,1:T(4,128)(2,1)S(1)} collective-permute-done((bf16[4,8,2304]{2,0,1:T(4,128)(2,1)S(1)}, bf16[4,8,2304]{2,0,1:T(4,128)(2,1)S(1)}, u32[]{:S(2)}, u32[]{:S(2)}) %collective-permute-start.59) | collective-permute-done | bytes 147488 | tf_op jit(solution)/shard_map/ppermute | solution.py:18
  332.5 4.6 %gather_fusion = bf16[4,48,2304]{2,0,1:T(4,128)(2,1)S(1)} fusion(bf16[4,104,2304]{2,0,1:T(4,128)(2,1)S(1)} %constant_dynamic-update-slice_fusion, s32[4]{0:T(128)S(1)} %copy-done.14), kind=kCustom, calls=%fused_computation | custom fusion | bytes 1769520 | tf_op jit(solution)/shard_map/vmap()/gather | solution.py:63
  (363 shorter events, 118.7 us)
Async XLA Ops:
  2.3 42.9 %collective-permute-start.12 = (bf16[4,100]{1,0:T(4,128)(2,1)S(1)}, bf16[4,100]{1,0:T(4,128)(2,1)S(1)}, u32[]{:S(2)}, u32[]{:S(2)}) collective-permute-start(bf16[4,100]{1,0:T(4,128)(2,1)S(1)} %get-tuple-element.129), channel_id=1, source_target_pairs={{26,0},{27,1},{28,2},{29,3},{30,4},{31,5},{0,6},{1,7},{2,8},{3,9},... | collective-permute-start | bytes 2408 | tf_op jit(solution)/shard_map/ppermute | solution.py:18
  6.2 39.0 %collective-permute-start.13 = (bf16[4,100]{1,0:T(4,128)(2,1)S(1)}, bf16[4,100]{1,0:T(4,128)(2,1)S(1)}, u32[]{:S(2)}, u32[]{:S(2)}) collective-permute-start(bf16[4,100]{1,0:T(4,128)(2,1)S(1)} %get-tuple-element.129), channel_id=1, source_target_pairs={{27,0},{28,1},{29,2},{30,3},{31,4},{0,5},{1,6},{2,7},{3,8},{4,9},{... | collective-permute-start | bytes 2408 | tf_op jit(solution)/shard_map/ppermute | solution.py:18
  7.0 43.6 %collective-permute-start.14 = (bf16[4,100]{1,0:T(4,128)(2,1)S(1)}, bf16[4,100]{1,0:T(4,128)(2,1)S(1)}, u32[]{:S(2)}, u32[]{:S(2)}) collective-permute-start(bf16[4,100]{1,0:T(4,128)(2,1)S(1)} %get-tuple-element.129), channel_id=1, source_target_pairs={{28,0},{29,1},{30,2},{31,3},{0,4},{1,5},{2,6},{3,7},{4,8},{5,9},{6... | collective-permute-start | bytes 2408 | tf_op jit(solution)/shard_map/ppermute | solution.py:18
  8.4 91.7 %collective-permute-start.15 = (bf16[4,100]{1,0:T(4,128)(2,1)S(1)}, bf16[4,100]{1,0:T(4,128)(2,1)S(1)}, u32[]{:S(2)}, u32[]{:S(2)}) collective-permute-start(bf16[4,100]{1,0:T(4,128)(2,1)S(1)} %get-tuple-element.129), channel_id=1, source_target_pairs={{29,0},{30,1},{31,2},{0,3},{1,4},{2,5},{3,6},{4,7},{5,8},{6,9},{7,... | collective-permute-start | bytes 2408 | tf_op jit(solution)/shard_map/ppermute | solution.py:18
  10.3 89.9 %collective-permute-start.16 = (bf16[4,100]{1,0:T(4,128)(2,1)S(1)}, bf16[4,100]{1,0:T(4,128)(2,1)S(1)}, u32[]{:S(2)}, u32[]{:S(2)}) collective-permute-start(bf16[4,100]{1,0:T(4,128)(2,1)S(1)} %get-tuple-element.129), channel_id=1, source_target_pairs={{30,0},{31,1},{0,2},{1,3},{2,4},{3,5},{4,6},{5,7},{6,8},{7,9},{8,1... | collective-permute-start | bytes 2408 | tf_op jit(solution)/shard_map/ppermute | solution.py:18
  45.2 56.0 %collective-permute-start.17 = (bf16[4,100]{1,0:T(4,128)(2,1)S(1)}, bf16[4,100]{1,0:T(4,128)(2,1)S(1)}, u32[]{:S(2)}, u32[]{:S(2)}) collective-permute-start(bf16[4,100]{1,0:T(4,128)(2,1)S(1)} %get-tuple-element.129), channel_id=1, source_target_pairs={{31,0},{0,1},{1,2},{2,3},{3,4},{4,5},{5,6},{6,7},{7,8},{8,9},{9,10... | collective-permute-start | bytes 2408 | tf_op jit(solution)/shard_map/ppermute | solution.py:18
  45.3 56.8 %collective-permute-start.18 = (bf16[4,100]{1,0:T(4,128)(2,1)S(1)}, bf16[4,100]{1,0:T(4,128)(2,1)S(1)}, u32[]{:S(2)}, u32[]{:S(2)}) collective-permute-start(bf16[4,100]{1,0:T(4,128)(2,1)S(1)} %get-tuple-element.129), channel_id=1, source_target_pairs={{1,0},{2,1},{3,2},{4,3},{5,4},{6,5},{7,6},{8,7},{9,8},{10,9},{11,1... | collective-permute-start | bytes 2408 | tf_op jit(solution)/shard_map/ppermute | solution.py:18
  50.6 53.8 %collective-permute-start.19 = (bf16[4,100]{1,0:T(4,128)(2,1)S(1)}, bf16[4,100]{1,0:T(4,128)(2,1)S(1)}, u32[]{:S(2)}, u32[]{:S(2)}) collective-permute-start(bf16[4,100]{1,0:T(4,128)(2,1)S(1)} %get-tuple-element.129), channel_id=1, source_target_pairs={{2,0},{3,1},{4,2},{5,3},{6,4},{7,5},{8,6},{9,7},{10,8},{11,9},{12,... | collective-permute-start | bytes 2408 | tf_op jit(solution)/shard_map/ppermute | solution.py:18
  100.2 12.2 %collective-permute-start.20 = (bf16[4,100]{1,0:T(4,128)(2,1)S(1)}, bf16[4,100]{1,0:T(4,128)(2,1)S(1)}, u32[]{:S(2)}, u32[]{:S(2)}) collective-permute-start(bf16[4,100]{1,0:T(4,128)(2,1)S(1)} %get-tuple-element.129), channel_id=1, source_target_pairs={{3,0},{4,1},{5,2},{6,3},{7,4},{8,5},{9,6},{10,7},{11,8},{12,9},{13... | collective-permute-start | bytes 2408 | tf_op jit(solution)/shard_map/ppermute | solution.py:18
  100.2 13.3 %collective-permute-start.21 = (bf16[4,100]{1,0:T(4,128)(2,1)S(1)}, bf16[4,100]{1,0:T(4,128)(2,1)S(1)}, u32[]{:S(2)}, u32[]{:S(2)}) collective-permute-start(bf16[4,100]{1,0:T(4,128)(2,1)S(1)} %get-tuple-element.129), channel_id=1, source_target_pairs={{4,0},{5,1},{6,2},{7,3},{8,4},{9,5},{10,6},{11,7},{12,8},{13,9},{1... | collective-permute-start | bytes 2408 | tf_op jit(solution)/shard_map/ppermute | solution.py:18
  101.2 13.7 %collective-permute-start.22 = (bf16[4,100]{1,0:T(4,128)(2,1)S(1)}, bf16[4,100]{1,0:T(4,128)(2,1)S(1)}, u32[]{:S(2)}, u32[]{:S(2)}) collective-permute-start(bf16[4,100]{1,0:T(4,128)(2,1)S(1)} %get-tuple-element.129), channel_id=1, source_target_pairs={{5,0},{6,1},{7,2},{8,3},{9,4},{10,5},{11,6},{12,7},{13,8},{14,9},{... | collective-permute-start | bytes 2408 | tf_op jit(solution)/shard_map/ppermute | solution.py:18
  102.0 15.0 %collective-permute-start.23 = (bf16[4,100]{1,0:T(4,128)(2,1)S(1)}, bf16[4,100]{1,0:T(4,128)(2,1)S(1)}, u32[]{:S(2)}, u32[]{:S(2)}) collective-permute-start(bf16[4,100]{1,0:T(4,128)(2,1)S(1)} %get-tuple-element.129), channel_id=1, source_target_pairs={{6,0},{7,1},{8,2},{9,3},{10,4},{11,5},{12,6},{13,7},{14,8},{15,9},... | collective-permute-start | bytes 2408 | tf_op jit(solution)/shard_map/ppermute | solution.py:18
  104.4 14.9 %collective-permute-start = (bf16[4,100]{1,0:T(4,128)(2,1)S(1)}, bf16[4,100]{1,0:T(4,128)(2,1)S(1)}, u32[]{:S(2)}, u32[]{:S(2)}) collective-permute-start(bf16[4,100]{1,0:T(4,128)(2,1)S(1)} %get-tuple-element.128), channel_id=1, source_target_pairs={{26,0},{27,1},{28,2},{29,3},{30,4},{31,5},{0,6},{1,7},{2,8},{3,9},... | collective-permute-start | bytes 2408 | tf_op jit(solution)/shard_map/ppermute | solution.py:18
  113.6 12.7 %collective-permute-start.2 = (bf16[4,100]{1,0:T(4,128)(2,1)S(1)}, bf16[4,100]{1,0:T(4,128)(2,1)S(1)}, u32[]{:S(2)}, u32[]{:S(2)}) collective-permute-start(bf16[4,100]{1,0:T(4,128)(2,1)S(1)} %get-tuple-element.128), channel_id=1, source_target_pairs={{28,0},{29,1},{30,2},{31,3},{0,4},{1,5},{2,6},{3,7},{4,8},{5,9},{6... | collective-permute-start | bytes 2408 | tf_op jit(solution)/shard_map/ppermute | solution.py:18
  114.9 11.3 %collective-permute-start.3 = (bf16[4,100]{1,0:T(4,128)(2,1)S(1)}, bf16[4,100]{1,0:T(4,128)(2,1)S(1)}, u32[]{:S(2)}, u32[]{:S(2)}) collective-permute-start(bf16[4,100]{1,0:T(4,128)(2,1)S(1)} %get-tuple-element.128), channel_id=1, source_target_pairs={{29,0},{30,1},{31,2},{0,3},{1,4},{2,5},{3,6},{4,7},{5,8},{6,9},{7,... | collective-permute-start | bytes 2408 | tf_op jit(solution)/shard_map/ppermute | solution.py:18
  129.7 43.5 %collective-permute-start.11 = (bf16[4,100]{1,0:T(4,128)(2,1)S(1)}, bf16[4,100]{1,0:T(4,128)(2,1)S(1)}, u32[]{:S(2)}, u32[]{:S(2)}) collective-permute-start(bf16[4,100]{1,0:T(4,128)(2,1)S(1)} %get-tuple-element.128), channel_id=1, source_target_pairs={{6,0},{7,1},{8,2},{9,3},{10,4},{11,5},{12,6},{13,7},{14,8},{15,9},... | collective-permute-start | bytes 2408 | tf_op jit(solution)/shard_map/ppermute | solution.py:18
  132.7 43.5 %collective-permute-start.36 = (bf16[4,8,2304]{2,0,1:T(4,128)(2,1)}, bf16[4,8,2304]{2,0,1:T(4,128)(2,1)S(1)}, u32[]{:S(2)}, u32[]{:S(2)}) collective-permute-start(bf16[4,8,2304]{2,0,1:T(4,128)(2,1)} %get-tuple-element.103), channel_id=1, source_target_pairs={{26,0},{27,1},{28,2},{29,3},{30,4},{31,5},{0,6},{1,7},{2,8},{3,9},... | collective-permute-start | bytes 442376 | tf_op jit(solution)/shard_map/ppermute | solution.py:18
  133.6 42.6 %collective-permute-start.37 = (bf16[4,8,2304]{2,0,1:T(4,128)(2,1)S(1)}, bf16[4,8,2304]{2,0,1:T(4,128)(2,1)S(1)}, u32[]{:S(2)}, u32[]{:S(2)}) collective-permute-start(bf16[4,8,2304]{2,0,1:T(4,128)(2,1)S(1)} %get-tuple-element.102), channel_id=1, source_target_pairs={{27,0},{28,1},{29,2},{30,3},{31,4},{0,5},{1,6},{2,7},{3,8},{4,9},{... | collective-permute-start | bytes 442376 | tf_op jit(solution)/shard_map/ppermute | solution.py:18
  134.7 46.9 %collective-permute-start.38 = (bf16[4,8,2304]{2,0,1:T(4,128)(2,1)}, bf16[4,8,2304]{2,0,1:T(4,128)(2,1)S(1)}, u32[]{:S(2)}, u32[]{:S(2)}) collective-permute-start(bf16[4,8,2304]{2,0,1:T(4,128)(2,1)} %get-tuple-element.101), channel_id=1, source_target_pairs={{28,0},{29,1},{30,2},{31,3},{0,4},{1,5},{2,6},{3,7},{4,8},{5,9},{6... | collective-permute-start | bytes 442376 | tf_op jit(solution)/shard_map/ppermute | solution.py:18
  136.0 45.6 %collective-permute-start.39 = (bf16[4,8,2304]{2,0,1:T(4,128)(2,1)}, bf16[4,8,2304]{2,0,1:T(4,128)(2,1)S(1)}, u32[]{:S(2)}, u32[]{:S(2)}) collective-permute-start(bf16[4,8,2304]{2,0,1:T(4,128)(2,1)} %get-tuple-element.100), channel_id=1, source_target_pairs={{29,0},{30,1},{31,2},{0,3},{1,4},{2,5},{3,6},{4,7},{5,8},{6,9},{7,... | collective-permute-start | bytes 442376 | tf_op jit(solution)/shard_map/ppermute | solution.py:18
  173.2 11.8 %collective-permute-start.40 = (bf16[4,8,2304]{2,0,1:T(4,128)(2,1)}, bf16[4,8,2304]{2,0,1:T(4,128)(2,1)S(1)}, u32[]{:S(2)}, u32[]{:S(2)}) collective-permute-start(bf16[4,8,2304]{2,0,1:T(4,128)(2,1)} %get-tuple-element.99), channel_id=1, source_target_pairs={{30,0},{31,1},{0,2},{1,3},{2,4},{3,5},{4,6},{5,7},{6,8},{7,9},{8,1... | collective-permute-start | bytes 442376 | tf_op jit(solution)/shard_map/ppermute | solution.py:18
  185.0 10.3 %collective-permute-start.45 = (bf16[4,8,2304]{2,0,1:T(4,128)(2,1)S(1)}, bf16[4,8,2304]{2,0,1:T(4,128)(2,1)S(1)}, u32[]{:S(2)}, u32[]{:S(2)}) collective-permute-start(bf16[4,8,2304]{2,0,1:T(4,128)(2,1)S(1)} %get-tuple-element.93), channel_id=1, source_target_pairs={{4,0},{5,1},{6,2},{7,3},{8,4},{9,5},{10,6},{11,7},{12,8},{13,9},{1... | collective-permute-start | bytes 442376 | tf_op jit(solution)/shard_map/ppermute | solution.py:18
  185.4 12.6 %collective-permute-start.46 = (bf16[4,8,2304]{2,0,1:T(4,128)(2,1)S(1)}, bf16[4,8,2304]{2,0,1:T(4,128)(2,1)S(1)}, u32[]{:S(2)}, u32[]{:S(2)}) collective-permute-start(bf16[4,8,2304]{2,0,1:T(4,128)(2,1)S(1)} %get-tuple-element.92), channel_id=1, source_target_pairs={{5,0},{6,1},{7,2},{8,3},{9,4},{10,5},{11,6},{12,7},{13,8},{14,9},{... | collective-permute-start | bytes 442376 | tf_op jit(solution)/shard_map/ppermute | solution.py:18
  185.8 15.4 %collective-permute-start.47 = (bf16[4,8,2304]{2,0,1:T(4,128)(2,1)S(1)}, bf16[4,8,2304]{2,0,1:T(4,128)(2,1)S(1)}, u32[]{:S(2)}, u32[]{:S(2)}) collective-permute-start(bf16[4,8,2304]{2,0,1:T(4,128)(2,1)S(1)} %get-tuple-element.91), channel_id=1, source_target_pairs={{6,0},{7,1},{8,2},{9,3},{10,4},{11,5},{12,6},{13,7},{14,8},{15,9},... | collective-permute-start | bytes 442376 | tf_op jit(solution)/shard_map/ppermute | solution.py:18
  191.1 14.4 %collective-permute-start.24 = (bf16[4,8,2304]{2,0,1:T(4,128)(2,1)S(1)}, bf16[4,8,2304]{2,0,1:T(4,128)(2,1)S(1)}, u32[]{:S(2)}, u32[]{:S(2)}) collective-permute-start(bf16[4,8,2304]{2,0,1:T(4,128)(2,1)S(1)} %get-tuple-element.90), channel_id=1, source_target_pairs={{26,0},{27,1},{28,2},{29,3},{30,4},{31,5},{0,6},{1,7},{2,8},{3,9},... | collective-permute-start | bytes 442376 | tf_op jit(solution)/shard_map/ppermute | solution.py:18
  192.8 12.7 %collective-permute-start.25 = (bf16[4,8,2304]{2,0,1:T(4,128)(2,1)S(1)}, bf16[4,8,2304]{2,0,1:T(4,128)(2,1)S(1)}, u32[]{:S(2)}, u32[]{:S(2)}) collective-permute-start(bf16[4,8,2304]{2,0,1:T(4,128)(2,1)S(1)} %get-tuple-element.89), channel_id=1, source_target_pairs={{27,0},{28,1},{29,2},{30,3},{31,4},{0,5},{1,6},{2,7},{3,8},{4,9},{... | collective-permute-start | bytes 442376 | tf_op jit(solution)/shard_map/ppermute | solution.py:18
  195.3 28.1 %collective-permute-start.26 = (bf16[4,8,2304]{2,0,1:T(4,128)(2,1)}, bf16[4,8,2304]{2,0,1:T(4,128)(2,1)}, u32[]{:S(2)}, u32[]{:S(2)}) collective-permute-start(bf16[4,8,2304]{2,0,1:T(4,128)(2,1)} %get-tuple-element.88), channel_id=1, source_target_pairs={{28,0},{29,1},{30,2},{31,3},{0,4},{1,5},{2,6},{3,7},{4,8},{5,9},{6... | collective-permute-start | bytes 442376 | tf_op jit(solution)/shard_map/ppermute | solution.py:18
  198.0 25.5 %collective-permute-start.27 = (bf16[4,8,2304]{2,0,1:T(4,128)(2,1)}, bf16[4,8,2304]{2,0,1:T(4,128)(2,1)}, u32[]{:S(2)}, u32[]{:S(2)}) collective-permute-start(bf16[4,8,2304]{2,0,1:T(4,128)(2,1)} %get-tuple-element.87), channel_id=1, source_target_pairs={{29,0},{30,1},{31,2},{0,3},{1,4},{2,5},{3,6},{4,7},{5,8},{6,9},{7,... | collective-permute-start | bytes 442376 | tf_op jit(solution)/shard_map/ppermute | solution.py:18
  201.2 22.4 %collective-permute-start.28 = (bf16[4,8,2304]{2,0,1:T(4,128)(2,1)}, bf16[4,8,2304]{2,0,1:T(4,128)(2,1)}, u32[]{:S(2)}, u32[]{:S(2)}) collective-permute-start(bf16[4,8,2304]{2,0,1:T(4,128)(2,1)} %get-tuple-element.86), channel_id=1, source_target_pairs={{30,0},{31,1},{0,2},{1,3},{2,4},{3,5},{4,6},{5,7},{6,8},{7,9},{8,1... | collective-permute-start | bytes 442376 | tf_op jit(solution)/shard_map/ppermute | solution.py:18
  205.5 21.2 %collective-permute-start.29 = (bf16[4,8,2304]{2,0,1:T(4,128)(2,1)}, bf16[4,8,2304]{2,0,1:T(4,128)(2,1)}, u32[]{:S(2)}, u32[]{:S(2)}) collective-permute-start(bf16[4,8,2304]{2,0,1:T(4,128)(2,1)} %get-tuple-element.85), channel_id=1, source_target_pairs={{31,0},{0,1},{1,2},{2,3},{3,4},{4,5},{5,6},{6,7},{7,8},{8,9},{9,10... | collective-permute-start | bytes 442376 | tf_op jit(solution)/shard_map/ppermute | solution.py:18
  205.5 21.3 %collective-permute-start.30 = (bf16[4,8,2304]{2,0,1:T(4,128)(2,1)}, bf16[4,8,2304]{2,0,1:T(4,128)(2,1)}, u32[]{:S(2)}, u32[]{:S(2)}) collective-permute-start(bf16[4,8,2304]{2,0,1:T(4,128)(2,1)} %get-tuple-element.83), channel_id=1, source_target_pairs={{1,0},{2,1},{3,2},{4,3},{5,4},{6,5},{7,6},{8,7},{9,8},{10,9},{11,1... | collective-permute-start | bytes 442376 | tf_op jit(solution)/shard_map/ppermute | solution.py:18
  223.6 10.8 %collective-permute-start.33 = (bf16[4,8,2304]{2,0,1:T(4,128)(2,1)}, bf16[4,8,2304]{2,0,1:T(4,128)(2,1)S(1)}, u32[]{:S(2)}, u32[]{:S(2)}) collective-permute-start(bf16[4,8,2304]{2,0,1:T(4,128)(2,1)} %get-tuple-element.80), channel_id=1, source_target_pairs={{4,0},{5,1},{6,2},{7,3},{8,4},{9,5},{10,6},{11,7},{12,8},{13,9},{1... | collective-permute-start | bytes 442376 | tf_op jit(solution)/shard_map/ppermute | solution.py:18
  226.7 10.9 %collective-permute-start.34 = (bf16[4,8,2304]{2,0,1:T(4,128)(2,1)}, bf16[4,8,2304]{2,0,1:T(4,128)(2,1)S(1)}, u32[]{:S(2)}, u32[]{:S(2)}) collective-permute-start(bf16[4,8,2304]{2,0,1:T(4,128)(2,1)} %get-tuple-element.79), channel_id=1, source_target_pairs={{5,0},{6,1},{7,2},{8,3},{9,4},{10,5},{11,6},{12,7},{13,8},{14,9},{... | collective-permute-start | bytes 442376 | tf_op jit(solution)/shard_map/ppermute | solution.py:18
  226.8 13.3 %collective-permute-start.35 = (bf16[4,8,2304]{2,0,1:T(4,128)(2,1)}, bf16[4,8,2304]{2,0,1:T(4,128)(2,1)S(1)}, u32[]{:S(2)}, u32[]{:S(2)}) collective-permute-start(bf16[4,8,2304]{2,0,1:T(4,128)(2,1)} %get-tuple-element.78), channel_id=1, source_target_pairs={{6,0},{7,1},{8,2},{9,3},{10,4},{11,5},{12,6},{13,7},{14,8},{15,9},... | collective-permute-start | bytes 442376 | tf_op jit(solution)/shard_map/ppermute | solution.py:18
  257.3 13.9 %collective-permute-start.74 = (bf16[4,100]{1,0:T(4,128)(2,1)S(1)}, bf16[4,100]{1,0:T(4,128)(2,1)S(1)}, u32[]{:S(2)}, u32[]{:S(2)}) collective-permute-start(bf16[4,100]{1,0:T(4,128)(2,1)S(1)} %get-tuple-element.113), channel_id=1, source_target_pairs={{28,0},{29,1},{30,2},{31,3},{0,4},{1,5},{2,6},{3,7},{4,8},{5,9},{6... | collective-permute-start | bytes 2408 | tf_op jit(solution)/shard_map/ppermute | solution.py:18
  258.4 15.7 %collective-permute-start.75 = (bf16[4,100]{1,0:T(4,128)(2,1)S(1)}, bf16[4,100]{1,0:T(4,128)(2,1)S(1)}, u32[]{:S(2)}, u32[]{:S(2)}) collective-permute-start(bf16[4,100]{1,0:T(4,128)(2,1)S(1)} %get-tuple-element.112), channel_id=1, source_target_pairs={{29,0},{30,1},{31,2},{0,3},{1,4},{2,5},{3,6},{4,7},{5,8},{6,9},{7,... | collective-permute-start | bytes 2408 | tf_op jit(solution)/shard_map/ppermute | solution.py:18
  263.7 10.5 %collective-permute-start.76 = (bf16[4,100]{1,0:T(4,128)(2,1)S(1)}, bf16[4,100]{1,0:T(4,128)(2,1)S(1)}, u32[]{:S(2)}, u32[]{:S(2)}) collective-permute-start(bf16[4,100]{1,0:T(4,128)(2,1)S(1)} %get-tuple-element.111), channel_id=1, source_target_pairs={{30,0},{31,1},{0,2},{1,3},{2,4},{3,5},{4,6},{5,7},{6,8},{7,9},{8,1... | collective-permute-start | bytes 2408 | tf_op jit(solution)/shard_map/ppermute | solution.py:18
  274.4 10.7 %collective-permute-start.83 = (bf16[4,100]{1,0:T(4,128)(2,1)S(1)}, bf16[4,100]{1,0:T(4,128)(2,1)S(1)}, u32[]{:S(2)}, u32[]{:S(2)}) collective-permute-start(bf16[4,100]{1,0:T(4,128)(2,1)S(1)} %get-tuple-element.115), channel_id=1, source_target_pairs={{6,0},{7,1},{8,2},{9,3},{10,4},{11,5},{12,6},{13,7},{14,8},{15,9},... | collective-permute-start | bytes 2408 | tf_op jit(solution)/shard_map/ppermute | solution.py:18
  280.5 11.7 %collective-permute-start.62 = (bf16[4,100]{1,0:T(4,128)(2,1)S(1)}, bf16[4,100]{1,0:T(4,128)(2,1)S(1)}, u32[]{:S(2)}, u32[]{:S(2)}) collective-permute-start(bf16[4,100]{1,0:T(4,128)(2,1)S(1)} %get-tuple-element.125), channel_id=1, source_target_pairs={{28,0},{29,1},{30,2},{31,3},{0,4},{1,5},{2,6},{3,7},{4,8},{5,9},{6... | collective-permute-start | bytes 2408 | tf_op jit(solution)/shard_map/ppermute | solution.py:18
  282.5 10.9 %collective-permute-start.63 = (bf16[4,100]{1,0:T(4,128)(2,1)S(1)}, bf16[4,100]{1,0:T(4,128)(2,1)S(1)}, u32[]{:S(2)}, u32[]{:S(2)}) collective-permute-start(bf16[4,100]{1,0:T(4,128)(2,1)S(1)} %get-tuple-element.124), channel_id=1, source_target_pairs={{29,0},{30,1},{31,2},{0,3},{1,4},{2,5},{3,6},{4,7},{5,8},{6,9},{7,... | collective-permute-start | bytes 2408 | tf_op jit(solution)/shard_map/ppermute | solution.py:18
  299.7 12.7 %collective-permute-start.50 = (bf16[4,8,2304]{2,0,1:T(4,128)(2,1)S(1)}, bf16[4,8,2304]{2,0,1:T(4,128)(2,1)S(1)}, u32[]{:S(2)}, u32[]{:S(2)}) collective-permute-start(bf16[4,8,2304]{2,0,1:T(4,128)(2,1)S(1)} %bitcast.104), channel_id=1, source_target_pairs={{28,0},{29,1},{30,2},{31,3},{0,4},{1,5},{2,6},{3,7},{4,8},{5,9},{6... | collective-permute-start | bytes 442376 | tf_op jit(solution)/shard_map/ppermute | solution.py:18
  301.2 11.7 %collective-permute-start.51 = (bf16[4,8,2304]{2,0,1:T(4,128)(2,1)S(1)}, bf16[4,8,2304]{2,0,1:T(4,128)(2,1)S(1)}, u32[]{:S(2)}, u32[]{:S(2)}) collective-permute-start(bf16[4,8,2304]{2,0,1:T(4,128)(2,1)S(1)} %bitcast.103), channel_id=1, source_target_pairs={{29,0},{30,1},{31,2},{0,3},{1,4},{2,5},{3,6},{4,7},{5,8},{6,9},{7,... | collective-permute-start | bytes 442376 | tf_op jit(solution)/shard_map/ppermute | solution.py:18
  303.7 16.0 %collective-permute-start.52 = (bf16[4,8,2304]{2,0,1:T(4,128)(2,1)S(1)}, bf16[4,8,2304]{2,0,1:T(4,128)(2,1)S(1)}, u32[]{:S(2)}, u32[]{:S(2)}) collective-permute-start(bf16[4,8,2304]{2,0,1:T(4,128)(2,1)S(1)} %bitcast.102), channel_id=1, source_target_pairs={{30,0},{31,1},{0,2},{1,3},{2,4},{3,5},{4,6},{5,7},{6,8},{7,9},{8,1... | collective-permute-start | bytes 442376 | tf_op jit(solution)/shard_map/ppermute | solution.py:18
  306.9 14.6 %collective-permute-start.53 = (bf16[4,8,2304]{2,0,1:T(4,128)(2,1)S(1)}, bf16[4,8,2304]{2,0,1:T(4,128)(2,1)S(1)}, u32[]{:S(2)}, u32[]{:S(2)}) collective-permute-start(bf16[4,8,2304]{2,0,1:T(4,128)(2,1)S(1)} %bitcast.101), channel_id=1, source_target_pairs={{31,0},{0,1},{1,2},{2,3},{3,4},{4,5},{5,6},{6,7},{7,8},{8,9},{9,10... | collective-permute-start | bytes 442376 | tf_op jit(solution)/shard_map/ppermute | solution.py:18
  307.0 14.7 %collective-permute-start.54 = (bf16[4,8,2304]{2,0,1:T(4,128)(2,1)S(1)}, bf16[4,8,2304]{2,0,1:T(4,128)(2,1)S(1)}, u32[]{:S(2)}, u32[]{:S(2)}) collective-permute-start(bf16[4,8,2304]{2,0,1:T(4,128)(2,1)S(1)} %bitcast.100), channel_id=1, source_target_pairs={{1,0},{2,1},{3,2},{4,3},{5,4},{6,5},{7,6},{8,7},{9,8},{10,9},{11,1... | collective-permute-start | bytes 442376 | tf_op jit(solution)/shard_map/ppermute | solution.py:18
  312.4 11.7 %collective-permute-start.55 = (bf16[4,8,2304]{2,0,1:T(4,128)(2,1)S(1)}, bf16[4,8,2304]{2,0,1:T(4,128)(2,1)S(1)}, u32[]{:S(2)}, u32[]{:S(2)}) collective-permute-start(bf16[4,8,2304]{2,0,1:T(4,128)(2,1)S(1)} %bitcast.99), channel_id=1, source_target_pairs={{2,0},{3,1},{4,2},{5,3},{6,4},{7,5},{8,6},{9,7},{10,8},{11,9},{12,... | collective-permute-start | bytes 442376 | tf_op jit(solution)/shard_map/ppermute | solution.py:18
  312.9 12.3 %collective-permute-start.56 = (bf16[4,8,2304]{2,0,1:T(4,128)(2,1)S(1)}, bf16[4,8,2304]{2,0,1:T(4,128)(2,1)S(1)}, u32[]{:S(2)}, u32[]{:S(2)}) collective-permute-start(bf16[4,8,2304]{2,0,1:T(4,128)(2,1)S(1)} %bitcast.98), channel_id=1, source_target_pairs={{3,0},{4,1},{5,2},{6,3},{7,4},{8,5},{9,6},{10,7},{11,8},{12,9},{13... | collective-permute-start | bytes 442376 | tf_op jit(solution)/shard_map/ppermute | solution.py:18
  321.7 10.8 %collective-permute-start.59 = (bf16[4,8,2304]{2,0,1:T(4,128)(2,1)S(1)}, bf16[4,8,2304]{2,0,1:T(4,128)(2,1)S(1)}, u32[]{:S(2)}, u32[]{:S(2)}) collective-permute-start(bf16[4,8,2304]{2,0,1:T(4,128)(2,1)S(1)} %bitcast.95), channel_id=1, source_target_pairs={{6,0},{7,1},{8,2},{9,3},{10,4},{11,5},{12,6},{13,7},{14,8},{15,9},... | collective-permute-start | bytes 442376 | tf_op jit(solution)/shard_map/ppermute | solution.py:18
  (97 other events, 1310.4 us)
where the time goes:
time: 341 us; the launch traced here: 338 us
  starting transfers between devices  124 us (36%)
  local copies, waits for them, and re-layouts  106 us (31%)
  other arithmetic  55.6 us (16%)
  waiting for transfers between devices  38.9 us (11%)
  matrix products  11.7 us (3%)
    ppermute x84, starting transfers between devices, shifted(): return lax.ppermute(block, axis, route)  124 us
    scatter x16, other arithmetic  40.6 us
    ppermute x84, waiting for transfers between devices, shifted(): return lax.ppermute(block, axis, route)  38.9 us
    convert_element_type x1, local copies, waits for them, and re-layouts, cross_matrix(): (jnp.kron(kin_float, identity) + jnp.kron(identity, kin_float)).astype(jn...  38.7 us
    scatter x24, local copies, waits for them, and re-layouts  25 us
    concatenate x2, local copies, waits for them, and re-layouts, shards(): jnp.concatenate([arrival[1] for arrival in arrived], axis=0)  13.5 us
    convert_element_type x1, other arithmetic, cross_matrix(): (jnp.kron(kin_float, identity) + jnp.kron(identity, kin_float)).astype(jn...  10.2 us
  transfers between devices with their start and end apart: 84, of which 20 were waited for; matrix products, arithmetic and copies ran while one was open for 44% of the time, Pallas kernels for 0%

commit v1 on v0

--- a/solution.py
+++ b/solution.py
@@ -1,8 +1,12 @@
+import functools
 import math
 
 import jax
 import jax.numpy as jnp
+import numpy as np
 from jax import lax
+from jax.experimental import pallas as pl
+from jax.experimental.pallas import tpu as pltpu
 from jax.sharding import PartitionSpec as P
 
 Q = 8
@@ -163,6 +167,372 @@
     return (gradient, margin_sum, energy_sum)
 
 
+SUBLANES = 8
+LANES = 128
+
+
+def iota(shape, dim):
+    return lax.broadcasted_iota(jnp.int32, shape, dim)
+
+
+def plan_of(devices, fn_count, edge_len, plane_len, band_width):
+    tiles = plane_len // LANES
+    for shares in range(1, tiles + 1):
+        if devices % shares or tiles % shares:
+            continue
+        classes = devices // shares
+        per_class = edge_len // classes
+        fits = (
+            plane_len % LANES == 0
+            and edge_len % classes == 0
+            and (devices * Q) % classes == 0
+            and classes & (classes - 1) == 0
+            and fn_count * 2 == SUBLANES
+            and per_class == 3
+            and edge_len % SUBLANES == 0
+            and band_width + 2 <= LANES
+            and devices * SUBLANES == 2 * LANES
+            and band_width == (4 * K + 1) * fn_count
+        )
+        if fits:
+            return classes, shares
+    return None
+
+
+def kinetic_numpy(edge_len):
+    positions = np.arange(edge_len)
+    gap = np.abs(positions[:, None] - positions[None, :])
+    sign = 1.0 - 2.0 * (gap % 2)
+    entries = sign / np.maximum(gap, 1).astype(np.float32) ** 2
+    entries = np.where(gap == 0, np.float32(math.pi**2 / 6.0), entries)
+    entries = np.where(gap <= filter_reach, entries, 0.0)
+    return entries.astype(np.float32)
+
+
+def cross_stack(edge_len, rows, reach):
+    kin = kinetic_numpy(edge_len).astype(jnp.bfloat16).astype(np.float32)
+    line = kin[0]
+    blocks = []
+    for step in range(-reach, reach + 1):
+        gap = np.abs(np.arange(rows)[:, None] + step * rows - np.arange(rows)[None, :])
+        along_y = np.where(gap <= filter_reach, line[np.minimum(gap, edge_len - 1)], 0.0)
+        block = np.kron(along_y, np.eye(edge_len, dtype=np.float32))
+        if step == 0:
+            block = block + np.kron(np.eye(rows, dtype=np.float32), kin)
+        blocks.append(block)
+    return np.concatenate(blocks, axis=0).astype(jnp.bfloat16)
+
+
+def dot(a, b):
+    return lax.dot_general(a, b, (((1,), (0,)), ((), ())), preferred_element_type=jnp.float32)
+
+
+def dot_nt(a, b):
+    return lax.dot_general(a, b, (((1,), (1,)), ((), ())), preferred_element_type=jnp.float32)
+
+
+def pick(index, values):
+    out = jnp.full(index.shape, values[0], jnp.int32)
+    for k in range(1, len(values)):
+        out = jnp.where(index == k, values[k], out)
+    return out
+
+
+def send_kernel(
+    dims, offs_ref, psi_ref, pot_ref, kin_ref, cross_ref, kern_ref, mult_ref, patt_ref, out_ref
+):
+    fn_count, edge, plane_len, classes, shares, chunk, reach = dims
+    rows = fn_count * edge
+    tiles = plane_len // LANES // shares
+    width = kern_ref.shape[1]
+    psi = psi_ref[...].reshape(rows, plane_len)
+    pot = pot_ref[...].reshape(rows, plane_len)
+    chunks = plane_len // chunk
+    offs = [offs_ref[k] for k in range(fn_count)]
+
+    group = out_ref.shape[2] // tiles * SUBLANES
+    shape = (classes, group, LANES)
+    cls, item = iota(shape, 0), iota(shape, 1)
+    kind = (item >= group // 2).astype(jnp.int32)
+    item = item - kind * (group // 2)
+    depth, member = item // fn_count, item % fn_count
+    source = kind * rows + member * edge + depth * classes
+    source = source + jnp.bitwise_and(cls - pick(member, offs), classes - 1)
+    lane = iota(shape, 2)
+    select = jnp.concatenate(
+        [
+            jnp.where(source == lane + k * LANES, 1.0, 0.0).astype(jnp.bfloat16)
+            for k in range(2 * rows // LANES)
+        ],
+        axis=2,
+    ).reshape(classes * group, 2 * rows)
+
+    for j in range(chunks):
+        lo, hi = max(0, j - reach), min(chunks, j + reach + 1)
+        here = slice(j * chunk, (j + 1) * chunk)
+        acc = dot(
+            psi[:, lo * chunk : hi * chunk],
+            cross_ref[(lo - j + reach) * chunk : (hi - j + reach) * chunk, :],
+        )
+        mine = psi[:, here]
+        acc = acc + dot(kin_ref[...], mine)
+        acc = acc + pot[:, here].astype(jnp.float32) * mine.astype(jnp.float32)
+        both = jnp.concatenate([mine, acc.astype(jnp.bfloat16)], axis=0)
+        ordered = dot(select, both)
+        for t in range(chunk // LANES):
+            tile = j * (chunk // LANES) + t
+            share, local = tile // tiles, tile % tiles
+            piece = ordered[:, t * LANES : (t + 1) * LANES].astype(jnp.bfloat16)
+            piece = piece.reshape(classes, group // SUBLANES, SUBLANES, LANES)
+            for part in range(group // SUBLANES):
+                out_ref[:, share, part * tiles + local] = piece[:, part]
+
+    blocks = patt_ref.shape[1]
+    spread = jnp.where(
+        iota((blocks, width), 1) // fn_count == iota((blocks, width), 0), 1.0, 0.0
+    ).astype(jnp.bfloat16)
+    flags = dot(patt_ref[...].astype(jnp.float32).astype(jnp.bfloat16), spread)
+    small = jnp.concatenate(
+        [
+            kern_ref[...].astype(jnp.float32) * flags,
+            mult_ref[...].astype(jnp.float32) * flags,
+        ],
+        axis=0,
+    )
+    small = jnp.concatenate(
+        [small, jnp.zeros((SUBLANES, LANES - width), jnp.float32)], axis=1
+    )
+    at, lane = iota((SUBLANES, LANES), 0), iota((SUBLANES, LANES), 1)
+    off = pick(at % fn_count, offs)
+    small = jnp.where(lane == width, (off // 256).astype(jnp.float32), small)
+    small = jnp.where(lane == width + 1, (off % 256).astype(jnp.float32), small)
+    small = small.astype(jnp.bfloat16)
+    for share in range(shares):
+        out_ref[:, share, group // SUBLANES * tiles] = jnp.broadcast_to(
+            small[None], (classes, SUBLANES, LANES)
+        )
+
+
+def grid_kernel(dims, in_ref, out_ref):
+    fn_count, edge, classes, shares, width, band_reach, sub_count = dims
+    devices, units = in_ref.shape[0], in_ref.shape[1]
+    tiles = (units - 1) // 3
+    full = devices * SUBLANES
+    my_class = (lax.axis_index("brick") * sub_count + lax.axis_index("sub")) // shares
+    classes_bits = classes.bit_length() - 1
+
+    small = in_ref[:, units - 1]
+    flat = small.reshape(full, LANES)
+    where_hi, where_lo = width, width + 1
+    lane_a, lane_b = iota((LANES, full), 0), iota((full, LANES), 1)
+    weigh_a = jnp.where(lane_a == where_hi, 256.0, jnp.where(lane_a == where_lo, 1.0, 0.0))
+    weigh_b = jnp.where(lane_b == where_hi, 256.0, jnp.where(lane_b == where_lo, 1.0, 0.0))
+    off_row = dot(flat, weigh_a.astype(jnp.bfloat16)).astype(jnp.int32)
+    off_col = dot_nt(weigh_b.astype(jnp.bfloat16), flat).astype(jnp.int32)
+
+    planes = devices * Q // classes
+
+    def first_plane(off):
+        inner = jnp.bitwise_and(my_class - off, classes - 1)
+        return jnp.right_shift(off + inner - my_class, classes_bits)
+
+    gap = first_plane(off_row) - first_plane(off_col)
+    half_row = jnp.bitwise_and(iota((full, full), 0) // fn_count, 1)
+    half_col = jnp.bitwise_and(iota((full, full), 1) // fn_count, 1)
+
+    def mask(row_depth, col_depth):
+        return jnp.bitwise_and(gap + row_depth - col_depth, planes - 1) == 0
+
+    col_depth = (half_col, jnp.where(half_col == 0, 2, 0), half_col + 1)
+    low = [mask(half_row, d) for d in col_depth]
+    top = [mask(2, d) for d in col_depth]
+
+    halves = small.astype(jnp.float32)
+    turned = pltpu.roll(halves, fn_count, axis=1)
+    upper = iota(halves.shape, 1) < fn_count
+    expand = jnp.where(
+        (iota((LANES, full), 0) == iota((LANES, full), 1) // SUBLANES * fn_count + iota((LANES, full), 1) % fn_count)
+        & (iota((LANES, full), 0) < width),
+        1.0,
+        0.0,
+    ).astype(jnp.bfloat16)
+
+    def dense(rows):
+        wide = dot(rows.reshape(full, LANES).astype(jnp.bfloat16), expand)
+        turned_rows = []
+        for owner in range(devices):
+            shift = (owner - band_reach) * SUBLANES % full
+            block = wide[owner * SUBLANES : (owner + 1) * SUBLANES]
+            turned_rows.append(pltpu.roll(block, shift, axis=1) if shift else block)
+        return jnp.concatenate(turned_rows, axis=0)
+
+    plus = dense(jnp.where(upper, halves, turned))
+    minus = -dense(jnp.where(upper, turned, halves))
+    coef = (minus, jnp.where(half_col == 0, minus, plus), plus)
+    mixed = jnp.concatenate(
+        [
+            jnp.concatenate([jnp.where(k, c, 0.0).astype(jnp.bfloat16) for k, c in zip(ks, coef)], axis=1)
+            for ks in (low, top)
+        ],
+        axis=0,
+    )
+
+    stacked = [
+        jnp.concatenate([in_ref[:, part * tiles + t].reshape(full, LANES) for t in range(tiles)], axis=1)
+        for part in range(3)
+    ]
+    grad = dot(mixed, jnp.concatenate(stacked, axis=0))
+    upper = iota((devices, SUBLANES, LANES), 1) < fn_count
+    for t in range(tiles):
+        out_ref[:, t] = (
+            grad[:full, t * LANES : (t + 1) * LANES].reshape(devices, SUBLANES, LANES).astype(jnp.bfloat16)
+        )
+    second = grad[full:].reshape(devices, SUBLANES, tiles * LANES)
+    for v in range((tiles + 1) // 2):
+        even = second[:, :, 2 * v * LANES : (2 * v + 1) * LANES]
+        if 2 * v + 1 < tiles:
+            even = jnp.where(upper, even, second[:, :, (2 * v + 1) * LANES : (2 * v + 2) * LANES])
+        out_ref[:, tiles + v] = even.astype(jnp.bfloat16)
+
+    sums = []
+    for part in range(3):
+        low_gram = jnp.where(low[part], dot_nt(stacked[0], stacked[part]), 0.0)
+        top_gram = dot_nt(stacked[1], stacked[part])
+        top_gram = jnp.where(top[part] & (half_row == 0), top_gram, 0.0)
+        total = (low_gram + top_gram).reshape(devices, SUBLANES, full)
+        sums.append(total + pltpu.roll(total, fn_count, axis=1))
+    first = sums[0] + pltpu.roll(sums[0], full - fn_count, axis=2)
+    third = sums[2] + pltpu.roll(sums[2], fn_count, axis=2)
+    lanes_half = jnp.bitwise_and(iota((devices, SUBLANES, full), 2) // fn_count, 1)
+    bands = sums[1] + jnp.where(lanes_half == 0, first, third)
+    bands = jnp.where(upper, bands[:, :, :LANES], bands[:, :, LANES:])
+    bands = bands * (1.0 / float(edge**3))
+    out_ref[:, tiles + (tiles + 1) // 2] = bands.astype(jnp.bfloat16)
+
+
+def receive_kernel(dims, offs_ref, in_ref, grad_ref, margin_ref, energy_ref):
+    fn_count, edge, plane_len, classes, shares, band_reach, sub_count = dims
+    tiles = plane_len // LANES // shares
+    rows = fn_count * edge
+    devices = classes * shares
+    width = margin_ref.shape[1]
+    rank = lax.axis_index("brick") * sub_count + lax.axis_index("sub")
+    offs = [offs_ref[k] for k in range(fn_count)]
+    inner = classes * SUBLANES
+
+    shape = (fn_count, edge, inner)
+    member, plane = iota(shape, 0), iota(shape, 1)
+    slot = iota(shape, 2)
+    cls, sub = slot // SUBLANES, slot % SUBLANES
+    half, owner_fn = sub // fn_count, sub % fn_count
+    at = jnp.bitwise_and(cls - pick(owner_fn, offs), classes - 1)
+    same = owner_fn == member
+    low = jnp.where(same & (plane == at + half * classes), 1.0, 0.0)
+    top = same & (plane == at + 2 * classes)
+    for parity in range(2):
+        tops = jnp.where(top & (half == parity), 1.0, 0.0)
+        place = jnp.concatenate([low.astype(jnp.bfloat16), tops.astype(jnp.bfloat16)], axis=2)
+        place = place.reshape(rows, 2 * inner)
+        columns, spots = [], []
+        for share in range(shares):
+            for t in range(parity, tiles, 2):
+                columns.append(
+                    jnp.concatenate(
+                        [
+                            in_ref[:, share, t].reshape(inner, LANES),
+                            in_ref[:, share, tiles + t // 2].reshape(inner, LANES),
+                        ],
+                        axis=0,
+                    )
+                )
+                spots.append((share * tiles + t) * LANES)
+        placed = dot(place, jnp.concatenate(columns, axis=1)).astype(jnp.bfloat16)
+        for n, spot in enumerate(spots):
+            grad_ref[:, :, spot : spot + LANES] = placed[:, n * LANES : (n + 1) * LANES].reshape(
+                fn_count, edge, LANES
+            )
+
+    total = jnp.sum(
+        in_ref[:, :, tiles + (tiles + 1) // 2].reshape(devices, SUBLANES, LANES).astype(jnp.float32), axis=0
+    )
+    lane, col = iota((LANES, LANES), 0), iota((LANES, LANES), 1)
+    partner = lax.rem(rank + col // fn_count - band_reach + devices, devices)
+    for kind, ref in ((0, margin_ref), (1, energy_ref)):
+        wanted = partner * SUBLANES + kind * fn_count + col % fn_count
+        picked = [
+            lax.dot_general(
+                total,
+                jnp.where(wanted == lane + part * LANES, 1.0, 0.0),
+                (((1,), (0,)), ((), ())),
+                preferred_element_type=jnp.float32,
+                precision=lax.Precision.HIGHEST,
+            )
+            for part in range(2)
+        ]
+        ref[...] = (picked[0][:fn_count] + picked[1][fn_count:])[:, :width]
+
+
+def transposed_shards(classes, shares, psi, potential, offsets, kernel, multipliers, pattern):
+    fn_count, edge, plane_len = psi.shape
+    sub_count = lax.axis_size("sub")
+    devices = sub_count * lax.axis_size("brick")
+    width = kernel.shape[1]
+    tiles = plane_len // LANES // shares
+    band_reach = 2 * K
+    chunk = edge * SUBLANES
+    reach = -(-filter_reach // SUBLANES)
+    params = pltpu.CompilerParams(vmem_limit_bytes=56 * 2**20)
+    smem = pl.BlockSpec(memory_space=pltpu.SMEM)
+    vmem = pl.BlockSpec(memory_space=pltpu.VMEM)
+
+    kinetic = np.kron(np.eye(fn_count, dtype=np.float32), kinetic_numpy(edge)).astype(jnp.bfloat16)
+    cross = cross_stack(edge, SUBLANES, reach)
+    units = 3 * tiles + 1
+    sent = pl.pallas_call(
+        functools.partial(send_kernel, (fn_count, edge, plane_len, classes, shares, chunk, reach)),
+        out_shape=jax.ShapeDtypeStruct((classes, shares, units, SUBLANES, LANES), jnp.bfloat16),
+        in_specs=[smem] + [vmem] * 7,
+        out_specs=vmem,
+        compiler_params=params,
+        name="send",
+    )(offsets, psi, potential, jnp.asarray(kinetic), jnp.asarray(cross), kernel, multipliers, pattern)
+    sent = sent.reshape(devices, units, SUBLANES, LANES)
+    axes = ("brick", "sub")
+    held = lax.all_to_all(sent, axes, 0, 0, tiled=True)
+
+    back_units = tiles + (tiles + 1) // 2 + 1
+    made = pl.pallas_call(
+        functools.partial(grid_kernel, (fn_count, edge, classes, shares, width, band_reach, sub_count)),
+        out_shape=jax.ShapeDtypeStruct((devices, back_units, SUBLANES, LANES), jnp.bfloat16),
+        in_specs=[vmem],
+        out_specs=vmem,
+        compiler_params=params,
+        name="grid",
+    )(held)
+    back = lax.all_to_all(made, axes, 0, 0, tiled=True)
+    back = back.reshape(classes, shares, back_units, SUBLANES, LANES)
+    return pl.pallas_call(
+        functools.partial(receive_kernel, (fn_count, edge, plane_len, classes, shares, band_reach, sub_count)),
+        out_shape=(
+            jax.ShapeDtypeStruct(psi.shape, jnp.bfloat16),
+            jax.ShapeDtypeStruct((fn_count, width), jnp.float32),
+            jax.ShapeDtypeStruct((fn_count, width), jnp.float32),
+        ),
+        in_specs=[smem, vmem],
+        out_specs=(vmem, vmem, vmem),
+        compiler_params=params,
+        name="receive",
+    )(offsets, back)
+
+
+def any_shards(psi, potential, offsets, kernel, multipliers, pattern):
+    devices = lax.axis_size("brick") * lax.axis_size("sub")
+    plan = plan_of(devices, *psi.shape, kernel.shape[1])
+    if plan is None:
+        return shards(psi, potential, offsets, kernel, multipliers, pattern)
+    return transposed_shards(*plan, psi, potential, offsets, kernel, multipliers, pattern)
+
+
 def solution(mesh):
     in_specs = (
         P(("brick", "sub"), None, None),
@@ -177,4 +547,4 @@
         P(("brick", "sub"), None),
         P(("brick", "sub"), None),
     )
-    return jax.shard_map(shards, mesh=mesh, in_specs=in_specs, out_specs=out_specs, check_vma=False)
+    return jax.shard_map(any_shards, mesh=mesh, in_specs=in_specs, out_specs=out_specs, check_vma=False)

time: 341 us -> 95 us (0.28)
  starting transfers between devices: 124 us -> 0 us
  local copies, waits for them, and re-layouts: 106 us -> 0 us
  blocking collectives: 0 us -> 79 us
  other arithmetic: 55.6 us -> 0 us
  waiting for transfers between devices: 38.9 us -> 0 us
  Pallas kernels: 0 us -> 15 us
  matrix products: 11.7 us -> 0 us
    ppermute x84 -> x0, starting transfers between devices: 124 us -> none  [shifted(): return lax.ppermute(block, axis, route)]
    all_to_all x0 -> x2, blocking collectives: none -> 79 us  [the longest x1 50.5 us: transposed_shards(): held = lax.all_to_all(sent, axes, 0, 0, tiled=True)]
    scatter x17 -> x0, other arithmetic: 40.6 us -> none
    ppermute x84 -> x0, waiting for transfers between devices: 38.9 us -> none  [shifted(): return lax.ppermute(block, axis, route)]
    convert_element_type x2 -> x0, local copies, waits for them, and re-layouts: 38.8 us -> none  [the longest x1 38.7 us: cross_matrix(): (jnp.kron(kin_float, identity) + jnp.kron(identity, kin_float)).astype(jn...]
    scatter x26 -> x0, local copies, waits for them, and re-layouts: 26.5 us -> none
    concatenate x7 -> x0, local copies, waits for them, and re-layouts: 24.6 us -> none  [the longest x2 13.5 us: shards(): jnp.concatenate([arrival[1] for arrival in arrived], axis=0)]
    pallas_call x0 -> x3, Pallas kernels: none -> 15 us  [the longest x1 7.22 us: transposed_shards(): pl.pallas_call(functools.partial(send_kernel, (fn_count, edge, plane_len,...]
  transfers between devices with their start and end apart: 84 -> 0, of which waited for: 20 -> 0; matrix products, arithmetic and copies ran while one was open for 44% -> 0% of each run, Pallas kernels for 0% -> 0%
where the time goes in v1:
time: 95 us; the launch traced here: 94.7 us
  blocking collectives  79 us (83%)
  Pallas kernels  15 us (16%)
    all_to_all x1, blocking collectives, transposed_shards(): held = lax.all_to_all(sent, axes, 0, 0, tiled=True)  50.5 us
    all_to_all x1, blocking collectives, transposed_shards(): back = lax.all_to_all(made, axes, 0, 0, tiled=True)  28.5 us
    pallas_call x1, Pallas kernels, transposed_shards(): pl.pallas_call(functools.partial(send_kernel, (fn_count, edge, plane_len,...  7.22 us
    pallas_call x1, Pallas kernels, transposed_shards(): pl.pallas_call(functools.partial(grid_kernel, (fn_count, edge, classes, s...  5.19 us
    pallas_call x1, Pallas kernels, transposed_shards(): pl.pallas_call(functools.partial(receive_kernel, (fn_count, edge, plane_l...  2.61 us

profile of v1, /device:TPU:0, one launch (start us, length us, event | category | flops | bytes accessed | tf_op | source)
XLA Modules:
  0.0 94.7 jit_solution(6930657082439885404)
XLA Ops:
  0.6 7.2 %send.1 = bf16[16,2,28,8,128]{4,3,2,1,0:T(8,128)(2,1)} custom-call(s32[4]{0:T(128)} %offs_ref.3, bf16[4,48,2304]{2,1,0:T(8,128)(2,1)} %psi_ref.1, bf16[4,48,2304]{2,1,0:T(8,128)(2,1)} %pot_ref.1, bf16[192,192]{1,0:T(8,128)(2,1)} %constant.4.clone.kin_ref, bf16[1920,384]{1,0:T(8,128)(2,1)} %constant.5.clone.cross_ref, bf16[4,100]{1,0:T(4,128)(2,1)} %kern_ref.1, ...), custom_call_target="tpu_custom_call" | custom-call | tf_op jit(solution)/shard_map/send/pallas_call | solution.py:491
  7.9 50.5 %all_to_all.10.in_ref = bf16[32,28,8,128]{3,2,1,0:T(8,128)(2,1)} all-to-all(bf16[32,28,8,128]{3,2,1,0:T(8,128)(2,1)} %bitcast.2), channel_id=1, replica_groups=mesh['brick'=8,'sub'=4] {'brick','sub'}, dimensions={0} | all-to-all | bytes 3670016 | tf_op jit(solution)/shard_map/all_to_all | solution.py:501
  58.4 5.2 %grid.1 = bf16[32,15,8,128]{3,2,1,0:T(8,128)(2,1)} custom-call(bf16[32,28,8,128]{3,2,1,0:T(8,128)(2,1)} %all_to_all.10.in_ref), custom_call_target="tpu_custom_call" | custom-call | tf_op jit(solution)/shard_map/grid/pallas_call | solution.py:504
  63.5 28.5 %all_to_all.11 = bf16[32,15,8,128]{3,2,1,0:T(8,128)(2,1)} all-to-all(bf16[32,15,8,128]{3,2,1,0:T(8,128)(2,1)} %grid.1), channel_id=1, replica_groups=mesh['brick'=8,'sub'=4] {'brick','sub'}, dimensions={0} | all-to-all | bytes 1966080 | tf_op jit(solution)/shard_map/all_to_all | solution.py:512
  92.1 2.6 %receive.1 = (bf16[4,48,2304]{2,1,0:T(8,128)(2,1)}, f32[4,100]{1,0:T(4,128)}, f32[4,100]{1,0:T(4,128)}) custom-call(s32[4]{0:T(128)} %offs_ref.3, bf16[16,2,15,8,128]{4,3,2,1,0:T(8,128)(2,1)} %bitcast.3), custom_call_target="tpu_custom_call" | custom-call | tf_op jit(solution)/shard_map/receive/pallas_call | solution.py:514

commit v2 on v1

--- a/solution.py
+++ b/solution.py
@@ -231,6 +231,10 @@
     return lax.dot_general(a, b, (((1,), (1,)), ((), ())), preferred_element_type=jnp.float32)
 
 
+def in_hbm(array):
+    return pltpu.with_memory_space_constraint(array, pltpu.HBM)
+
+
 def pick(index, values):
     out = jnp.full(index.shape, values[0], jnp.int32)
     for k in range(1, len(values)):
@@ -239,33 +243,56 @@
 
 
 def send_kernel(
-    dims, offs_ref, psi_ref, pot_ref, kin_ref, cross_ref, kern_ref, mult_ref, patt_ref, out_ref
+    dims, offs_hbm, psi_hbm, pot_hbm, kin_hbm, cross_hbm, kern_hbm, mult_hbm, patt_hbm, out_ref,
+    offs_ref, psi_ref, pot_ref, kin_ref, cross_ref, kern_ref, mult_ref, patt_ref, sems
 ):
     fn_count, edge, plane_len, classes, shares, chunk, reach = dims
     rows = fn_count * edge
     tiles = plane_len // LANES // shares
+    parts = 3
+    copies = [
+        pltpu.make_async_copy(source, target, sems.at[n])
+        for n, (source, target) in enumerate(
+            (
+                (offs_hbm, offs_ref),
+                (psi_hbm, psi_ref),
+                (kin_hbm, kin_ref),
+                (cross_hbm, cross_ref),
+                (pot_hbm, pot_ref),
+                (kern_hbm, kern_ref),
+                (mult_hbm, mult_ref),
+                (patt_hbm, patt_ref),
+            )
+        )
+    ]
+    for copy in copies:
+        copy.start()
     width = kern_ref.shape[1]
+    chunks = plane_len // chunk
+    copies[0].wait()
+    offs = [offs_ref[k] for k in range(fn_count)]
+
+    shape = (classes, 2 * SUBLANES, LANES)
+    cls, item, lane = iota(shape, 0), iota(shape, 1), iota(shape, 2)
+    inner = jnp.bitwise_and(cls - pick(item % fn_count, offs), classes - 1)
+    base = item % fn_count * edge + inner
+
+    def select(first):
+        depth = item // fn_count - first
+        source = jnp.where((depth >= 0) & (depth < parts), base + depth * classes, -1)
+        wide = [
+            jnp.where(source == lane + k * LANES, 1.0, 0.0).astype(jnp.bfloat16)
+            for k in range(-(-rows // LANES))
+        ]
+        return jnp.concatenate(wide, axis=2).reshape(classes * 2 * SUBLANES, -1)[:, :rows]
+
+    own, applied = select(0), select(1)
+    for copy in copies[1:4]:
+        copy.wait()
     psi = psi_ref[...].reshape(rows, plane_len)
+    lead = jnp.concatenate([kin_ref[...], own], axis=0)
+    copies[4].wait()
     pot = pot_ref[...].reshape(rows, plane_len)
-    chunks = plane_len // chunk
-    offs = [offs_ref[k] for k in range(fn_count)]
-
-    group = out_ref.shape[2] // tiles * SUBLANES
-    shape = (classes, group, LANES)
-    cls, item = iota(shape, 0), iota(shape, 1)
-    kind = (item >= group // 2).astype(jnp.int32)
-    item = item - kind * (group // 2)
-    depth, member = item // fn_count, item % fn_count
-    source = kind * rows + member * edge + depth * classes
-    source = source + jnp.bitwise_and(cls - pick(member, offs), classes - 1)
-    lane = iota(shape, 2)
-    select = jnp.concatenate(
-        [
-            jnp.where(source == lane + k * LANES, 1.0, 0.0).astype(jnp.bfloat16)
-            for k in range(2 * rows // LANES)
-        ],
-        axis=2,
-    ).reshape(classes * group, 2 * rows)
 
     for j in range(chunks):
         lo, hi = max(0, j - reach), min(chunks, j + reach + 1)
@@ -275,18 +302,22 @@
             cross_ref[(lo - j + reach) * chunk : (hi - j + reach) * chunk, :],
         )
         mine = psi[:, here]
-        acc = acc + dot(kin_ref[...], mine)
+        led = dot(lead, mine)
+        acc = acc + led[:rows]
         acc = acc + pot[:, here].astype(jnp.float32) * mine.astype(jnp.float32)
-        both = jnp.concatenate([mine, acc.astype(jnp.bfloat16)], axis=0)
-        ordered = dot(select, both)
+        sorted_h = dot(applied, acc.astype(jnp.bfloat16))
         for t in range(chunk // LANES):
             tile = j * (chunk // LANES) + t
             share, local = tile // tiles, tile % tiles
-            piece = ordered[:, t * LANES : (t + 1) * LANES].astype(jnp.bfloat16)
-            piece = piece.reshape(classes, group // SUBLANES, SUBLANES, LANES)
-            for part in range(group // SUBLANES):
-                out_ref[:, share, part * tiles + local] = piece[:, part]
-
+            at = slice(t * LANES, (t + 1) * LANES)
+            first = led[rows:, at].reshape(classes, 2, SUBLANES, LANES)
+            second = sorted_h[:, at].reshape(classes, 2, SUBLANES, LANES)
+            out_ref[:, share, local] = first[:, 0].astype(jnp.bfloat16)
+            out_ref[:, share, tiles + local] = (first[:, 1] + second[:, 0]).astype(jnp.bfloat16)
+            out_ref[:, share, 2 * tiles + local] = second[:, 1].astype(jnp.bfloat16)
+
+    for copy in copies[5:]:
+        copy.wait()
     blocks = patt_ref.shape[1]
     spread = jnp.where(
         iota((blocks, width), 1) // fn_count == iota((blocks, width), 0), 1.0, 0.0
@@ -308,9 +339,7 @@
     small = jnp.where(lane == width + 1, (off % 256).astype(jnp.float32), small)
     small = small.astype(jnp.bfloat16)
     for share in range(shares):
-        out_ref[:, share, group // SUBLANES * tiles] = jnp.broadcast_to(
-            small[None], (classes, SUBLANES, LANES)
-        )
+        out_ref[:, share, parts * tiles] = jnp.broadcast_to(small[None], (classes, SUBLANES, LANES))
 
 
 def grid_kernel(dims, in_ref, out_ref):
@@ -410,12 +439,15 @@
     out_ref[:, tiles + (tiles + 1) // 2] = bands.astype(jnp.bfloat16)
 
 
-def receive_kernel(dims, offs_ref, in_ref, grad_ref, margin_ref, energy_ref):
+def receive_kernel(dims, offs_hbm, in_ref, grad_ref, margin_ref, energy_ref, offs_ref, sem):
     fn_count, edge, plane_len, classes, shares, band_reach, sub_count = dims
     tiles = plane_len // LANES // shares
     rows = fn_count * edge
     devices = classes * shares
     width = margin_ref.shape[1]
+    copy = pltpu.make_async_copy(offs_hbm, offs_ref, sem)
+    copy.start()
+    copy.wait()
     rank = lax.axis_index("brick") * sub_count + lax.axis_index("sub")
     offs = [offs_ref[k] for k in range(fn_count)]
     inner = classes * SUBLANES
@@ -481,21 +513,36 @@
     band_reach = 2 * K
     chunk = edge * SUBLANES
     reach = -(-filter_reach // SUBLANES)
-    params = pltpu.CompilerParams(vmem_limit_bytes=56 * 2**20)
-    smem = pl.BlockSpec(memory_space=pltpu.SMEM)
+    params = pltpu.CompilerParams(vmem_limit_bytes=20 * 2**20)
     vmem = pl.BlockSpec(memory_space=pltpu.VMEM)
 
     kinetic = np.kron(np.eye(fn_count, dtype=np.float32), kinetic_numpy(edge)).astype(jnp.bfloat16)
     cross = cross_stack(edge, SUBLANES, reach)
     units = 3 * tiles + 1
+    offsets = in_hbm(offsets)
     sent = pl.pallas_call(
         functools.partial(send_kernel, (fn_count, edge, plane_len, classes, shares, chunk, reach)),
         out_shape=jax.ShapeDtypeStruct((classes, shares, units, SUBLANES, LANES), jnp.bfloat16),
-        in_specs=[smem] + [vmem] * 7,
+        in_specs=[pl.BlockSpec(memory_space=pltpu.HBM)] * 8,
         out_specs=vmem,
+        scratch_shapes=[
+            pltpu.SMEM(offsets.shape, offsets.dtype),
+            pltpu.VMEM(psi.shape, psi.dtype),
+            pltpu.VMEM(potential.shape, potential.dtype),
+            pltpu.VMEM(kinetic.shape, jnp.bfloat16),
+            pltpu.VMEM(cross.shape, jnp.bfloat16),
+            pltpu.VMEM(kernel.shape, kernel.dtype),
+            pltpu.VMEM(multipliers.shape, multipliers.dtype),
+            pltpu.VMEM(pattern.shape, pattern.dtype),
+            pltpu.SemaphoreType.DMA((8,)),
+        ],
         compiler_params=params,
         name="send",
-    )(offsets, psi, potential, jnp.asarray(kinetic), jnp.asarray(cross), kernel, multipliers, pattern)
+    )(
+        offsets,
+        *(in_hbm(x) for x in (psi, potential, jnp.asarray(kinetic), jnp.asarray(cross))),
+        *(in_hbm(x) for x in (kernel, multipliers, pattern)),
+    )
     sent = sent.reshape(devices, units, SUBLANES, LANES)
     axes = ("brick", "sub")
     held = lax.all_to_all(sent, axes, 0, 0, tiled=True)
@@ -518,8 +565,9 @@
             jax.ShapeDtypeStruct((fn_count, width), jnp.float32),
             jax.ShapeDtypeStruct((fn_count, width), jnp.float32),
         ),
-        in_specs=[smem, vmem],
+        in_specs=[pl.BlockSpec(memory_space=pltpu.HBM), vmem],
         out_specs=(vmem, vmem, vmem),
+        scratch_shapes=[pltpu.SMEM(offsets.shape, offsets.dtype), pltpu.SemaphoreType.DMA],
         compiler_params=params,
         name="receive",
     )(offsets, back)

time: 95 us -> 90.2 us (0.949)
  Pallas kernels: 15 us -> 10.9 us
    pallas_call x1, Pallas kernels: 5.19 us -> 2.74 us  [transposed_shards(): pl.pallas_call(functools.partial(grid_kernel, (fn_count, edge, classes, s...]
    pallas_call x1, Pallas kernels: 7.22 us -> 6.09 us  [transposed_shards(): pl.pallas_call(functools.partial(send_kernel, (fn_count, edge, plane_len,...]
where the time goes in v2:
time: 90.2 us; the launch traced here: 90 us
  blocking collectives  78.4 us (87%)
  Pallas kernels  10.9 us (12%)
    all_to_all x1, blocking collectives, transposed_shards(): held = lax.all_to_all(sent, axes, 0, 0, tiled=True)  50.2 us
    all_to_all x1, blocking collectives, transposed_shards(): back = lax.all_to_all(made, axes, 0, 0, tiled=True)  28.2 us
    pallas_call x1, Pallas kernels, transposed_shards(): pl.pallas_call(functools.partial(send_kernel, (fn_count, edge, plane_len,...  6.09 us
    pallas_call x1, Pallas kernels, transposed_shards(): pl.pallas_call(functools.partial(grid_kernel, (fn_count, edge, classes, s...  2.74 us
    pallas_call x1, Pallas kernels, transposed_shards(): pl.pallas_call(functools.partial(receive_kernel, (fn_count, edge, plane_l...  2.06 us

profile of v2, /device:TPU:0, one launch (start us, length us, event | category | flops | bytes accessed | tf_op | source)
XLA Modules:
  0.0 90.0 jit_solution(5503802575835375787)
XLA Ops:
  0.6 6.1 %send.1 = bf16[16,2,28,8,128]{4,3,2,1,0:T(8,128)(2,1)S(1)} custom-call(s32[4]{0:T(128)} %offs_hbm.3, bf16[4,48,2304]{2,1,0:T(8,128)(2,1)} %psi_hbm.1, bf16[4,48,2304]{2,1,0:T(8,128)(2,1)} %pot_hbm.1, bf16[192,192]{1,0:T(8,128)(2,1)} %constant.4.clone.kin_hbm, bf16[1920,384]{1,0:T(8,128)(2,1)} %constant.5.clone.cross_hbm, bf16[4,100]{1,0:T(4,128)(2,1)} %kern_hbm.1, ...), custom_call_target="tpu_custom_call" | custom-call | tf_op jit(solution)/shard_map/send/pallas_call | solution.py:523
  6.7 50.2 %all_to_all.10.in_ref = bf16[32,28,8,128]{3,2,1,0:T(8,128)(2,1)S(1)} all-to-all(bf16[32,28,8,128]{3,2,1,0:T(8,128)(2,1)S(1)} %bitcast.2), channel_id=1, replica_groups=mesh['brick'=8,'sub'=4] {'brick','sub'}, dimensions={0} | all-to-all | bytes 3670016 | tf_op jit(solution)/shard_map/all_to_all | solution.py:548
  56.9 2.7 %grid.1 = bf16[32,15,8,128]{3,2,1,0:T(8,128)(2,1)S(1)} custom-call(bf16[32,28,8,128]{3,2,1,0:T(8,128)(2,1)S(1)} %all_to_all.10.in_ref), custom_call_target="tpu_custom_call" | custom-call | tf_op jit(solution)/shard_map/grid/pallas_call | solution.py:551
  59.7 28.2 %all_to_all.11 = bf16[32,15,8,128]{3,2,1,0:T(8,128)(2,1)S(1)} all-to-all(bf16[32,15,8,128]{3,2,1,0:T(8,128)(2,1)S(1)} %grid.1), channel_id=1, replica_groups=mesh['brick'=8,'sub'=4] {'brick','sub'}, dimensions={0} | all-to-all | bytes 1966080 | tf_op jit(solution)/shard_map/all_to_all | solution.py:559
  87.9 2.1 %receive.1 = (bf16[4,48,2304]{2,1,0:T(8,128)(2,1)}, f32[4,100]{1,0:T(4,128)}, f32[4,100]{1,0:T(4,128)}) custom-call(s32[4]{0:T(128)} %offs_hbm.3, bf16[16,2,15,8,128]{4,3,2,1,0:T(8,128)(2,1)S(1)} %bitcast.3), custom_call_target="tpu_custom_call" | custom-call | tf_op jit(solution)/shard_map/receive/pallas_call | solution.py:561

commit v3 on v1

--- a/solution.py
+++ b/solution.py
@@ -231,6 +231,10 @@
     return lax.dot_general(a, b, (((1,), (1,)), ((), ())), preferred_element_type=jnp.float32)
 
 
+def in_hbm(array):
+    return pltpu.with_memory_space_constraint(array, pltpu.HBM)
+
+
 def pick(index, values):
     out = jnp.full(index.shape, values[0], jnp.int32)
     for k in range(1, len(values)):
@@ -238,35 +242,102 @@
     return out
 
 
-def send_kernel(
-    dims, offs_ref, psi_ref, pot_ref, kin_ref, cross_ref, kern_ref, mult_ref, patt_ref, out_ref
+def fetch(pairs, sems):
+    copies = [pltpu.make_async_copy(source, target, sems.at[n]) for n, (source, target) in enumerate(pairs)]
+    for copy in copies:
+        copy.start()
+    return copies
+
+
+def class_select(target, offs, fn_count, edge, classes, least=0):
+    shape = target.shape
+    item, lane = iota(shape, 1), iota(shape, 2)
+    member = item % fn_count
+    depth = jnp.minimum(item // fn_count + least, 2)
+    inner = jnp.bitwise_and(target - pick(member, offs), classes - 1)
+    source = member * edge + depth * classes + inner
+    rows = fn_count * edge
+    wide = [
+        jnp.where(source == lane + k * LANES, 1.0, 0.0).astype(jnp.bfloat16)
+        for k in range(-(-rows // LANES))
+    ]
+    return jnp.concatenate(wide, axis=2).reshape(shape[0] * shape[1], -1)[:, :rows]
+
+
+def coefficient_rows(band, pattern, offs, fn_count):
+    width, blocks = band.shape[1], pattern.shape[1]
+    spread = jnp.where(
+        iota((blocks, width), 1) // fn_count == iota((blocks, width), 0), 1.0, 0.0
+    ).astype(jnp.bfloat16)
+    small = band.astype(jnp.float32) * dot(pattern.astype(jnp.float32).astype(jnp.bfloat16), spread)
+    small = jnp.concatenate([small, small], axis=0)
+    small = jnp.concatenate([small, jnp.zeros((SUBLANES, LANES - width), jnp.float32)], axis=1)
+    at, lane = iota((SUBLANES, LANES), 0), iota((SUBLANES, LANES), 1)
+    off = pick(at % fn_count, offs)
+    small = jnp.where(lane == width, (off // 256).astype(jnp.float32), small)
+    return jnp.where(lane == width + 1, (off % 256).astype(jnp.float32), small)
+
+
+def pack_kernel(dims, offs_hbm, *refs):
+    fn_count, edge, plane_len, classes, shares, groups, sub_count, carried = dims
+    sources, outs, kept = refs[:carried], refs[carried : carried + groups], refs[carried + groups : -2]
+    offs_ref, sems = refs[-2:]
+    copies = fetch(((offs_hbm, offs_ref), *zip(sources, kept)), sems)
+    rows = fn_count * edge
+    tiles = plane_len // LANES // shares
+    near = classes // groups
+    rank = lax.axis_index("brick") * sub_count + lax.axis_index("sub")
+    mine = jnp.bitwise_and(rank, shares - 1)
+    copies[0].wait()
+    offs = [offs_ref[k] for k in range(fn_count)]
+    target = jnp.bitwise_xor(iota((classes, SUBLANES, LANES), 0), rank // shares)
+    select = class_select(target, offs, fn_count, edge, classes)
+    copies[1].wait()
+    psi = kept[0][...].reshape(rows, plane_len)
+    for share in range(shares):
+        there = jnp.bitwise_xor(mine, share)
+        ordered = dot(select, psi[:, share * tiles * LANES : (share + 1) * tiles * LANES])
+        ordered = ordered.reshape(groups, near, SUBLANES, tiles * LANES)
+        for k in range(groups):
+            for t in range(tiles):
+                outs[k][:, there, t] = ordered[k, :, :, t * LANES : (t + 1) * LANES].astype(jnp.bfloat16)
+    for copy in copies[2:]:
+        copy.wait()
+
+
+def apply_kernel(
+    dims,
+    offs_hbm,
+    psi_ref,
+    pot_ref,
+    cross_ref,
+    kin_ref,
+    kern_ref,
+    mult_ref,
+    patt_ref,
+    out_ref,
+    offs_ref,
+    sems,
 ):
     fn_count, edge, plane_len, classes, shares, chunk, reach = dims
+    copies = fetch(((offs_hbm, offs_ref),), sems)
     rows = fn_count * edge
     tiles = plane_len // LANES // shares
-    width = kern_ref.shape[1]
+    pairs = (tiles + 1) // 2
+    chunks = plane_len // chunk
     psi = psi_ref[...].reshape(rows, plane_len)
     pot = pot_ref[...].reshape(rows, plane_len)
-    chunks = plane_len // chunk
+    copies[0].wait()
     offs = [offs_ref[k] for k in range(fn_count)]
-
-    group = out_ref.shape[2] // tiles * SUBLANES
-    shape = (classes, group, LANES)
-    cls, item = iota(shape, 0), iota(shape, 1)
-    kind = (item >= group // 2).astype(jnp.int32)
-    item = item - kind * (group // 2)
-    depth, member = item // fn_count, item % fn_count
-    source = kind * rows + member * edge + depth * classes
-    source = source + jnp.bitwise_and(cls - pick(member, offs), classes - 1)
-    lane = iota(shape, 2)
-    select = jnp.concatenate(
-        [
-            jnp.where(source == lane + k * LANES, 1.0, 0.0).astype(jnp.bfloat16)
-            for k in range(2 * rows // LANES)
-        ],
-        axis=2,
-    ).reshape(classes * group, 2 * rows)
-
+    shape = (classes, 2 * SUBLANES, LANES)
+    select = class_select(iota(shape, 0), offs, fn_count, edge, classes)
+    shape = (classes, SUBLANES, LANES)
+    deep = class_select(iota(shape, 0), offs, fn_count, edge, classes, 2)
+    lead = jnp.concatenate([kin_ref[...], deep], axis=0)
+    patt = patt_ref[...]
+    small = [coefficient_rows(ref[...], patt, offs, fn_count)[None] for ref in (mult_ref, kern_ref)]
+    upper = iota(shape, 1) < fn_count
+    held = {}
     for j in range(chunks):
         lo, hi = max(0, j - reach), min(chunks, j + reach + 1)
         here = slice(j * chunk, (j + 1) * chunk)
@@ -274,55 +345,62 @@
             psi[:, lo * chunk : hi * chunk],
             cross_ref[(lo - j + reach) * chunk : (hi - j + reach) * chunk, :],
         )
-        mine = psi[:, here]
-        acc = acc + dot(kin_ref[...], mine)
-        acc = acc + pot[:, here].astype(jnp.float32) * mine.astype(jnp.float32)
-        both = jnp.concatenate([mine, acc.astype(jnp.bfloat16)], axis=0)
-        ordered = dot(select, both)
-        for t in range(chunk // LANES):
-            tile = j * (chunk // LANES) + t
-            share, local = tile // tiles, tile % tiles
-            piece = ordered[:, t * LANES : (t + 1) * LANES].astype(jnp.bfloat16)
-            piece = piece.reshape(classes, group // SUBLANES, SUBLANES, LANES)
-            for part in range(group // SUBLANES):
-                out_ref[:, share, part * tiles + local] = piece[:, part]
-
-    blocks = patt_ref.shape[1]
-    spread = jnp.where(
-        iota((blocks, width), 1) // fn_count == iota((blocks, width), 0), 1.0, 0.0
-    ).astype(jnp.bfloat16)
-    flags = dot(patt_ref[...].astype(jnp.float32).astype(jnp.bfloat16), spread)
-    small = jnp.concatenate(
-        [
-            kern_ref[...].astype(jnp.float32) * flags,
-            mult_ref[...].astype(jnp.float32) * flags,
-        ],
-        axis=0,
-    )
-    small = jnp.concatenate(
-        [small, jnp.zeros((SUBLANES, LANES - width), jnp.float32)], axis=1
-    )
-    at, lane = iota((SUBLANES, LANES), 0), iota((SUBLANES, LANES), 1)
-    off = pick(at % fn_count, offs)
-    small = jnp.where(lane == width, (off // 256).astype(jnp.float32), small)
-    small = jnp.where(lane == width + 1, (off % 256).astype(jnp.float32), small)
-    small = small.astype(jnp.bfloat16)
-    for share in range(shares):
-        out_ref[:, share, group // SUBLANES * tiles] = jnp.broadcast_to(
-            small[None], (classes, SUBLANES, LANES)
-        )
-
-
-def grid_kernel(dims, in_ref, out_ref):
+        led = dot(lead, psi[:, here])
+        acc = acc + led[:rows]
+        acc = acc + pot[:, here].astype(jnp.float32) * psi[:, here].astype(jnp.float32)
+        ordered = dot(select, acc.astype(jnp.bfloat16)).reshape(classes, 2, SUBLANES, chunk)
+        deeps = (ordered[:, 1], led[rows:].reshape(classes, SUBLANES, chunk))
+        for n in range(chunk // LANES):
+            share, t = divmod(j * (chunk // LANES) + n, tiles)
+            at = slice(n * LANES, (n + 1) * LANES)
+            out_ref[:, share, t] = ordered[:, 0, :, at].astype(jnp.bfloat16)
+            for kind in range(2):
+                value = deeps[kind][:, :, at]
+                if t % 2 == 0 and t + 1 < tiles:
+                    held[kind, share] = value
+                    continue
+                pair = (held[kind, share], value) if t % 2 else (value, small[kind])
+                out_ref[:, share, tiles + kind * pairs + t // 2] = jnp.where(upper, *pair).astype(jnp.bfloat16)
+
+
+def turn_kernel(*refs):
+    groups = len(refs) - refs[0].shape[0]
+    arrived, outs = refs[:groups], refs[groups:]
+    for near, out in enumerate(outs):
+        for far in range(groups):
+            out[far] = arrived[far][near]
+
+
+def grid_kernel(dims, *refs):
     fn_count, edge, classes, shares, width, band_reach, sub_count = dims
-    devices, units = in_ref.shape[0], in_ref.shape[1]
-    tiles = (units - 1) // 3
+    psi_refs, (h_ref, out_ref, psi_all) = refs[:-3], refs[-3:]
+    devices = h_ref.shape[0]
+    tiles = psi_refs[0].shape[1]
+    pairs = (tiles + 1) // 2
     full = devices * SUBLANES
-    my_class = (lax.axis_index("brick") * sub_count + lax.axis_index("sub")) // shares
+    rank = lax.axis_index("brick") * sub_count + lax.axis_index("sub")
+    my_class = rank // shares
     classes_bits = classes.bit_length() - 1
-
-    small = in_ref[:, units - 1]
-    flat = small.reshape(full, LANES)
+    near = len(psi_refs)
+    for n, ref in enumerate(psi_refs):
+        for far in range(ref.shape[0]):
+            psi_all[jnp.bitwise_xor(rank, far * near + n)] = ref[far]
+
+    upper = iota((devices, SUBLANES, LANES), 1) < fn_count
+    both = []
+    for v in range(pairs):
+        ours = h_ref[:, tiles + pairs + v].astype(jnp.float32)
+        theirs = h_ref[:, tiles + v].astype(jnp.float32)
+        both.append(jnp.where(upper, ours, pltpu.roll(theirs, fn_count, axis=1)))
+        both.append(jnp.where(upper, pltpu.roll(ours, fn_count, axis=1), theirs))
+    halves = both.pop()
+    stacked = [
+        jnp.concatenate([psi_all[:, t].reshape(full, LANES) for t in range(tiles)], axis=1),
+        jnp.concatenate([x.reshape(full, LANES).astype(jnp.bfloat16) for x in both], axis=1),
+        jnp.concatenate([h_ref[:, t].reshape(full, LANES) for t in range(tiles)], axis=1),
+    ]
+
+    flat = halves.reshape(full, LANES).astype(jnp.bfloat16)
     where_hi, where_lo = width, width + 1
     lane_a, lane_b = iota((LANES, full), 0), iota((full, LANES), 1)
     weigh_a = jnp.where(lane_a == where_hi, 256.0, jnp.where(lane_a == where_lo, 1.0, 0.0))
@@ -343,13 +421,11 @@
     def mask(row_depth, col_depth):
         return jnp.bitwise_and(gap + row_depth - col_depth, planes - 1) == 0
 
-    col_depth = (half_col, jnp.where(half_col == 0, 2, 0), half_col + 1)
+    col_depth = (half_col, 2, half_col)
     low = [mask(half_row, d) for d in col_depth]
     top = [mask(2, d) for d in col_depth]
 
-    halves = small.astype(jnp.float32)
     turned = pltpu.roll(halves, fn_count, axis=1)
-    upper = iota(halves.shape, 1) < fn_count
     expand = jnp.where(
         (iota((LANES, full), 0) == iota((LANES, full), 1) // SUBLANES * fn_count + iota((LANES, full), 1) % fn_count)
         & (iota((LANES, full), 0) < width),
@@ -377,12 +453,7 @@
         axis=0,
     )
 
-    stacked = [
-        jnp.concatenate([in_ref[:, part * tiles + t].reshape(full, LANES) for t in range(tiles)], axis=1)
-        for part in range(3)
-    ]
     grad = dot(mixed, jnp.concatenate(stacked, axis=0))
-    upper = iota((devices, SUBLANES, LANES), 1) < fn_count
     for t in range(tiles):
         out_ref[:, t] = (
             grad[:full, t * LANES : (t + 1) * LANES].reshape(devices, SUBLANES, LANES).astype(jnp.bfloat16)
@@ -410,12 +481,15 @@
     out_ref[:, tiles + (tiles + 1) // 2] = bands.astype(jnp.bfloat16)
 
 
-def receive_kernel(dims, offs_ref, in_ref, grad_ref, margin_ref, energy_ref):
+def receive_kernel(dims, offs_hbm, in_ref, grad_ref, margin_ref, energy_ref, offs_ref, sem):
     fn_count, edge, plane_len, classes, shares, band_reach, sub_count = dims
     tiles = plane_len // LANES // shares
     rows = fn_count * edge
     devices = classes * shares
     width = margin_ref.shape[1]
+    copy = pltpu.make_async_copy(offs_hbm, offs_ref, sem)
+    copy.start()
+    copy.wait()
     rank = lax.axis_index("brick") * sub_count + lax.axis_index("sub")
     offs = [offs_ref[k] for k in range(fn_count)]
     inner = classes * SUBLANES
@@ -481,34 +555,86 @@
     band_reach = 2 * K
     chunk = edge * SUBLANES
     reach = -(-filter_reach // SUBLANES)
-    params = pltpu.CompilerParams(vmem_limit_bytes=56 * 2**20)
-    smem = pl.BlockSpec(memory_space=pltpu.SMEM)
+    params = pltpu.CompilerParams(vmem_limit_bytes=20 * 2**20)
     vmem = pl.BlockSpec(memory_space=pltpu.VMEM)
 
+    hbm = pl.BlockSpec(memory_space=pltpu.HBM)
+    groups = 4
+    near = devices // groups
     kinetic = np.kron(np.eye(fn_count, dtype=np.float32), kinetic_numpy(edge)).astype(jnp.bfloat16)
     cross = cross_stack(edge, SUBLANES, reach)
-    units = 3 * tiles + 1
-    sent = pl.pallas_call(
-        functools.partial(send_kernel, (fn_count, edge, plane_len, classes, shares, chunk, reach)),
-        out_shape=jax.ShapeDtypeStruct((classes, shares, units, SUBLANES, LANES), jnp.bfloat16),
-        in_specs=[smem] + [vmem] * 7,
+    units = tiles + (tiles + 1) // 2 * 2
+    offsets = in_hbm(offsets)
+
+    def block(*lead):
+        return jax.ShapeDtypeStruct((*lead, SUBLANES, LANES), jnp.bfloat16)
+
+    def cost(flops, moved):
+        return pl.CostEstimate(flops=flops, bytes_accessed=moved, transcendentals=0)
+
+    def exchange(array, bits):
+        return lax.ppermute(array, axes, [(i, i ^ bits) for i in range(devices)])
+
+    axes = ("brick", "sub")
+    size = psi.size
+    kinetic, cross = jnp.asarray(kinetic), jnp.asarray(cross)
+    carried = (psi, potential, cross, kinetic, kernel, multipliers, pattern)
+    results = pl.pallas_call(
+        functools.partial(
+            pack_kernel, (fn_count, edge, plane_len, classes, shares, groups, sub_count, len(carried))
+        ),
+        out_shape=[block(near // shares, shares, tiles)] * groups
+        + [jax.ShapeDtypeStruct(x.shape, x.dtype) for x in carried],
+        in_specs=[hbm] * (1 + len(carried)),
+        out_specs=[vmem] * (groups + len(carried)),
+        scratch_shapes=[
+            pltpu.SMEM(offsets.shape, offsets.dtype),
+            pltpu.SemaphoreType.DMA((1 + len(carried),)),
+        ],
+        compiler_params=params,
+        cost_estimate=cost(512 * size, 4 * size),
+        name="pack",
+    )(offsets, *(in_hbm(x) for x in carried))
+    packed, kept = results[:groups], results[groups:]
+    packed = [x.reshape(near, tiles, SUBLANES, LANES) for x in packed]
+    arrived = [None] * groups
+    arrived[0] = packed[0]
+    for far in (3, 2, 1):
+        arrived[far] = exchange(packed[far], far * near)
+
+    applied = pl.pallas_call(
+        functools.partial(apply_kernel, (fn_count, edge, plane_len, classes, shares, chunk, reach)),
+        out_shape=block(classes, shares, units),
+        in_specs=[hbm] + [vmem] * len(kept),
         out_specs=vmem,
+        scratch_shapes=[pltpu.SMEM(offsets.shape, offsets.dtype), pltpu.SemaphoreType.DMA((1,))],
         compiler_params=params,
-        name="send",
-    )(offsets, psi, potential, jnp.asarray(kinetic), jnp.asarray(cross), kernel, multipliers, pattern)
-    sent = sent.reshape(devices, units, SUBLANES, LANES)
-    axes = ("brick", "sub")
-    held = lax.all_to_all(sent, axes, 0, 0, tiled=True)
+        cost_estimate=cost(4608 * size, 8 * size),
+        name="apply",
+    )(offsets, *kept)
+    held = lax.all_to_all(applied.reshape(devices, units, SUBLANES, LANES), axes, 0, 0, tiled=True)
+
+    turned = pl.pallas_call(
+        turn_kernel,
+        out_shape=[block(groups, tiles)] * near,
+        in_specs=[vmem] * groups,
+        out_specs=[vmem] * near,
+        compiler_params=params,
+        cost_estimate=cost(0, 4 * size),
+        name="turn",
+    )(*arrived)
+    gathered = [x if n == 0 else exchange(x, n) for n, x in enumerate(turned)]
 
     back_units = tiles + (tiles + 1) // 2 + 1
     made = pl.pallas_call(
         functools.partial(grid_kernel, (fn_count, edge, classes, shares, width, band_reach, sub_count)),
         out_shape=jax.ShapeDtypeStruct((devices, back_units, SUBLANES, LANES), jnp.bfloat16),
-        in_specs=[vmem],
+        in_specs=[vmem] * (near + 1),
         out_specs=vmem,
+        scratch_shapes=[pltpu.VMEM((devices, tiles, SUBLANES, LANES), jnp.bfloat16)],
         compiler_params=params,
         name="grid",
-    )(held)
+    )(*gathered, held)
     back = lax.all_to_all(made, axes, 0, 0, tiled=True)
     back = back.reshape(classes, shares, back_units, SUBLANES, LANES)
     return pl.pallas_call(
@@ -518,8 +644,9 @@
             jax.ShapeDtypeStruct((fn_count, width), jnp.float32),
             jax.ShapeDtypeStruct((fn_count, width), jnp.float32),
         ),
-        in_specs=[smem, vmem],
+        in_specs=[pl.BlockSpec(memory_space=pltpu.HBM), vmem],
         out_specs=(vmem, vmem, vmem),
+        scratch_shapes=[pltpu.SMEM(offsets.shape, offsets.dtype), pltpu.SemaphoreType.DMA],
         compiler_params=params,
         name="receive",
     )(offsets, back)

time: 95 us -> 102 us (1.074)
  blocking collectives: 79 us -> 28.7 us
  waiting for transfers between devices: 0 us -> 41.7 us
  starting transfers between devices: 0 us -> 18.1 us
  Pallas kernels: 15 us -> 12.5 us
    all_to_all x1 -> x0, blocking collectives: 50.5 us -> none  [transposed_shards(): held = lax.all_to_all(sent, axes, 0, 0, tiled=True)]
    ppermute x0 -> x10, waiting for transfers between devices: none -> 41.7 us  [exchange(): return lax.ppermute(array, axes, [(i, i ^ bits) for i in range(devices)])]
    ppermute x0 -> x10, starting transfers between devices: none -> 10.8 us  [exchange(): return lax.ppermute(array, axes, [(i, i ^ bits) for i in range(devices)])]
    all_to_all x0 -> x1, starting transfers between devices: none -> 7.33 us  [transposed_shards(): lax.all_to_all(applied.reshape(devices, units, SUBLANES, LANES), axes, 0,...]
    pallas_call x1, Pallas kernels: 5.19 us -> 2.81 us  [transposed_shards(): pl.pallas_call(functools.partial(grid_kernel, (fn_count, edge, classes, s...]
    pallas_call x1 -> x3, Pallas kernels: 7.22 us -> 7.6 us  [the longest x1 5.56 us: transposed_shards(): pl.pallas_call(functools.partial(apply_kernel, (fn_count, edge, plane_len...]
  transfers between devices with their start and end apart: 0 -> 11, of which waited for: 0 -> 6; matrix products, arithmetic and copies ran while one was open for 0% -> 0% of each run, Pallas kernels for 0% -> 0%
where the time goes in v3:
time: 102 us
  waiting for transfers between devices  41.7 us (41%)
  blocking collectives  28.7 us (28%)
  starting transfers between devices  18.1 us (18%)
  Pallas kernels  12.5 us (12%)
    ppermute x10, waiting for transfers between devices, exchange(): return lax.ppermute(array, axes, [(i, i ^ bits) for i in range(devices)])  41.7 us
    all_to_all x1, blocking collectives, transposed_shards(): back = lax.all_to_all(made, axes, 0, 0, tiled=True)  28.7 us
    ppermute x10, starting transfers between devices, exchange(): return lax.ppermute(array, axes, [(i, i ^ bits) for i in range(devices)])  10.8 us
    all_to_all x1, starting transfers between devices, transposed_shards(): lax.all_to_all(applied.reshape(devices, units, SUBLANES, LANES), axes, 0,...  7.33 us
    pallas_call x1, Pallas kernels, transposed_shards(): pl.pallas_call(functools.partial(apply_kernel, (fn_count, edge, plane_len...  5.56 us
    pallas_call x1, Pallas kernels, transposed_shards(): pl.pallas_call(functools.partial(grid_kernel, (fn_count, edge, classes, s...  2.81 us
    pallas_call x1, Pallas kernels, transposed_shards(): pl.pallas_call(functools.partial(receive_kernel, (fn_count, edge, plane_l...  2.07 us
  transfers between devices with their start and end apart: 11, of which 6 were waited for; matrix products, arithmetic and copies ran while one was open for 0% of the time, Pallas kernels for 0%

profile of v3, /device:TPU:0, one launch (start us, length us, event | category | flops | bytes accessed | tf_op | source)
XLA Modules:
  0.0 101.7 jit_solution(9500620351784228087)
XLA Ops:
  0.6 2.0 %pack.1 = (bf16[4,2,9,8,128]{4,3,2,1,0:T(8,128)(2,1)S(1)}, bf16[4,2,9,8,128]{4,3,2,1,0:T(8,128)(2,1)S(1)}, bf16[4,2,9,8,128]{4,3,2,1,0:T(8,128)(2,1)S(1)}, bf16[...) custom-call(s32[4]{0:T(128)} %offs_hbm.5, ...), custom_call_target="tpu_custom_call" | custom-call | flops 226492416 | bytes 1769472 | tf_op jit(solution)/shard_map/pack/pallas_call | solution.py:582
  2.6 5.6 %apply.1 = bf16[16,2,19,8,128]{4,3,2,1,0:T(8,128)(2,1)} custom-call(s32[4]{0:T(128)} %offs_hbm.5, bf16[4,48,2304]{2,1,0:T(8,128)(2,1)S(1)} %get-tuple-element.34.psi_ref, bf16[4,48,2304]{2,1,0:T(8,128)(2,1)S(1)} %get-tuple-element.35.pot_ref, bf16[1920,384]{1,0:T(8,128)(2,1)S(1)} %get-tuple-element.36.cross_ref, ...), custom_call_target="tpu_custom_call" | custom-call | flops 2038431744 | bytes 3538944 | tf_op jit(solution)/shard_map/apply/pallas_call | solution.py:605
  8.2 7.3 %all-to-all-start = ((bf16[32,19,8,128]{3,2,1,0:T(8,128)(2,1)}), bf16[32,19,8,128]{3,2,1,0:T(8,128)(2,1)S(1)}, u32[]{:S(2)}, u32[]{:S(2)}) async-start(bf16[32,19,8,128]{3,2,1,0:T(8,128)(2,1)} %bitcast.4), calls=%async_computation | async-start | bytes 2490368 | tf_op jit(solution)/shard_map/all_to_all | solution.py:615
  15.5 1.8 %collective-permute-start = (bf16[8,9,8,128]{3,2,1,0:T(8,128)(2,1)S(1)}, bf16[8,9,8,128]{3,2,1,0:T(8,128)(2,1)S(1)}, u32[]{:S(2)}, u32[]{:S(2)}) collective-permute-start(bf16[8,9,8,128]{3,2,1,0:T(8,128)(2,1)S(1)} %bitcast.10), channel_id=1, source_target_pairs={{0,8},{1,9},{2,10},{3,11},{4,12},{5,13},{6,14},{7,15},{8,0},{9,1},... | collective-permute-start | bytes 442376 | tf_op jit(solution)/shard_map/ppermute | solution.py:576
  17.4 2.4 %collective-permute-start.1 = (bf16[8,9,8,128]{3,2,1,0:T(8,128)(2,1)S(1)}, bf16[8,9,8,128]{3,2,1,0:T(8,128)(2,1)S(1)}, u32[]{:S(2)}, u32[]{:S(2)}) collective-permute-start(bf16[8,9,8,128]{3,2,1,0:T(8,128)(2,1)S(1)} %bitcast.9), channel_id=1, source_target_pairs={{0,16},{1,17},{2,18},{3,19},{4,20},{5,21},{6,22},{7,23},{8,24},{9,... | collective-permute-start | bytes 442376 | tf_op jit(solution)/shard_map/ppermute | solution.py:576
  19.8 0.2 collective-permute-start.2
  20.0 19.8 %collective-permute-done.refs_1_ = bf16[8,9,8,128]{3,2,1,0:T(8,128)(2,1)S(1)} collective-permute-done((bf16[8,9,8,128]{3,2,1,0:T(8,128)(2,1)S(1)}, bf16[8,9,8,128]{3,2,1,0:T(8,128)(2,1)S(1)}, u32[]{:S(2)}, u32[]{:S(2)}) %collective-permute-start) | collective-permute-done | bytes 147488 | tf_op jit(solution)/shard_map/ppermute | solution.py:576
  39.8 16.2 %collective-permute-done.1.refs_2_ = bf16[8,9,8,128]{3,2,1,0:T(8,128)(2,1)S(1)} collective-permute-done((bf16[8,9,8,128]{3,2,1,0:T(8,128)(2,1)S(1)}, bf16[8,9,8,128]{3,2,1,0:T(8,128)(2,1)S(1)}, u32[]{:S(2)}, u32[]{:S(2)}) %collective-permute-start.1) | collective-permute-done | bytes 147488 | tf_op jit(solution)/shard_map/ppermute | solution.py:576
  56.0 0.0 collective-permute-done.2.refs_3_
  56.1 0.1 collective-permute-start.3
  56.1 1.6 %collective-permute-start.4 = (bf16[4,9,8,128]{3,2,1,0:T(8,128)(2,1)S(1)}, bf16[4,9,8,128]{3,2,1,0:T(8,128)(2,1)S(1)}, u32[]{:S(2)}, u32[]{:S(2)}) collective-permute-start(bf16[4,9,8,128]{3,2,1,0:T(8,128)(2,1)S(1)} %get-tuple-element.28), channel_id=1, source_target_pairs={{0,2},{1,3},{2,0},{3,1},{4,6},{5,7},{6,4},{7,5},{8,10},{9,11},{10,... | collective-permute-start | bytes 221192 | tf_op jit(solution)/shard_map/ppermute | solution.py:576
  57.7 0.3 collective-permute-start.5
  58.0 1.5 %collective-permute-start.6 = (bf16[4,9,8,128]{3,2,1,0:T(8,128)(2,1)S(1)}, bf16[4,9,8,128]{3,2,1,0:T(8,128)(2,1)S(1)}, u32[]{:S(2)}, u32[]{:S(2)}) collective-permute-start(bf16[4,9,8,128]{3,2,1,0:T(8,128)(2,1)S(1)} %get-tuple-element.30), channel_id=1, source_target_pairs={{0,4},{1,5},{2,6},{3,7},{4,0},{5,1},{6,2},{7,3},{8,12},{9,13},{10,... | collective-permute-start | bytes 221192 | tf_op jit(solution)/shard_map/ppermute | solution.py:576
  59.5 0.2 collective-permute-start.7
  59.7 0.0 collective-permute-done.3.refs_1_
  59.7 2.4 %collective-permute-start.8 = (bf16[4,9,8,128]{3,2,1,0:T(8,128)(2,1)S(1)}, bf16[4,9,8,128]{3,2,1,0:T(8,128)(2,1)S(1)}, u32[]{:S(2)}, u32[]{:S(2)}) collective-permute-start(bf16[4,9,8,128]{3,2,1,0:T(8,128)(2,1)S(1)} %get-tuple-element.32), channel_id=1, source_target_pairs={{0,6},{1,7},{2,4},{3,5},{4,2},{5,3},{6,0},{7,1},{8,14},{9,15},{10,... | collective-permute-start | bytes 221192 | tf_op jit(solution)/shard_map/ppermute | solution.py:576
  62.1 0.0 collective-permute-done.4.refs_2_
  62.1 0.3 collective-permute-start.9
  62.4 0.0 collective-permute-done.5.refs_3_
  62.4 0.2 collective-permute-done.6.refs_4_
  62.6 1.3 %collective-permute-done.7.refs_5_ = bf16[4,9,8,128]{3,2,1,0:T(8,128)(2,1)S(1)} collective-permute-done((bf16[4,9,8,128]{3,2,1,0:T(8,128)(2,1)S(1)}, bf16[4,9,8,128]{3,2,1,0:T(8,128)(2,1)S(1)}, u32[]{:S(2)}, u32[]{:S(2)}) %collective-permute-start.7) | collective-permute-done | bytes 73760 | tf_op jit(solution)/shard_map/ppermute | solution.py:576
  63.9 2.9 %collective-permute-done.8.refs_6_ = bf16[4,9,8,128]{3,2,1,0:T(8,128)(2,1)S(1)} collective-permute-done((bf16[4,9,8,128]{3,2,1,0:T(8,128)(2,1)S(1)}, bf16[4,9,8,128]{3,2,1,0:T(8,128)(2,1)S(1)}, u32[]{:S(2)}, u32[]{:S(2)}) %collective-permute-start.8) | collective-permute-done | bytes 73760 | tf_op jit(solution)/shard_map/ppermute | solution.py:576
  66.8 1.3 %collective-permute-done.9.refs_7_ = bf16[4,9,8,128]{3,2,1,0:T(8,128)(2,1)S(1)} collective-permute-done((bf16[4,9,8,128]{3,2,1,0:T(8,128)(2,1)S(1)}, bf16[4,9,8,128]{3,2,1,0:T(8,128)(2,1)S(1)}, u32[]{:S(2)}, u32[]{:S(2)}) %collective-permute-start.9) | collective-permute-done | bytes 73760 | tf_op jit(solution)/shard_map/ppermute | solution.py:576
  68.1 0.0 all-to-all-done.refs_8_
  68.1 2.8 %grid.1 = bf16[32,15,8,128]{3,2,1,0:T(8,128)(2,1)S(1)} custom-call(bf16[4,9,8,128]{3,2,1,0:T(8,128)(2,1)S(1)} %get-tuple-element.26.refs_0_, bf16[4,9,8,128]{3,2,1,0:T(8,128)(2,1)S(1)} %collective-permute-done.3.refs_1_, bf16[4,9,8,128]{3,2,1,0:T(8,128)(2,1)S(1)} %collective-permute-done.4.refs_2_, ...), custom_call_target="tpu_custom_call" | custom-call | tf_op jit(solution)/shard_map/grid/pallas_call | solution.py:629
  70.9 28.7 %all_to_all.10 = bf16[32,15,8,128]{3,2,1,0:T(8,128)(2,1)S(1)} all-to-all(bf16[32,15,8,128]{3,2,1,0:T(8,128)(2,1)S(1)} %grid.1), channel_id=1, replica_groups=mesh['brick'=8,'sub'=4] {'brick','sub'}, dimensions={0} | all-to-all | bytes 1966080 | tf_op jit(solution)/shard_map/all_to_all | solution.py:638
  99.6 2.1 %receive.1 = (bf16[4,48,2304]{2,1,0:T(8,128)(2,1)}, f32[4,100]{1,0:T(4,128)}, f32[4,100]{1,0:T(4,128)}) custom-call(s32[4]{0:T(128)} %offs_hbm.5, bf16[16,2,15,8,128]{4,3,2,1,0:T(8,128)(2,1)S(1)} %bitcast.6), custom_call_target="tpu_custom_call" | custom-call | tf_op jit(solution)/shard_map/receive/pallas_call | solution.py:640
  (1 shorter events, 0.0 us)
Async XLA Ops:
  8.2 59.9 %all-to-all-start = ((bf16[32,19,8,128]{3,2,1,0:T(8,128)(2,1)}), bf16[32,19,8,128]{3,2,1,0:T(8,128)(2,1)S(1)}, u32[]{:S(2)}, u32[]{:S(2)}) async-start(bf16[32,19,8,128]{3,2,1,0:T(8,128)(2,1)} %bitcast.4), calls=%async_computation | async-start | bytes 2490368 | tf_op jit(solution)/shard_map/all_to_all | solution.py:615
  15.5 24.3 %collective-permute-start = (bf16[8,9,8,128]{3,2,1,0:T(8,128)(2,1)S(1)}, bf16[8,9,8,128]{3,2,1,0:T(8,128)(2,1)S(1)}, u32[]{:S(2)}, u32[]{:S(2)}) collective-permute-start(bf16[8,9,8,128]{3,2,1,0:T(8,128)(2,1)S(1)} %bitcast.10), channel_id=1, source_target_pairs={{0,8},{1,9},{2,10},{3,11},{4,12},{5,13},{6,14},{7,15},{8,0},{9,1},... | collective-permute-start | bytes 442376 | tf_op jit(solution)/shard_map/ppermute | solution.py:576
  17.4 38.6 %collective-permute-start.1 = (bf16[8,9,8,128]{3,2,1,0:T(8,128)(2,1)S(1)}, bf16[8,9,8,128]{3,2,1,0:T(8,128)(2,1)S(1)}, u32[]{:S(2)}, u32[]{:S(2)}) collective-permute-start(bf16[8,9,8,128]{3,2,1,0:T(8,128)(2,1)S(1)} %bitcast.9), channel_id=1, source_target_pairs={{0,16},{1,17},{2,18},{3,19},{4,20},{5,21},{6,22},{7,23},{8,24},{9,... | collective-permute-start | bytes 442376 | tf_op jit(solution)/shard_map/ppermute | solution.py:576
  19.8 36.2 %collective-permute-start.2 = (bf16[8,9,8,128]{3,2,1,0:T(8,128)(2,1)S(1)}, bf16[8,9,8,128]{3,2,1,0:T(8,128)(2,1)S(1)}, u32[]{:S(2)}, u32[]{:S(2)}) collective-permute-start(bf16[8,9,8,128]{3,2,1,0:T(8,128)(2,1)S(1)} %bitcast.8), channel_id=1, source_target_pairs={{0,24},{1,25},{2,26},{3,27},{4,28},{5,29},{6,30},{7,31},{8,16},{9,... | collective-permute-start | bytes 442376 | tf_op jit(solution)/shard_map/ppermute | solution.py:576
  56.1 3.6 %collective-permute-start.3 = (bf16[4,9,8,128]{3,2,1,0:T(8,128)(2,1)S(1)}, bf16[4,9,8,128]{3,2,1,0:T(8,128)(2,1)S(1)}, u32[]{:S(2)}, u32[]{:S(2)}) collective-permute-start(bf16[4,9,8,128]{3,2,1,0:T(8,128)(2,1)S(1)} %get-tuple-element.27), channel_id=1, source_target_pairs={{0,1},{1,0},{2,3},{3,2},{4,5},{5,4},{6,7},{7,6},{8,9},{9,8},{10,11... | collective-permute-start | bytes 221192 | tf_op jit(solution)/shard_map/ppermute | solution.py:576
  56.1 6.0 %collective-permute-start.4 = (bf16[4,9,8,128]{3,2,1,0:T(8,128)(2,1)S(1)}, bf16[4,9,8,128]{3,2,1,0:T(8,128)(2,1)S(1)}, u32[]{:S(2)}, u32[]{:S(2)}) collective-permute-start(bf16[4,9,8,128]{3,2,1,0:T(8,128)(2,1)S(1)} %get-tuple-element.28), channel_id=1, source_target_pairs={{0,2},{1,3},{2,0},{3,1},{4,6},{5,7},{6,4},{7,5},{8,10},{9,11},{10,... | collective-permute-start | bytes 221192 | tf_op jit(solution)/shard_map/ppermute | solution.py:576
  57.7 4.7 %collective-permute-start.5 = (bf16[4,9,8,128]{3,2,1,0:T(8,128)(2,1)S(1)}, bf16[4,9,8,128]{3,2,1,0:T(8,128)(2,1)S(1)}, u32[]{:S(2)}, u32[]{:S(2)}) collective-permute-start(bf16[4,9,8,128]{3,2,1,0:T(8,128)(2,1)S(1)} %get-tuple-element.29), channel_id=1, source_target_pairs={{0,3},{1,2},{2,1},{3,0},{4,7},{5,6},{6,5},{7,4},{8,11},{9,10},{10,... | collective-permute-start | bytes 221192 | tf_op jit(solution)/shard_map/ppermute | solution.py:576
  58.0 4.6 %collective-permute-start.6 = (bf16[4,9,8,128]{3,2,1,0:T(8,128)(2,1)S(1)}, bf16[4,9,8,128]{3,2,1,0:T(8,128)(2,1)S(1)}, u32[]{:S(2)}, u32[]{:S(2)}) collective-permute-start(bf16[4,9,8,128]{3,2,1,0:T(8,128)(2,1)S(1)} %get-tuple-element.30), channel_id=1, source_target_pairs={{0,4},{1,5},{2,6},{3,7},{4,0},{5,1},{6,2},{7,3},{8,12},{9,13},{10,... | collective-permute-start | bytes 221192 | tf_op jit(solution)/shard_map/ppermute | solution.py:576
  59.5 4.5 %collective-permute-start.7 = (bf16[4,9,8,128]{3,2,1,0:T(8,128)(2,1)S(1)}, bf16[4,9,8,128]{3,2,1,0:T(8,128)(2,1)S(1)}, u32[]{:S(2)}, u32[]{:S(2)}) collective-permute-start(bf16[4,9,8,128]{3,2,1,0:T(8,128)(2,1)S(1)} %get-tuple-element.31), channel_id=1, source_target_pairs={{0,5},{1,4},{2,7},{3,6},{4,1},{5,0},{6,3},{7,2},{8,13},{9,12},{10,... | collective-permute-start | bytes 221192 | tf_op jit(solution)/shard_map/ppermute | solution.py:576
  59.7 7.1 %collective-permute-start.8 = (bf16[4,9,8,128]{3,2,1,0:T(8,128)(2,1)S(1)}, bf16[4,9,8,128]{3,2,1,0:T(8,128)(2,1)S(1)}, u32[]{:S(2)}, u32[]{:S(2)}) collective-permute-start(bf16[4,9,8,128]{3,2,1,0:T(8,128)(2,1)S(1)} %get-tuple-element.32), channel_id=1, source_target_pairs={{0,6},{1,7},{2,4},{3,5},{4,2},{5,3},{6,0},{7,1},{8,14},{9,15},{10,... | collective-permute-start | bytes 221192 | tf_op jit(solution)/shard_map/ppermute | solution.py:576
  62.1 6.0 %collective-permute-start.9 = (bf16[4,9,8,128]{3,2,1,0:T(8,128)(2,1)S(1)}, bf16[4,9,8,128]{3,2,1,0:T(8,128)(2,1)S(1)}, u32[]{:S(2)}, u32[]{:S(2)}) collective-permute-start(bf16[4,9,8,128]{3,2,1,0:T(8,128)(2,1)S(1)} %get-tuple-element.33), channel_id=1, source_target_pairs={{0,7},{1,6},{2,5},{3,4},{4,3},{5,2},{6,1},{7,0},{8,15},{9,14},{10,... | collective-permute-start | bytes 221192 | tf_op jit(solution)/shard_map/ppermute | solution.py:576

commit v4 on v3

--- a/solution.py
+++ b/solution.py
@@ -167,6 +167,7 @@
     return (gradient, margin_sum, energy_sum)
 
 
+EARLY_PAIRS = 1
 SUBLANES = 8
 LANES = 128
 
@@ -183,8 +184,9 @@
         classes = devices // shares
         per_class = edge_len // classes
         fits = (
-            plane_len % LANES == 0
+            plane_len % (2 * LANES) == 0
             and edge_len % classes == 0
+            and tiles // shares > 2 * EARLY_PAIRS
             and (devices * Q) % classes == 0
             and classes & (classes - 1) == 0
             and fn_count * 2 == SUBLANES
@@ -209,18 +211,21 @@
     return entries.astype(np.float32)
 
 
-def cross_stack(edge_len, rows, reach):
-    kin = kinetic_numpy(edge_len).astype(jnp.bfloat16).astype(np.float32)
-    line = kin[0]
-    blocks = []
-    for step in range(-reach, reach + 1):
-        gap = np.abs(np.arange(rows)[:, None] + step * rows - np.arange(rows)[None, :])
-        along_y = np.where(gap <= filter_reach, line[np.minimum(gap, edge_len - 1)], 0.0)
-        block = np.kron(along_y, np.eye(edge_len, dtype=np.float32))
-        if step == 0:
-            block = block + np.kron(np.eye(rows, dtype=np.float32), kin)
-        blocks.append(block)
-    return np.concatenate(blocks, axis=0).astype(jnp.bfloat16)
+def cross_blocks(edge_len, chunk):
+    line = kinetic_numpy(edge_len).astype(jnp.bfloat16).astype(np.float32)[0]
+    period = math.lcm(edge_len, chunk)
+    reach = -(-filter_reach * edge_len // chunk)
+    stacks = []
+    for first in range(0, period, chunk):
+        row = np.arange(first - reach * chunk, first + (reach + 1) * chunk)[:, None]
+        col = np.arange(first, first + chunk)[None, :]
+        gap_y = np.abs(row // edge_len - col // edge_len)
+        gap_z = np.abs(row % edge_len - col % edge_len)
+        weight = np.where(np.arange(edge_len) <= filter_reach, line, 0.0)
+        block = np.where(gap_z == 0, weight[np.minimum(gap_y, edge_len - 1)], 0.0)
+        block = block + np.where(gap_y == 0, weight[gap_z], 0.0)
+        stacks.append(block)
+    return np.stack(stacks).astype(jnp.bfloat16), reach
 
 
 def dot(a, b):
@@ -249,12 +254,13 @@
     return copies
 
 
-def class_select(target, offs, fn_count, edge, classes, least=0):
+def class_select(target, off_rows, fn_count, edge, classes, least=0):
     shape = target.shape
     item, lane = iota(shape, 1), iota(shape, 2)
     member = item % fn_count
     depth = jnp.minimum(item // fn_count + least, 2)
-    inner = jnp.bitwise_and(target - pick(member, offs), classes - 1)
+    off_rows = jnp.concatenate([off_rows] * (shape[1] // SUBLANES), axis=0)[None]
+    inner = jnp.bitwise_and(target - off_rows, classes - 1)
     source = member * edge + depth * classes + inner
     rows = fn_count * edge
     wide = [
@@ -264,7 +270,7 @@
     return jnp.concatenate(wide, axis=2).reshape(shape[0] * shape[1], -1)[:, :rows]
 
 
-def coefficient_rows(band, pattern, offs, fn_count):
+def coefficient_rows(band, pattern, off_rows, fn_count):
     width, blocks = band.shape[1], pattern.shape[1]
     spread = jnp.where(
         iota((blocks, width), 1) // fn_count == iota((blocks, width), 0), 1.0, 0.0
@@ -272,16 +278,24 @@
     small = band.astype(jnp.float32) * dot(pattern.astype(jnp.float32).astype(jnp.bfloat16), spread)
     small = jnp.concatenate([small, small], axis=0)
     small = jnp.concatenate([small, jnp.zeros((SUBLANES, LANES - width), jnp.float32)], axis=1)
-    at, lane = iota((SUBLANES, LANES), 0), iota((SUBLANES, LANES), 1)
-    off = pick(at % fn_count, offs)
-    small = jnp.where(lane == width, (off // 256).astype(jnp.float32), small)
-    return jnp.where(lane == width + 1, (off % 256).astype(jnp.float32), small)
+    lane = iota((SUBLANES, LANES), 1)
+    small = jnp.where(lane == width, jnp.right_shift(off_rows, 8).astype(jnp.float32), small)
+    return jnp.where(lane == width + 1, jnp.bitwise_and(off_rows, 255).astype(jnp.float32), small)
+
+
+def pair_units(deep, count, upper, last):
+    made = []
+    for t in range(0, count, 2):
+        even = deep[..., t * LANES : (t + 1) * LANES]
+        odd = deep[..., (t + 1) * LANES : (t + 2) * LANES] if t + 1 < count else last
+        made.append(jnp.where(upper, even, odd).astype(jnp.bfloat16))
+    return made
 
 
 def pack_kernel(dims, offs_hbm, *refs):
     fn_count, edge, plane_len, classes, shares, groups, sub_count, carried = dims
-    sources, outs, kept = refs[:carried], refs[carried : carried + groups], refs[carried + groups : -2]
-    offs_ref, sems = refs[-2:]
+    sources, outs, kept = refs[:carried], refs[carried : carried + groups], refs[carried + groups : -4]
+    off_rows_ref, off_lanes_ref, offs_ref, sems = refs[-4:]
     copies = fetch(((offs_hbm, offs_ref), *zip(sources, kept)), sems)
     rows = fn_count * edge
     tiles = plane_len // LANES // shares
@@ -290,8 +304,13 @@
     mine = jnp.bitwise_and(rank, shares - 1)
     copies[0].wait()
     offs = [offs_ref[k] for k in range(fn_count)]
+    off_rows = pick(iota((SUBLANES, LANES), 0) % fn_count, offs)
+    off_rows_ref[...] = off_rows
+    off_lanes_ref[...] = pick(iota((SUBLANES, LANES), 1) % fn_count, offs)
     target = jnp.bitwise_xor(iota((classes, SUBLANES, LANES), 0), rank // shares)
-    select = class_select(target, offs, fn_count, edge, classes)
+    select = class_select(target, off_rows, fn_count, edge, classes)
+    deep = class_select(target, off_rows, fn_count, edge, classes, 2)
+    upper = iota((near, SUBLANES, LANES), 1) < fn_count
     copies[1].wait()
     psi = kept[0][...].reshape(rows, plane_len)
     for share in range(shares):
@@ -301,66 +320,71 @@
         for k in range(groups):
             for t in range(tiles):
                 outs[k][:, there, t] = ordered[k, :, :, t * LANES : (t + 1) * LANES].astype(jnp.bfloat16)
+        start = share * tiles * LANES
+        second = dot(deep, psi[:, start : start + 2 * EARLY_PAIRS * LANES])
+        second = second.reshape(groups, near, SUBLANES, 2 * EARLY_PAIRS * LANES)
+        for k in range(groups):
+            for v, piece in enumerate(pair_units(second[k], 2 * EARLY_PAIRS, upper, None)):
+                outs[k][:, there, tiles + v] = piece
     for copy in copies[2:]:
         copy.wait()
 
 
 def apply_kernel(
     dims,
-    offs_hbm,
+    off_rows_ref,
     psi_ref,
     pot_ref,
-    cross_ref,
     kin_ref,
     kern_ref,
     mult_ref,
     patt_ref,
+    cross_hbm,
     out_ref,
-    offs_ref,
+    result_ref,
+    cross_ref,
     sems,
 ):
     fn_count, edge, plane_len, classes, shares, chunk, reach = dims
-    copies = fetch(((offs_hbm, offs_ref),), sems)
+    copies = fetch([(cross_hbm.at[k], cross_ref.at[k]) for k in range(cross_ref.shape[0])], sems)
     rows = fn_count * edge
     tiles = plane_len // LANES // shares
-    pairs = (tiles + 1) // 2
     chunks = plane_len // chunk
     psi = psi_ref[...].reshape(rows, plane_len)
     pot = pot_ref[...].reshape(rows, plane_len)
-    copies[0].wait()
-    offs = [offs_ref[k] for k in range(fn_count)]
+    off_rows = off_rows_ref[...]
     shape = (classes, 2 * SUBLANES, LANES)
-    select = class_select(iota(shape, 0), offs, fn_count, edge, classes)
+    select = class_select(iota(shape, 0), off_rows, fn_count, edge, classes)
     shape = (classes, SUBLANES, LANES)
-    deep = class_select(iota(shape, 0), offs, fn_count, edge, classes, 2)
-    lead = jnp.concatenate([kin_ref[...], deep], axis=0)
+    deep = class_select(iota(shape, 0), off_rows, fn_count, edge, classes, 2)
     patt = patt_ref[...]
-    small = [coefficient_rows(ref[...], patt, offs, fn_count)[None] for ref in (mult_ref, kern_ref)]
+    small = [coefficient_rows(ref[...], patt, off_rows, fn_count)[None] for ref in (mult_ref, kern_ref)]
     upper = iota(shape, 1) < fn_count
-    held = {}
+    led = dot(kin_ref[...], psi)
     for j in range(chunks):
+        if j < len(copies):
+            copies[j].wait()
         lo, hi = max(0, j - reach), min(chunks, j + reach + 1)
         here = slice(j * chunk, (j + 1) * chunk)
         acc = dot(
             psi[:, lo * chunk : hi * chunk],
-            cross_ref[(lo - j + reach) * chunk : (hi - j + reach) * chunk, :],
+            cross_ref[j % cross_ref.shape[0], (lo - j + reach) * chunk : (hi - j + reach) * chunk],
         )
-        led = dot(lead, psi[:, here])
-        acc = acc + led[:rows]
+        acc = acc + led[:, here]
         acc = acc + pot[:, here].astype(jnp.float32) * psi[:, here].astype(jnp.float32)
-        ordered = dot(select, acc.astype(jnp.bfloat16)).reshape(classes, 2, SUBLANES, chunk)
-        deeps = (ordered[:, 1], led[rows:].reshape(classes, SUBLANES, chunk))
-        for n in range(chunk // LANES):
-            share, t = divmod(j * (chunk // LANES) + n, tiles)
-            at = slice(n * LANES, (n + 1) * LANES)
+        result_ref[:, here] = acc.astype(jnp.bfloat16)
+    ordered = dot(select, result_ref[...]).reshape(classes, 2, SUBLANES, plane_len)
+    late = 2 * EARLY_PAIRS
+    for share in range(shares):
+        first, last = share * tiles * LANES, (share + 1) * tiles * LANES
+        for t in range(tiles):
+            at = slice(first + t * LANES, first + (t + 1) * LANES)
             out_ref[:, share, t] = ordered[:, 0, :, at].astype(jnp.bfloat16)
-            for kind in range(2):
-                value = deeps[kind][:, :, at]
-                if t % 2 == 0 and t + 1 < tiles:
-                    held[kind, share] = value
-                    continue
-                pair = (held[kind, share], value) if t % 2 else (value, small[kind])
-                out_ref[:, share, tiles + kind * pairs + t // 2] = jnp.where(upper, *pair).astype(jnp.bfloat16)
+        rest = dot(deep, psi[:, first + late * LANES : last]).reshape(classes, SUBLANES, -1)
+        made = pair_units(ordered[:, 1, :, first:last], tiles, upper, small[0])
+        made += pair_units(rest, tiles - late, upper, small[1])
+        for v, piece in enumerate(made):
+            out_ref[:, share, tiles + v] = piece
 
 
 def turn_kernel(*refs):
@@ -375,7 +399,7 @@
     fn_count, edge, classes, shares, width, band_reach, sub_count = dims
     psi_refs, (h_ref, out_ref, psi_all) = refs[:-3], refs[-3:]
     devices = h_ref.shape[0]
-    tiles = psi_refs[0].shape[1]
+    tiles = psi_refs[0].shape[1] - EARLY_PAIRS
     pairs = (tiles + 1) // 2
     full = devices * SUBLANES
     rank = lax.axis_index("brick") * sub_count + lax.axis_index("sub")
@@ -389,7 +413,9 @@
     upper = iota((devices, SUBLANES, LANES), 1) < fn_count
     both = []
     for v in range(pairs):
-        ours = h_ref[:, tiles + pairs + v].astype(jnp.float32)
+        early = v < EARLY_PAIRS
+        ours = psi_all[:, tiles + v] if early else h_ref[:, tiles + pairs + v - EARLY_PAIRS]
+        ours = ours.astype(jnp.float32)
         theirs = h_ref[:, tiles + v].astype(jnp.float32)
         both.append(jnp.where(upper, ours, pltpu.roll(theirs, fn_count, axis=1)))
         both.append(jnp.where(upper, pltpu.roll(ours, fn_count, axis=1), theirs))
@@ -481,17 +507,13 @@
     out_ref[:, tiles + (tiles + 1) // 2] = bands.astype(jnp.bfloat16)
 
 
-def receive_kernel(dims, offs_hbm, in_ref, grad_ref, margin_ref, energy_ref, offs_ref, sem):
+def receive_kernel(dims, off_lanes_ref, in_ref, grad_hbm, margin_ref, energy_ref, grad_ref, sems):
     fn_count, edge, plane_len, classes, shares, band_reach, sub_count = dims
     tiles = plane_len // LANES // shares
     rows = fn_count * edge
     devices = classes * shares
     width = margin_ref.shape[1]
-    copy = pltpu.make_async_copy(offs_hbm, offs_ref, sem)
-    copy.start()
-    copy.wait()
     rank = lax.axis_index("brick") * sub_count + lax.axis_index("sub")
-    offs = [offs_ref[k] for k in range(fn_count)]
     inner = classes * SUBLANES
 
     shape = (fn_count, edge, inner)
@@ -499,51 +521,61 @@
     slot = iota(shape, 2)
     cls, sub = slot // SUBLANES, slot % SUBLANES
     half, owner_fn = sub // fn_count, sub % fn_count
-    at = jnp.bitwise_and(cls - pick(owner_fn, offs), classes - 1)
+    off_lanes = jnp.concatenate([off_lanes_ref[...]] * (inner // LANES), axis=1)[:1, None]
+    at = jnp.bitwise_and(cls - off_lanes, classes - 1)
     same = owner_fn == member
-    low = jnp.where(same & (plane == at + half * classes), 1.0, 0.0)
+    low = jnp.where(same & (plane == at + half * classes), 1.0, 0.0).astype(jnp.bfloat16)
     top = same & (plane == at + 2 * classes)
+    place = []
     for parity in range(2):
-        tops = jnp.where(top & (half == parity), 1.0, 0.0)
-        place = jnp.concatenate([low.astype(jnp.bfloat16), tops.astype(jnp.bfloat16)], axis=2)
-        place = place.reshape(rows, 2 * inner)
-        columns, spots = [], []
-        for share in range(shares):
-            for t in range(parity, tiles, 2):
-                columns.append(
-                    jnp.concatenate(
-                        [
-                            in_ref[:, share, t].reshape(inner, LANES),
-                            in_ref[:, share, tiles + t // 2].reshape(inner, LANES),
-                        ],
-                        axis=0,
-                    )
+        tops = jnp.where(top & (half == parity), 1.0, 0.0).astype(jnp.bfloat16)
+        place.append(jnp.concatenate([low, tops], axis=2).reshape(rows, 2 * inner))
+    copies = []
+    for share in range(shares):
+        for parity in range(2):
+            columns = [
+                jnp.concatenate(
+                    [
+                        in_ref[:, share, t].reshape(inner, LANES),
+                        in_ref[:, share, tiles + t // 2].reshape(inner, LANES),
+                    ],
+                    axis=0,
                 )
-                spots.append((share * tiles + t) * LANES)
-        placed = dot(place, jnp.concatenate(columns, axis=1)).astype(jnp.bfloat16)
-        for n, spot in enumerate(spots):
-            grad_ref[:, :, spot : spot + LANES] = placed[:, n * LANES : (n + 1) * LANES].reshape(
-                fn_count, edge, LANES
-            )
+                for t in range(parity, tiles, 2)
+            ]
+            placed = dot(place[parity], jnp.concatenate(columns, axis=1)).astype(jnp.bfloat16)
+            for n, t in enumerate(range(parity, tiles, 2)):
+                spot = (share * tiles + t) * LANES
+                grad_ref[:, :, spot : spot + LANES] = placed[:, n * LANES : (n + 1) * LANES].reshape(
+                    fn_count, edge, LANES
+                )
+        part = pl.ds(share * tiles * LANES, tiles * LANES)
+        copies.append(
+            pltpu.make_async_copy(grad_ref.at[:, :, part], grad_hbm.at[:, :, part], sems.at[share])
+        )
+        copies[-1].start()
 
     total = jnp.sum(
         in_ref[:, :, tiles + (tiles + 1) // 2].reshape(devices, SUBLANES, LANES).astype(jnp.float32), axis=0
     )
+    terms = []
+    for _ in range(3):
+        terms.append(total.astype(jnp.bfloat16))
+        total = total - terms[-1].astype(jnp.float32)
+    terms = jnp.concatenate(terms + terms[-1:], axis=0)
     lane, col = iota((LANES, LANES), 0), iota((LANES, LANES), 1)
     partner = lax.rem(rank + col // fn_count - band_reach + devices, devices)
     for kind, ref in ((0, margin_ref), (1, energy_ref)):
         wanted = partner * SUBLANES + kind * fn_count + col % fn_count
-        picked = [
-            lax.dot_general(
-                total,
-                jnp.where(wanted == lane + part * LANES, 1.0, 0.0),
-                (((1,), (0,)), ((), ())),
-                preferred_element_type=jnp.float32,
-                precision=lax.Precision.HIGHEST,
-            )
-            for part in range(2)
-        ]
-        ref[...] = (picked[0][:fn_count] + picked[1][fn_count:])[:, :width]
+        row = jnp.zeros((fn_count, LANES), jnp.float32)
+        for part in range(2):
+            picked = dot(terms, jnp.where(wanted == lane + part * LANES, 1.0, 0.0).astype(jnp.bfloat16))
+            for n in range(3):
+                first = n * SUBLANES + part * fn_count
+                row = row + picked[first : first + fn_count]
+        ref[...] = row[:, :width]
+    for copy in copies:
+        copy.wait()
 
 
 def transposed_shards(classes, shares, psi, potential, offsets, kernel, multipliers, pattern):
@@ -553,8 +585,7 @@
     width = kernel.shape[1]
     tiles = plane_len // LANES // shares
     band_reach = 2 * K
-    chunk = edge * SUBLANES
-    reach = -(-filter_reach // SUBLANES)
+    chunk = 2 * LANES
     params = pltpu.CompilerParams(vmem_limit_bytes=20 * 2**20)
     vmem = pl.BlockSpec(memory_space=pltpu.VMEM)
 
@@ -562,8 +593,9 @@
     groups = 4
     near = devices // groups
     kinetic = np.kron(np.eye(fn_count, dtype=np.float32), kinetic_numpy(edge)).astype(jnp.bfloat16)
-    cross = cross_stack(edge, SUBLANES, reach)
-    units = tiles + (tiles + 1) // 2 * 2
+    cross, reach = cross_blocks(edge, chunk)
+    early = tiles + EARLY_PAIRS
+    units = tiles + (tiles + 1) // 2 * 2 - EARLY_PAIRS
     offsets = in_hbm(offsets)
 
     def block(*lead):
@@ -578,15 +610,16 @@
     axes = ("brick", "sub")
     size = psi.size
     kinetic, cross = jnp.asarray(kinetic), jnp.asarray(cross)
-    carried = (psi, potential, cross, kinetic, kernel, multipliers, pattern)
+    carried = (psi, potential, kinetic, kernel, multipliers, pattern)
     results = pl.pallas_call(
         functools.partial(
             pack_kernel, (fn_count, edge, plane_len, classes, shares, groups, sub_count, len(carried))
         ),
-        out_shape=[block(near // shares, shares, tiles)] * groups
-        + [jax.ShapeDtypeStruct(x.shape, x.dtype) for x in carried],
+        out_shape=[block(near // shares, shares, early)] * groups
+        + [jax.ShapeDtypeStruct(x.shape, x.dtype) for x in carried]
+        + [jax.ShapeDtypeStruct((SUBLANES, LANES), jnp.int32)] * 2,
         in_specs=[hbm] * (1 + len(carried)),
-        out_specs=[vmem] * (groups + len(carried)),
+        out_specs=[vmem] * (groups + len(carried) + 2),
         scratch_shapes=[
             pltpu.SMEM(offsets.shape, offsets.dtype),
             pltpu.SemaphoreType.DMA((1 + len(carried),)),
@@ -595,8 +628,9 @@
         cost_estimate=cost(512 * size, 4 * size),
         name="pack",
     )(offsets, *(in_hbm(x) for x in carried))
-    packed, kept = results[:groups], results[groups:]
-    packed = [x.reshape(near, tiles, SUBLANES, LANES) for x in packed]
+    packed, kept = results[:groups], results[groups:-2]
+    off_rows, off_lanes = results[-2:]
+    packed = [x.reshape(near, early, SUBLANES, LANES) for x in packed]
     arrived = [None] * groups
     arrived[0] = packed[0]
     for far in (3, 2, 1):
@@ -605,18 +639,22 @@
     applied = pl.pallas_call(
         functools.partial(apply_kernel, (fn_count, edge, plane_len, classes, shares, chunk, reach)),
         out_shape=block(classes, shares, units),
-        in_specs=[hbm] + [vmem] * len(kept),
+        in_specs=[vmem] * (1 + len(kept)) + [hbm],
         out_specs=vmem,
-        scratch_shapes=[pltpu.SMEM(offsets.shape, offsets.dtype), pltpu.SemaphoreType.DMA((1,))],
+        scratch_shapes=[
+            pltpu.VMEM((fn_count * edge, plane_len), jnp.bfloat16),
+            pltpu.VMEM(cross.shape, jnp.bfloat16),
+            pltpu.SemaphoreType.DMA((cross.shape[0],)),
+        ],
         compiler_params=params,
         cost_estimate=cost(4608 * size, 8 * size),
         name="apply",
-    )(offsets, *kept)
+    )(off_rows, *kept, in_hbm(cross))
     held = lax.all_to_all(applied.reshape(devices, units, SUBLANES, LANES), axes, 0, 0, tiled=True)
 
     turned = pl.pallas_call(
         turn_kernel,
-        out_shape=[block(groups, tiles)] * near,
+        out_shape=[block(groups, early)] * near,
         in_specs=[vmem] * groups,
         out_specs=[vmem] * near,
         compiler_params=params,
@@ -631,7 +669,7 @@
         out_shape=jax.ShapeDtypeStruct((devices, back_units, SUBLANES, LANES), jnp.bfloat16),
         in_specs=[vmem] * (near + 1),
         out_specs=vmem,
-        scratch_shapes=[pltpu.VMEM((devices, tiles, SUBLANES, LANES), jnp.bfloat16)],
+        scratch_shapes=[pltpu.VMEM((devices, early, SUBLANES, LANES), jnp.bfloat16)],
         compiler_params=params,
         name="grid",
     )(*gathered, held)
@@ -644,12 +682,12 @@
             jax.ShapeDtypeStruct((fn_count, width), jnp.float32),
             jax.ShapeDtypeStruct((fn_count, width), jnp.float32),
         ),
-        in_specs=[pl.BlockSpec(memory_space=pltpu.HBM), vmem],
-        out_specs=(vmem, vmem, vmem),
-        scratch_shapes=[pltpu.SMEM(offsets.shape, offsets.dtype), pltpu.SemaphoreType.DMA],
+        in_specs=[vmem, vmem],
+        out_specs=(hbm, vmem, vmem),
+        scratch_shapes=[pltpu.VMEM(psi.shape, jnp.bfloat16), pltpu.SemaphoreType.DMA((shares,))],
         compiler_params=params,
         name="receive",
-    )(offsets, back)
+    )(off_lanes, back)
 
 
 def any_shards(psi, potential, offsets, kernel, multipliers, pattern):

time: 102 us -> 101 us (level)
  Pallas kernels: 12.5 us -> 11.1 us
where the time goes in v4:
time: 101 us
  waiting for transfers between devices  41.7 us (41%)
  blocking collectives  29.1 us (29%)
  starting transfers between devices  18.3 us (18%)
  Pallas kernels  11.1 us (11%)
    ppermute x10, waiting for transfers between devices, exchange(): return lax.ppermute(array, axes, [(i, i ^ bits) for i in range(devices)])  41.7 us
    all_to_all x1, blocking collectives, transposed_shards(): back = lax.all_to_all(made, axes, 0, 0, tiled=True)  29.1 us
    ppermute x10, starting transfers between devices, exchange(): return lax.ppermute(array, axes, [(i, i ^ bits) for i in range(devices)])  10.9 us
    all_to_all x1, starting transfers between devices, transposed_shards(): lax.all_to_all(applied.reshape(devices, units, SUBLANES, LANES), axes, 0,...  7.33 us
    pallas_call x1, Pallas kernels, transposed_shards(): pl.pallas_call(functools.partial(apply_kernel, (fn_count, edge, plane_len...  4.78 us
    pallas_call x1, Pallas kernels, transposed_shards(): pl.pallas_call(functools.partial(grid_kernel, (fn_count, edge, classes, s...  2.81 us
  transfers between devices with their start and end apart: 11, of which 6 were waited for; matrix products, arithmetic and copies ran while one was open for 0% of the time, Pallas kernels for 0%

profile of v4, /device:TPU:0, one launch (start us, length us, event | category | flops | bytes accessed | tf_op | source)
XLA Modules:
  0.0 100.8 jit_solution(4358488044624228497)
XLA Ops:
  0.6 1.6 %pack.1 = (bf16[4,2,10,8,128]{4,3,2,1,0:T(8,128)(2,1)S(1)}, bf16[4,2,10,8,128]{4,3,2,1,0:T(8,128)(2,1)S(1)}, bf16[4,2,10,8,128]{4,3,2,1,0:T(8,128)(2,1)S(1)}, bf...) custom-call(s32[4]{0:T(128)} %offs_hbm.1, ...), custom_call_target="tpu_custom_call" | custom-call | flops 226492416 | bytes 1769472 | tf_op jit(solution)/shard_map/pack/pallas_call | solution.py:614
  2.3 4.8 %apply.1 = bf16[16,2,18,8,128]{4,3,2,1,0:T(8,128)(2,1)} custom-call(s32[8,128]{1,0:T(8,128)S(1)} %get-tuple-element.36.off_rows_ref, bf16[4,48,2304]{2,1,0:T(8,128)(2,1)S(1)} %get-tuple-element.37.psi_ref, bf16[4,48,2304]{2,1,0:T(8,128)(2,1)S(1)} %get-tuple-element.38.pot_ref, bf16[192,192]{1,0:T(8,128)(2,1)S(1)} %get-tuple-element.39.kin_ref, ...), custom_call_target="tpu_custom_call" | custom-call | flops 2038431744 | bytes 3538944 | tf_op jit(solution)/shard_map/apply/pallas_call | solution.py:639
  7.0 7.3 %all-to-all-start = ((bf16[32,18,8,128]{3,2,1,0:T(8,128)(2,1)}), bf16[32,18,8,128]{3,2,1,0:T(8,128)(2,1)S(1)}, u32[]{:S(2)}, u32[]{:S(2)}) async-start(bf16[32,18,8,128]{3,2,1,0:T(8,128)(2,1)} %bitcast.4), calls=%async_computation | async-start | bytes 2359296 | tf_op jit(solution)/shard_map/all_to_all | solution.py:653
  14.4 1.8 %collective-permute-start = (bf16[8,10,8,128]{3,2,1,0:T(8,128)(2,1)S(1)}, bf16[8,10,8,128]{3,2,1,0:T(8,128)(2,1)S(1)}, u32[]{:S(2)}, u32[]{:S(2)}) collective-permute-start(bf16[8,10,8,128]{3,2,1,0:T(8,128)(2,1)S(1)} %bitcast.10), channel_id=1, source_target_pairs={{0,8},{1,9},{2,10},{3,11},{4,12},{5,13},{6,14},{7,15},{8,0},{9,1},... | collective-permute-start | bytes 491528 | tf_op jit(solution)/shard_map/ppermute | solution.py:608
  16.2 2.4 %collective-permute-start.1 = (bf16[8,10,8,128]{3,2,1,0:T(8,128)(2,1)S(1)}, bf16[8,10,8,128]{3,2,1,0:T(8,128)(2,1)S(1)}, u32[]{:S(2)}, u32[]{:S(2)}) collective-permute-start(bf16[8,10,8,128]{3,2,1,0:T(8,128)(2,1)S(1)} %bitcast.9), channel_id=1, source_target_pairs={{0,16},{1,17},{2,18},{3,19},{4,20},{5,21},{6,22},{7,23},{8,24},{9,... | collective-permute-start | bytes 491528 | tf_op jit(solution)/shard_map/ppermute | solution.py:608
  18.6 0.2 collective-permute-start.2
  18.8 19.1 %collective-permute-done.refs_1_ = bf16[8,10,8,128]{3,2,1,0:T(8,128)(2,1)S(1)} collective-permute-done((bf16[8,10,8,128]{3,2,1,0:T(8,128)(2,1)S(1)}, bf16[8,10,8,128]{3,2,1,0:T(8,128)(2,1)S(1)}, u32[]{:S(2)}, u32[]{:S(2)}) %collective-permute-start) | collective-permute-done | bytes 163872 | tf_op jit(solution)/shard_map/ppermute | solution.py:608
  37.9 16.6 %collective-permute-done.1.refs_2_ = bf16[8,10,8,128]{3,2,1,0:T(8,128)(2,1)S(1)} collective-permute-done((bf16[8,10,8,128]{3,2,1,0:T(8,128)(2,1)S(1)}, bf16[8,10,8,128]{3,2,1,0:T(8,128)(2,1)S(1)}, u32[]{:S(2)}, u32[]{:S(2)}) %collective-permute-start.1) | collective-permute-done | bytes 163872 | tf_op jit(solution)/shard_map/ppermute | solution.py:608
  54.5 0.0 collective-permute-done.2.refs_3_
  54.5 0.1 collective-permute-start.3
  54.6 1.6 %collective-permute-start.4 = (bf16[4,10,8,128]{3,2,1,0:T(8,128)(2,1)S(1)}, bf16[4,10,8,128]{3,2,1,0:T(8,128)(2,1)S(1)}, u32[]{:S(2)}, u32[]{:S(2)}) collective-permute-start(bf16[4,10,8,128]{3,2,1,0:T(8,128)(2,1)S(1)} %get-tuple-element.30), channel_id=1, source_target_pairs={{0,2},{1,3},{2,0},{3,1},{4,6},{5,7},{6,4},{7,5},{8,10},{9,11},{10,... | collective-permute-start | bytes 245768 | tf_op jit(solution)/shard_map/ppermute | solution.py:608
  56.2 0.3 collective-permute-start.5
  56.5 1.5 %collective-permute-start.6 = (bf16[4,10,8,128]{3,2,1,0:T(8,128)(2,1)S(1)}, bf16[4,10,8,128]{3,2,1,0:T(8,128)(2,1)S(1)}, u32[]{:S(2)}, u32[]{:S(2)}) collective-permute-start(bf16[4,10,8,128]{3,2,1,0:T(8,128)(2,1)S(1)} %get-tuple-element.32), channel_id=1, source_target_pairs={{0,4},{1,5},{2,6},{3,7},{4,0},{5,1},{6,2},{7,3},{8,12},{9,13},{10,... | collective-permute-start | bytes 245768 | tf_op jit(solution)/shard_map/ppermute | solution.py:608
  57.9 0.2 collective-permute-start.7
  58.2 0.0 collective-permute-done.3.refs_1_
  58.2 2.4 %collective-permute-start.8 = (bf16[4,10,8,128]{3,2,1,0:T(8,128)(2,1)S(1)}, bf16[4,10,8,128]{3,2,1,0:T(8,128)(2,1)S(1)}, u32[]{:S(2)}, u32[]{:S(2)}) collective-permute-start(bf16[4,10,8,128]{3,2,1,0:T(8,128)(2,1)S(1)} %get-tuple-element.34), channel_id=1, source_target_pairs={{0,6},{1,7},{2,4},{3,5},{4,2},{5,3},{6,0},{7,1},{8,14},{9,15},{10,... | collective-permute-start | bytes 245768 | tf_op jit(solution)/shard_map/ppermute | solution.py:608
  60.6 0.0 collective-permute-done.4.refs_2_
  60.6 0.5 collective-permute-start.9
  61.0 0.0 collective-permute-done.5.refs_3_
  61.0 0.4 collective-permute-done.6.refs_4_
  61.4 1.3 %collective-permute-done.7.refs_5_ = bf16[4,10,8,128]{3,2,1,0:T(8,128)(2,1)S(1)} collective-permute-done((bf16[4,10,8,128]{3,2,1,0:T(8,128)(2,1)S(1)}, bf16[4,10,8,128]{3,2,1,0:T(8,128)(2,1)S(1)}, u32[]{:S(2)}, u32[]{:S(2)}) %collective-permute-start.7) | collective-permute-done | bytes 81952 | tf_op jit(solution)/shard_map/ppermute | solution.py:608
  62.7 3.3 %collective-permute-done.8.refs_6_ = bf16[4,10,8,128]{3,2,1,0:T(8,128)(2,1)S(1)} collective-permute-done((bf16[4,10,8,128]{3,2,1,0:T(8,128)(2,1)S(1)}, bf16[4,10,8,128]{3,2,1,0:T(8,128)(2,1)S(1)}, u32[]{:S(2)}, u32[]{:S(2)}) %collective-permute-start.8) | collective-permute-done | bytes 81952 | tf_op jit(solution)/shard_map/ppermute | solution.py:608
  65.9 1.2 %collective-permute-done.9.refs_7_ = bf16[4,10,8,128]{3,2,1,0:T(8,128)(2,1)S(1)} collective-permute-done((bf16[4,10,8,128]{3,2,1,0:T(8,128)(2,1)S(1)}, bf16[4,10,8,128]{3,2,1,0:T(8,128)(2,1)S(1)}, u32[]{:S(2)}, u32[]{:S(2)}) %collective-permute-start.9) | collective-permute-done | bytes 81952 | tf_op jit(solution)/shard_map/ppermute | solution.py:608
  67.1 0.0 all-to-all-done.refs_8_
  67.1 2.8 %grid.1 = bf16[32,15,8,128]{3,2,1,0:T(8,128)(2,1)S(1)} custom-call(bf16[4,10,8,128]{3,2,1,0:T(8,128)(2,1)S(1)} %get-tuple-element.28.refs_0_, bf16[4,10,8,128]{3,2,1,0:T(8,128)(2,1)S(1)} %collective-permute-done.3.refs_1_, bf16[4,10,8,128]{3,2,1,0:T(8,128)(2,1)S(1)} %collective-permute-done.4.refs_2_, ...), custom_call_target="tpu_custom_call" | custom-call | tf_op jit(solution)/shard_map/grid/pallas_call | solution.py:667
  69.9 29.1 %all_to_all.10 = bf16[32,15,8,128]{3,2,1,0:T(8,128)(2,1)S(1)} all-to-all(bf16[32,15,8,128]{3,2,1,0:T(8,128)(2,1)S(1)} %grid.1), channel_id=1, replica_groups=mesh['brick'=8,'sub'=4] {'brick','sub'}, dimensions={0} | all-to-all | bytes 1966080 | tf_op jit(solution)/shard_map/all_to_all | solution.py:676
  99.0 1.8 %receive.1 = (bf16[4,48,2304]{2,1,0:T(8,128)(2,1)}, f32[4,100]{1,0:T(4,128)}, f32[4,100]{1,0:T(4,128)}) custom-call(s32[8,128]{1,0:T(8,128)S(1)} %get-tuple-element.23.off_lanes_ref, bf16[16,2,15,8,128]{4,3,2,1,0:T(8,128)(2,1)S(1)} %bitcast.6), custom_call_target="tpu_custom_call" | custom-call | tf_op jit(solution)/shard_map/receive/pallas_call | solution.py:678
  (1 shorter events, 0.0 us)
Async XLA Ops:
  7.0 60.1 %all-to-all-start = ((bf16[32,18,8,128]{3,2,1,0:T(8,128)(2,1)}), bf16[32,18,8,128]{3,2,1,0:T(8,128)(2,1)S(1)}, u32[]{:S(2)}, u32[]{:S(2)}) async-start(bf16[32,18,8,128]{3,2,1,0:T(8,128)(2,1)} %bitcast.4), calls=%async_computation | async-start | bytes 2359296 | tf_op jit(solution)/shard_map/all_to_all | solution.py:653
  14.4 23.6 %collective-permute-start = (bf16[8,10,8,128]{3,2,1,0:T(8,128)(2,1)S(1)}, bf16[8,10,8,128]{3,2,1,0:T(8,128)(2,1)S(1)}, u32[]{:S(2)}, u32[]{:S(2)}) collective-permute-start(bf16[8,10,8,128]{3,2,1,0:T(8,128)(2,1)S(1)} %bitcast.10), channel_id=1, source_target_pairs={{0,8},{1,9},{2,10},{3,11},{4,12},{5,13},{6,14},{7,15},{8,0},{9,1},... | collective-permute-start | bytes 491528 | tf_op jit(solution)/shard_map/ppermute | solution.py:608
  16.2 38.3 %collective-permute-start.1 = (bf16[8,10,8,128]{3,2,1,0:T(8,128)(2,1)S(1)}, bf16[8,10,8,128]{3,2,1,0:T(8,128)(2,1)S(1)}, u32[]{:S(2)}, u32[]{:S(2)}) collective-permute-start(bf16[8,10,8,128]{3,2,1,0:T(8,128)(2,1)S(1)} %bitcast.9), channel_id=1, source_target_pairs={{0,16},{1,17},{2,18},{3,19},{4,20},{5,21},{6,22},{7,23},{8,24},{9,... | collective-permute-start | bytes 491528 | tf_op jit(solution)/shard_map/ppermute | solution.py:608
  18.6 35.9 %collective-permute-start.2 = (bf16[8,10,8,128]{3,2,1,0:T(8,128)(2,1)S(1)}, bf16[8,10,8,128]{3,2,1,0:T(8,128)(2,1)S(1)}, u32[]{:S(2)}, u32[]{:S(2)}) collective-permute-start(bf16[8,10,8,128]{3,2,1,0:T(8,128)(2,1)S(1)} %bitcast.8), channel_id=1, source_target_pairs={{0,24},{1,25},{2,26},{3,27},{4,28},{5,29},{6,30},{7,31},{8,16},{9,... | collective-permute-start | bytes 491528 | tf_op jit(solution)/shard_map/ppermute | solution.py:608
  54.5 3.6 %collective-permute-start.3 = (bf16[4,10,8,128]{3,2,1,0:T(8,128)(2,1)S(1)}, bf16[4,10,8,128]{3,2,1,0:T(8,128)(2,1)S(1)}, u32[]{:S(2)}, u32[]{:S(2)}) collective-permute-start(bf16[4,10,8,128]{3,2,1,0:T(8,128)(2,1)S(1)} %get-tuple-element.29), channel_id=1, source_target_pairs={{0,1},{1,0},{2,3},{3,2},{4,5},{5,4},{6,7},{7,6},{8,9},{9,8},{10,11... | collective-permute-start | bytes 245768 | tf_op jit(solution)/shard_map/ppermute | solution.py:608
  54.6 6.0 %collective-permute-start.4 = (bf16[4,10,8,128]{3,2,1,0:T(8,128)(2,1)S(1)}, bf16[4,10,8,128]{3,2,1,0:T(8,128)(2,1)S(1)}, u32[]{:S(2)}, u32[]{:S(2)}) collective-permute-start(bf16[4,10,8,128]{3,2,1,0:T(8,128)(2,1)S(1)} %get-tuple-element.30), channel_id=1, source_target_pairs={{0,2},{1,3},{2,0},{3,1},{4,6},{5,7},{6,4},{7,5},{8,10},{9,11},{10,... | collective-permute-start | bytes 245768 | tf_op jit(solution)/shard_map/ppermute | solution.py:608
  56.2 4.8 %collective-permute-start.5 = (bf16[4,10,8,128]{3,2,1,0:T(8,128)(2,1)S(1)}, bf16[4,10,8,128]{3,2,1,0:T(8,128)(2,1)S(1)}, u32[]{:S(2)}, u32[]{:S(2)}) collective-permute-start(bf16[4,10,8,128]{3,2,1,0:T(8,128)(2,1)S(1)} %get-tuple-element.31), channel_id=1, source_target_pairs={{0,3},{1,2},{2,1},{3,0},{4,7},{5,6},{6,5},{7,4},{8,11},{9,10},{10,... | collective-permute-start | bytes 245768 | tf_op jit(solution)/shard_map/ppermute | solution.py:608
  56.5 5.0 %collective-permute-start.6 = (bf16[4,10,8,128]{3,2,1,0:T(8,128)(2,1)S(1)}, bf16[4,10,8,128]{3,2,1,0:T(8,128)(2,1)S(1)}, u32[]{:S(2)}, u32[]{:S(2)}) collective-permute-start(bf16[4,10,8,128]{3,2,1,0:T(8,128)(2,1)S(1)} %get-tuple-element.32), channel_id=1, source_target_pairs={{0,4},{1,5},{2,6},{3,7},{4,0},{5,1},{6,2},{7,3},{8,12},{9,13},{10,... | collective-permute-start | bytes 245768 | tf_op jit(solution)/shard_map/ppermute | solution.py:608
  57.9 4.7 %collective-permute-start.7 = (bf16[4,10,8,128]{3,2,1,0:T(8,128)(2,1)S(1)}, bf16[4,10,8,128]{3,2,1,0:T(8,128)(2,1)S(1)}, u32[]{:S(2)}, u32[]{:S(2)}) collective-permute-start(bf16[4,10,8,128]{3,2,1,0:T(8,128)(2,1)S(1)} %get-tuple-element.33), channel_id=1, source_target_pairs={{0,5},{1,4},{2,7},{3,6},{4,1},{5,0},{6,3},{7,2},{8,13},{9,12},{10,... | collective-permute-start | bytes 245768 | tf_op jit(solution)/shard_map/ppermute | solution.py:608
  58.2 7.8 %collective-permute-start.8 = (bf16[4,10,8,128]{3,2,1,0:T(8,128)(2,1)S(1)}, bf16[4,10,8,128]{3,2,1,0:T(8,128)(2,1)S(1)}, u32[]{:S(2)}, u32[]{:S(2)}) collective-permute-start(bf16[4,10,8,128]{3,2,1,0:T(8,128)(2,1)S(1)} %get-tuple-element.34), channel_id=1, source_target_pairs={{0,6},{1,7},{2,4},{3,5},{4,2},{5,3},{6,0},{7,1},{8,14},{9,15},{10,... | collective-permute-start | bytes 245768 | tf_op jit(solution)/shard_map/ppermute | solution.py:608
  60.6 6.5 %collective-permute-start.9 = (bf16[4,10,8,128]{3,2,1,0:T(8,128)(2,1)S(1)}, bf16[4,10,8,128]{3,2,1,0:T(8,128)(2,1)S(1)}, u32[]{:S(2)}, u32[]{:S(2)}) collective-permute-start(bf16[4,10,8,128]{3,2,1,0:T(8,128)(2,1)S(1)} %get-tuple-element.35), channel_id=1, source_target_pairs={{0,7},{1,6},{2,5},{3,4},{4,3},{5,2},{6,1},{7,0},{8,15},{9,14},{10,... | collective-permute-start | bytes 245768 | tf_op jit(solution)/shard_map/ppermute | solution.py:608

commit v5 on v4

--- a/solution.py
+++ b/solution.py
@@ -167,7 +167,8 @@
     return (gradient, margin_sum, energy_sum)
 
 
-EARLY_PAIRS = 1
+EARLY_PAIRS = 2
+EARLY_TILES = 7
 SUBLANES = 8
 LANES = 128
 
@@ -395,69 +396,79 @@
             out[far] = arrived[far][near]
 
 
-def grid_kernel(dims, *refs):
-    fn_count, edge, classes, shares, width, band_reach, sub_count = dims
-    psi_refs, (h_ref, out_ref, psi_all) = refs[:-3], refs[-3:]
+def grid_rows(psi_all, h_ref, tiles, fn_count, wanted):
     devices = h_ref.shape[0]
+    full = devices * SUBLANES
+    pairs = (tiles + 1) // 2
+    upper = iota((devices, SUBLANES, LANES), 1) < fn_count
+    both = {}
+    for v in range(pairs):
+        if 2 * v not in wanted and 2 * v + 1 not in wanted:
+            continue
+        ours = psi_all[:, tiles + v] if v < EARLY_PAIRS else h_ref[:, tiles + pairs + v - EARLY_PAIRS]
+        ours, theirs = ours.astype(jnp.float32), h_ref[:, tiles + v].astype(jnp.float32)
+        both[2 * v] = jnp.where(upper, ours, pltpu.roll(theirs, fn_count, axis=1))
+        both[2 * v + 1] = jnp.where(upper, pltpu.roll(ours, fn_count, axis=1), theirs)
+    inside = [t for t in wanted if t < tiles]
+    stacked = [
+        jnp.concatenate([psi_all[:, t].reshape(full, LANES) for t in inside], axis=1),
+        jnp.concatenate([both[t].reshape(full, LANES).astype(jnp.bfloat16) for t in inside], axis=1),
+        jnp.concatenate([h_ref[:, t].reshape(full, LANES) for t in inside], axis=1),
+    ]
+    return stacked, both
+
+
+def same_plane(gap, planes, row_depth, fn_count):
+    half_col = jnp.bitwise_and(iota(gap.shape, 1) // fn_count, 1)
+    return [
+        jnp.bitwise_and(gap + row_depth - depth, planes - 1) == 0 for depth in (half_col, 2, half_col)
+    ]
+
+
+def masked(masks, plus, minus, fn_count):
+    half_col = jnp.bitwise_and(iota(plus.shape, 1) // fn_count, 1)
+    coef = (minus, jnp.where(half_col == 0, minus, plus), plus)
+    return jnp.concatenate(
+        [jnp.where(k, c, 0.0).astype(jnp.bfloat16) for k, c in zip(masks, coef)], axis=1
+    )
+
+
+def first_kernel(dims, *refs):
+    fn_count, _, classes, shares, width, band_reach, sub_count, groups = dims
+    near = len(refs) - groups - 7
+    psi_refs, h_ref, outs = refs[:near], refs[near], refs[near + 1 : near + 1 + groups]
+    psi_all, low_ref, plus_ref, minus_ref, gap_ref, grad_ref = refs[near + 1 + groups :]
     tiles = psi_refs[0].shape[1] - EARLY_PAIRS
-    pairs = (tiles + 1) // 2
+    devices = h_ref.shape[0]
     full = devices * SUBLANES
     rank = lax.axis_index("brick") * sub_count + lax.axis_index("sub")
     my_class = rank // shares
     classes_bits = classes.bit_length() - 1
-    near = len(psi_refs)
     for n, ref in enumerate(psi_refs):
-        for far in range(ref.shape[0]):
+        for far in range(groups):
             psi_all[jnp.bitwise_xor(rank, far * near + n)] = ref[far]
 
-    upper = iota((devices, SUBLANES, LANES), 1) < fn_count
-    both = []
-    for v in range(pairs):
-        early = v < EARLY_PAIRS
-        ours = psi_all[:, tiles + v] if early else h_ref[:, tiles + pairs + v - EARLY_PAIRS]
-        ours = ours.astype(jnp.float32)
-        theirs = h_ref[:, tiles + v].astype(jnp.float32)
-        both.append(jnp.where(upper, ours, pltpu.roll(theirs, fn_count, axis=1)))
-        both.append(jnp.where(upper, pltpu.roll(ours, fn_count, axis=1), theirs))
-    halves = both.pop()
-    stacked = [
-        jnp.concatenate([psi_all[:, t].reshape(full, LANES) for t in range(tiles)], axis=1),
-        jnp.concatenate([x.reshape(full, LANES).astype(jnp.bfloat16) for x in both], axis=1),
-        jnp.concatenate([h_ref[:, t].reshape(full, LANES) for t in range(tiles)], axis=1),
-    ]
-
+    stacked, both = grid_rows(psi_all, h_ref, tiles, fn_count, (*range(EARLY_TILES), tiles))
+    halves = both[tiles]
     flat = halves.reshape(full, LANES).astype(jnp.bfloat16)
-    where_hi, where_lo = width, width + 1
     lane_a, lane_b = iota((LANES, full), 0), iota((full, LANES), 1)
-    weigh_a = jnp.where(lane_a == where_hi, 256.0, jnp.where(lane_a == where_lo, 1.0, 0.0))
-    weigh_b = jnp.where(lane_b == where_hi, 256.0, jnp.where(lane_b == where_lo, 1.0, 0.0))
+    weigh_a = jnp.where(lane_a == width, 256.0, jnp.where(lane_a == width + 1, 1.0, 0.0))
+    weigh_b = jnp.where(lane_b == width, 256.0, jnp.where(lane_b == width + 1, 1.0, 0.0))
     off_row = dot(flat, weigh_a.astype(jnp.bfloat16)).astype(jnp.int32)
     off_col = dot_nt(weigh_b.astype(jnp.bfloat16), flat).astype(jnp.int32)
-
-    planes = devices * Q // classes
 
     def first_plane(off):
         inner = jnp.bitwise_and(my_class - off, classes - 1)
         return jnp.right_shift(off + inner - my_class, classes_bits)
 
     gap = first_plane(off_row) - first_plane(off_col)
-    half_row = jnp.bitwise_and(iota((full, full), 0) // fn_count, 1)
-    half_col = jnp.bitwise_and(iota((full, full), 1) // fn_count, 1)
-
-    def mask(row_depth, col_depth):
-        return jnp.bitwise_and(gap + row_depth - col_depth, planes - 1) == 0
-
-    col_depth = (half_col, 2, half_col)
-    low = [mask(half_row, d) for d in col_depth]
-    top = [mask(2, d) for d in col_depth]
+    gap_ref[...] = gap
 
     turned = pltpu.roll(halves, fn_count, axis=1)
-    expand = jnp.where(
-        (iota((LANES, full), 0) == iota((LANES, full), 1) // SUBLANES * fn_count + iota((LANES, full), 1) % fn_count)
-        & (iota((LANES, full), 0) < width),
-        1.0,
-        0.0,
-    ).astype(jnp.bfloat16)
+    upper = iota(halves.shape, 1) < fn_count
+    column = iota((LANES, full), 1)
+    column = column // SUBLANES * fn_count + column % fn_count
+    expand = jnp.where((lane_a == column) & (lane_a < width), 1.0, 0.0).astype(jnp.bfloat16)
 
     def dense(rows):
         wide = dot(rows.reshape(full, LANES).astype(jnp.bfloat16), expand)
@@ -470,26 +481,42 @@
 
     plus = dense(jnp.where(upper, halves, turned))
     minus = -dense(jnp.where(upper, turned, halves))
-    coef = (minus, jnp.where(half_col == 0, minus, plus), plus)
-    mixed = jnp.concatenate(
-        [
-            jnp.concatenate([jnp.where(k, c, 0.0).astype(jnp.bfloat16) for k, c in zip(ks, coef)], axis=1)
-            for ks in (low, top)
-        ],
-        axis=0,
-    )
-
-    grad = dot(mixed, jnp.concatenate(stacked, axis=0))
-    for t in range(tiles):
-        out_ref[:, t] = (
-            grad[:full, t * LANES : (t + 1) * LANES].reshape(devices, SUBLANES, LANES).astype(jnp.bfloat16)
-        )
-    second = grad[full:].reshape(devices, SUBLANES, tiles * LANES)
-    for v in range((tiles + 1) // 2):
-        even = second[:, :, 2 * v * LANES : (2 * v + 1) * LANES]
-        if 2 * v + 1 < tiles:
-            even = jnp.where(upper, even, second[:, :, (2 * v + 1) * LANES : (2 * v + 2) * LANES])
-        out_ref[:, tiles + v] = even.astype(jnp.bfloat16)
+    plus_ref[...] = plus
+    minus_ref[...] = minus
+    half_row = jnp.bitwise_and(iota((full, full), 0) // fn_count, 1)
+    low = masked(same_plane(gap, devices * Q // classes, half_row, fn_count), plus, minus, fn_count)
+    low_ref[...] = low
+    grad = dot(low, jnp.concatenate(stacked, axis=0))
+    for t in range(EARLY_TILES):
+        piece = grad[:, t * LANES : (t + 1) * LANES].reshape(devices, SUBLANES, LANES)
+        grad_ref[:, t] = piece.astype(jnp.bfloat16)
+    for far in range(groups):
+        for n in range(near):
+            outs[far][n] = grad_ref[jnp.bitwise_xor(rank, far * near + n)]
+
+
+def second_kernel(dims, psi_all, h_ref, low_ref, plus_ref, minus_ref, gap_ref, out_ref):
+    fn_count, edge, classes = dims
+    tiles = psi_all.shape[1] - EARLY_PAIRS
+    devices = h_ref.shape[0]
+    full = devices * SUBLANES
+    planes = devices * Q // classes
+    pairs = (tiles + 1) // 2
+    stacked, _ = grid_rows(psi_all, h_ref, tiles, fn_count, range(tiles))
+    gap = gap_ref[...]
+    half_row = jnp.bitwise_and(iota((full, full), 0) // fn_count, 1)
+    low = same_plane(gap, planes, half_row, fn_count)
+    top = same_plane(gap, planes, 2, fn_count)
+    rows = jnp.concatenate(stacked, axis=0)
+    rest = dot(low_ref[...], rows[:, EARLY_TILES * LANES :])
+    for t in range(tiles - EARLY_TILES):
+        piece = rest[:, t * LANES : (t + 1) * LANES].reshape(devices, SUBLANES, LANES)
+        out_ref[:, t] = piece.astype(jnp.bfloat16)
+    upper = iota((devices, SUBLANES, LANES), 1) < fn_count
+    second = dot(masked(top, plus_ref[...], minus_ref[...], fn_count), rows)
+    second = second.reshape(devices, SUBLANES, tiles * LANES)
+    for v, piece in enumerate(pair_units(second, tiles, upper, 0.0)):
+        out_ref[:, tiles - EARLY_TILES + v] = piece
 
     sums = []
     for part in range(3):
@@ -504,17 +531,23 @@
     bands = sums[1] + jnp.where(lanes_half == 0, first, third)
     bands = jnp.where(upper, bands[:, :, :LANES], bands[:, :, LANES:])
     bands = bands * (1.0 / float(edge**3))
-    out_ref[:, tiles + (tiles + 1) // 2] = bands.astype(jnp.bfloat16)
-
-
-def receive_kernel(dims, off_lanes_ref, in_ref, grad_hbm, margin_ref, energy_ref, grad_ref, sems):
-    fn_count, edge, plane_len, classes, shares, band_reach, sub_count = dims
+    out_ref[:, tiles - EARLY_TILES + pairs] = bands.astype(jnp.bfloat16)
+
+
+def receive_kernel(dims, off_lanes_ref, in_ref, *refs):
+    fn_count, edge, plane_len, classes, shares, band_reach, sub_count, near = dims
+    early_refs, (grad_hbm, margin_ref, energy_ref, grad_ref, early_ref, sems) = refs[:near], refs[near:]
     tiles = plane_len // LANES // shares
     rows = fn_count * edge
     devices = classes * shares
     width = margin_ref.shape[1]
     rank = lax.axis_index("brick") * sub_count + lax.axis_index("sub")
     inner = classes * SUBLANES
+    for n, ref in enumerate(early_refs):
+        for far in range(ref.shape[0]):
+            source = jnp.bitwise_xor(rank, far * near + n)
+            early_ref[source // shares, jnp.bitwise_and(source, shares - 1)] = ref[far]
+    pair_at = tiles - EARLY_TILES
 
     shape = (fn_count, edge, inner)
     member, plane = iota(shape, 0), iota(shape, 1)
@@ -536,8 +569,10 @@
             columns = [
                 jnp.concatenate(
                     [
-                        in_ref[:, share, t].reshape(inner, LANES),
-                        in_ref[:, share, tiles + t // 2].reshape(inner, LANES),
+                        (
+                            early_ref[:, share, t] if t < EARLY_TILES else in_ref[:, share, t - EARLY_TILES]
+                        ).reshape(inner, LANES),
+                        in_ref[:, share, pair_at + t // 2].reshape(inner, LANES),
                     ],
                     axis=0,
                 )
@@ -556,7 +591,7 @@
         copies[-1].start()
 
     total = jnp.sum(
-        in_ref[:, :, tiles + (tiles + 1) // 2].reshape(devices, SUBLANES, LANES).astype(jnp.float32), axis=0
+        in_ref[:, :, pair_at + (tiles + 1) // 2].reshape(devices, SUBLANES, LANES).astype(jnp.float32), axis=0
     )
     terms = []
     for _ in range(3):
@@ -663,31 +698,72 @@
     )(*arrived)
     gathered = [x if n == 0 else exchange(x, n) for n, x in enumerate(turned)]
 
-    back_units = tiles + (tiles + 1) // 2 + 1
+    full = devices * SUBLANES
+    results = pl.pallas_call(
+        functools.partial(
+            first_kernel, (fn_count, edge, classes, shares, width, band_reach, sub_count, groups)
+        ),
+        out_shape=[block(near, EARLY_TILES)] * groups
+        + [
+            block(devices, early),
+            jax.ShapeDtypeStruct((full, 3 * full), jnp.bfloat16),
+            jax.ShapeDtypeStruct((full, full), jnp.float32),
+            jax.ShapeDtypeStruct((full, full), jnp.float32),
+            jax.ShapeDtypeStruct((full, full), jnp.int32),
+        ],
+        in_specs=[vmem] * (near + 1),
+        out_specs=[vmem] * (groups + 5),
+        scratch_shapes=[pltpu.VMEM((devices, EARLY_TILES, SUBLANES, LANES), jnp.bfloat16)],
+        compiler_params=params,
+        cost_estimate=cost(1024 * size, 4 * size),
+        name="first",
+    )(*gathered, held)
+    leaving, tables = results[:groups], results[groups:]
+    returned = [leaving[0]] + [None] * (groups - 1)
+    for far in (3, 2, 1):
+        returned[far] = exchange(leaving[far], far * near)
+
+    back_units = tiles - EARLY_TILES + (tiles + 1) // 2 + 1
     made = pl.pallas_call(
-        functools.partial(grid_kernel, (fn_count, edge, classes, shares, width, band_reach, sub_count)),
-        out_shape=jax.ShapeDtypeStruct((devices, back_units, SUBLANES, LANES), jnp.bfloat16),
-        in_specs=[vmem] * (near + 1),
+        functools.partial(second_kernel, (fn_count, edge, classes)),
+        out_shape=block(devices, back_units),
+        in_specs=[vmem] * 6,
         out_specs=vmem,
-        scratch_shapes=[pltpu.VMEM((devices, early, SUBLANES, LANES), jnp.bfloat16)],
         compiler_params=params,
-        name="grid",
-    )(*gathered, held)
+        cost_estimate=cost(2048 * size, 4 * size),
+        name="second",
+    )(tables[0], held, *tables[1:])
     back = lax.all_to_all(made, axes, 0, 0, tiled=True)
     back = back.reshape(classes, shares, back_units, SUBLANES, LANES)
+    spread = pl.pallas_call(
+        turn_kernel,
+        out_shape=[block(groups, EARLY_TILES)] * near,
+        in_specs=[vmem] * groups,
+        out_specs=[vmem] * near,
+        compiler_params=params,
+        cost_estimate=cost(0, 4 * size),
+        name="spread",
+    )(*returned)
+    homed = [x if n == 0 else exchange(x, n) for n, x in enumerate(spread)]
     return pl.pallas_call(
-        functools.partial(receive_kernel, (fn_count, edge, plane_len, classes, shares, band_reach, sub_count)),
+        functools.partial(
+            receive_kernel, (fn_count, edge, plane_len, classes, shares, band_reach, sub_count, near)
+        ),
         out_shape=(
             jax.ShapeDtypeStruct(psi.shape, jnp.bfloat16),
             jax.ShapeDtypeStruct((fn_count, width), jnp.float32),
             jax.ShapeDtypeStruct((fn_count, width), jnp.float32),
         ),
-        in_specs=[vmem, vmem],
+        in_specs=[vmem] * (2 + near),
         out_specs=(hbm, vmem, vmem),
-        scratch_shapes=[pltpu.VMEM(psi.shape, jnp.bfloat16), pltpu.SemaphoreType.DMA((shares,))],
+        scratch_shapes=[
+            pltpu.VMEM(psi.shape, jnp.bfloat16),
+            pltpu.VMEM((classes, shares, EARLY_TILES, SUBLANES, LANES), jnp.bfloat16),
+            pltpu.SemaphoreType.DMA((shares,)),
+        ],
         compiler_params=params,
         name="receive",
-    )(off_lanes, back)
+    )(off_lanes, back, *homed)
 
 
 def any_shards(psi, potential, offsets, kernel, multipliers, pattern):

time: 101 us -> 112 us (1.11)
  blocking collectives: 29.1 us -> 0 us
  waiting for transfers between devices: 41.7 us -> 64.7 us
  starting transfers between devices: 18.3 us -> 34.2 us
  Pallas kernels: 11.1 us -> 12.3 us
    all_to_all x1 -> x0, blocking collectives: 29.1 us -> none  [transposed_shards(): back = lax.all_to_all(made, axes, 0, 0, tiled=True)]
    ppermute x10 -> x20, waiting for transfers between devices: 41.7 us -> 64.7 us  [exchange(): return lax.ppermute(array, axes, [(i, i ^ bits) for i in range(devices)])]
    ppermute x10 -> x20, starting transfers between devices: 10.9 us -> 21.9 us  [exchange(): return lax.ppermute(array, axes, [(i, i ^ bits) for i in range(devices)])]
    all_to_all x0 -> x1, starting transfers between devices: none -> 4.99 us  [transposed_shards(): back = lax.all_to_all(made, axes, 0, 0, tiled=True)]
    pallas_call x1 -> x3, Pallas kernels: 2.81 us -> 3.88 us  [the longest x1 2.8 us: transposed_shards(): pl.pallas_call(functools.partial(second_kernel, (fn_count, edge, classes)...]
  transfers between devices with their start and end apart: 11 -> 22, of which waited for: 6 -> 11; matrix products, arithmetic and copies ran while one was open for 0% -> 0% of each run, Pallas kernels for 0% -> 0%
where the time goes in v5:
time: 112 us
  waiting for transfers between devices  64.7 us (58%)
  starting transfers between devices  34.2 us (31%)
  Pallas kernels  12.3 us (11%)
    ppermute x20, waiting for transfers between devices, exchange(): return lax.ppermute(array, axes, [(i, i ^ bits) for i in range(devices)])  64.7 us
    ppermute x20, starting transfers between devices, exchange(): return lax.ppermute(array, axes, [(i, i ^ bits) for i in range(devices)])  21.9 us
    all_to_all x1, starting transfers between devices, transposed_shards(): lax.all_to_all(applied.reshape(devices, units, SUBLANES, LANES), axes, 0,...  7.33 us
    all_to_all x1, starting transfers between devices, transposed_shards(): back = lax.all_to_all(made, axes, 0, 0, tiled=True)  4.99 us
    pallas_call x1, Pallas kernels, transposed_shards(): pl.pallas_call(functools.partial(apply_kernel, (fn_count, edge, plane_len...  4.73 us
    pallas_call x1, Pallas kernels, transposed_shards(): pl.pallas_call(functools.partial(second_kernel, (fn_count, edge, classes)...  2.8 us
  transfers between devices with their start and end apart: 22, of which 11 were waited for; matrix products, arithmetic and copies ran while one was open for 0% of the time, Pallas kernels for 0%

profile of v5, /device:TPU:0, one launch (start us, length us, event | category | flops | bytes accessed | tf_op | source)
XLA Modules:
  0.0 112.0 jit_solution(5265197197902339146)
XLA Ops:
  0.6 1.6 %pack.1 = (bf16[4,2,11,8,128]{4,3,2,1,0:T(8,128)(2,1)S(1)}, bf16[4,2,11,8,128]{4,3,2,1,0:T(8,128)(2,1)S(1)}, bf16[4,2,11,8,128]{4,3,2,1,0:T(8,128)(2,1)S(1)}, bf...) custom-call(s32[4]{0:T(128)} %offs_hbm.1, ...), custom_call_target="tpu_custom_call" | custom-call | flops 226492416 | bytes 1769472 | tf_op jit(solution)/shard_map/pack/pallas_call | solution.py:649
  2.3 4.7 %apply.1 = bf16[16,2,17,8,128]{4,3,2,1,0:T(8,128)(2,1)} custom-call(s32[8,128]{1,0:T(8,128)S(1)} %get-tuple-element.53.off_rows_ref, bf16[4,48,2304]{2,1,0:T(8,128)(2,1)S(1)} %get-tuple-element.54.psi_ref, bf16[4,48,2304]{2,1,0:T(8,128)(2,1)S(1)} %get-tuple-element.55.pot_ref, bf16[192,192]{1,0:T(8,128)(2,1)S(1)} %get-tuple-element.56.kin_ref, ...), custom_call_target="tpu_custom_call" | custom-call | flops 2038431744 | bytes 3538944 | tf_op jit(solution)/shard_map/apply/pallas_call | solution.py:674
  7.0 7.3 %all-to-all-start = ((bf16[32,17,8,128]{3,2,1,0:T(8,128)(2,1)}), bf16[32,17,8,128]{3,2,1,0:T(8,128)(2,1)S(1)}, u32[]{:S(2)}, u32[]{:S(2)}) async-start(bf16[32,17,8,128]{3,2,1,0:T(8,128)(2,1)} %bitcast.4), calls=%async_computation | async-start | bytes 2228224 | tf_op jit(solution)/shard_map/all_to_all | solution.py:688
  14.4 1.8 %collective-permute-start = (bf16[8,11,8,128]{3,2,1,0:T(8,128)(2,1)S(1)}, bf16[8,11,8,128]{3,2,1,0:T(8,128)(2,1)S(1)}, u32[]{:S(2)}, u32[]{:S(2)}) collective-permute-start(bf16[8,11,8,128]{3,2,1,0:T(8,128)(2,1)S(1)} %bitcast.10), channel_id=1, source_target_pairs={{0,8},{1,9},{2,10},{3,11},{4,12},{5,13},{6,14},{7,15},{8,0},{9,1},... | collective-permute-start | bytes 540680 | tf_op jit(solution)/shard_map/ppermute | solution.py:643
  16.2 2.4 %collective-permute-start.1 = (bf16[8,11,8,128]{3,2,1,0:T(8,128)(2,1)S(1)}, bf16[8,11,8,128]{3,2,1,0:T(8,128)(2,1)S(1)}, u32[]{:S(2)}, u32[]{:S(2)}) collective-permute-start(bf16[8,11,8,128]{3,2,1,0:T(8,128)(2,1)S(1)} %bitcast.9), channel_id=1, source_target_pairs={{0,16},{1,17},{2,18},{3,19},{4,20},{5,21},{6,22},{7,23},{8,24},{9,... | collective-permute-start | bytes 540680 | tf_op jit(solution)/shard_map/ppermute | solution.py:643
  18.6 0.2 collective-permute-start.2
  18.8 18.4 %collective-permute-done.refs_1_ = bf16[8,11,8,128]{3,2,1,0:T(8,128)(2,1)S(1)} collective-permute-done((bf16[8,11,8,128]{3,2,1,0:T(8,128)(2,1)S(1)}, bf16[8,11,8,128]{3,2,1,0:T(8,128)(2,1)S(1)}, u32[]{:S(2)}, u32[]{:S(2)}) %collective-permute-start) | collective-permute-done | bytes 180256 | tf_op jit(solution)/shard_map/ppermute | solution.py:643
  37.2 16.9 %collective-permute-done.1.refs_2_ = bf16[8,11,8,128]{3,2,1,0:T(8,128)(2,1)S(1)} collective-permute-done((bf16[8,11,8,128]{3,2,1,0:T(8,128)(2,1)S(1)}, bf16[8,11,8,128]{3,2,1,0:T(8,128)(2,1)S(1)}, u32[]{:S(2)}, u32[]{:S(2)}) %collective-permute-start.1) | collective-permute-done | bytes 180256 | tf_op jit(solution)/shard_map/ppermute | solution.py:643
  54.1 0.0 collective-permute-done.2.refs_3_
  54.1 0.1 turn.1
  54.2 0.1 collective-permute-start.3
  54.3 1.6 %collective-permute-start.4 = (bf16[4,11,8,128]{3,2,1,0:T(8,128)(2,1)S(1)}, bf16[4,11,8,128]{3,2,1,0:T(8,128)(2,1)S(1)}, u32[]{:S(2)}, u32[]{:S(2)}) collective-permute-start(bf16[4,11,8,128]{3,2,1,0:T(8,128)(2,1)S(1)} %get-tuple-element.47), channel_id=1, source_target_pairs={{0,2},{1,3},{2,0},{3,1},{4,6},{5,7},{6,4},{7,5},{8,10},{9,11},{10,... | collective-permute-start | bytes 270344 | tf_op jit(solution)/shard_map/ppermute | solution.py:643
  55.8 0.3 collective-permute-start.5
  56.1 1.5 %collective-permute-start.6 = (bf16[4,11,8,128]{3,2,1,0:T(8,128)(2,1)S(1)}, bf16[4,11,8,128]{3,2,1,0:T(8,128)(2,1)S(1)}, u32[]{:S(2)}, u32[]{:S(2)}) collective-permute-start(bf16[4,11,8,128]{3,2,1,0:T(8,128)(2,1)S(1)} %get-tuple-element.49), channel_id=1, source_target_pairs={{0,4},{1,5},{2,6},{3,7},{4,0},{5,1},{6,2},{7,3},{8,12},{9,13},{10,... | collective-permute-start | bytes 270344 | tf_op jit(solution)/shard_map/ppermute | solution.py:643
  57.6 0.2 collective-permute-start.7
  57.8 0.0 collective-permute-done.3.refs_1_
  57.8 2.4 %collective-permute-start.8 = (bf16[4,11,8,128]{3,2,1,0:T(8,128)(2,1)S(1)}, bf16[4,11,8,128]{3,2,1,0:T(8,128)(2,1)S(1)}, u32[]{:S(2)}, u32[]{:S(2)}) collective-permute-start(bf16[4,11,8,128]{3,2,1,0:T(8,128)(2,1)S(1)} %get-tuple-element.51), channel_id=1, source_target_pairs={{0,6},{1,7},{2,4},{3,5},{4,2},{5,3},{6,0},{7,1},{8,14},{9,15},{10,... | collective-permute-start | bytes 270344 | tf_op jit(solution)/shard_map/ppermute | solution.py:643
  60.2 0.0 collective-permute-done.4.refs_2_
  60.2 0.6 collective-permute-start.9
  60.9 0.0 collective-permute-done.5.refs_3_
  60.9 0.6 collective-permute-done.6.refs_4_
  61.4 1.1 collective-permute-done.7.refs_5_
  62.5 3.7 %collective-permute-done.8.refs_6_ = bf16[4,11,8,128]{3,2,1,0:T(8,128)(2,1)S(1)} collective-permute-done((bf16[4,11,8,128]{3,2,1,0:T(8,128)(2,1)S(1)}, bf16[4,11,8,128]{3,2,1,0:T(8,128)(2,1)S(1)}, u32[]{:S(2)}, u32[]{:S(2)}) %collective-permute-start.8) | collective-permute-done | bytes 90144 | tf_op jit(solution)/shard_map/ppermute | solution.py:643
  66.3 1.0 collective-permute-done.9.refs_7_
  67.3 0.0 all-to-all-done.refs_8_.h_ref
  67.3 1.0 first.1
  68.3 2.8 %second.1 = bf16[32,8,8,128]{3,2,1,0:T(8,128)(2,1)} custom-call(bf16[32,11,8,128]{3,2,1,0:T(8,128)(2,1)S(1)} %get-tuple-element.60.psi_all, bf16[32,17,8,128]{3,2,1,0:T(8,128)(2,1)S(1)} %all-to-all-done.refs_8_.h_ref, bf16[256,768]{1,0:T(8,128)(2,1)S(1)} %get-tuple-element.61.low_ref, f32[256,256]{1,0:T(8,128)S(1)} %get-tuple-element.62.plus_ref, ...), custom_call_target="tpu_custom_call" | custom-call | flops 905969664 | bytes 1769472 | tf_op jit(solution)/shard_map/second/pallas_call | solution.py:727
  71.1 5.0 %all-to-all-start.1 = ((bf16[32,8,8,128]{3,2,1,0:T(8,128)(2,1)}), bf16[32,8,8,128]{3,2,1,0:T(8,128)(2,1)S(1)}, u32[]{:S(2)}, u32[]{:S(2)}) async-start(bf16[32,8,8,128]{3,2,1,0:T(8,128)(2,1)} %second.1), calls=%async_computation.1 | async-start | bytes 1048576 | tf_op jit(solution)/shard_map/all_to_all | solution.py:736
  76.1 1.8 %collective-permute-start.10 = (bf16[8,7,8,128]{3,2,1,0:T(8,128)(2,1)S(1)}, bf16[8,7,8,128]{3,2,1,0:T(8,128)(2,1)S(1)}, u32[]{:S(2)}, u32[]{:S(2)}) collective-permute-start(bf16[8,7,8,128]{3,2,1,0:T(8,128)(2,1)S(1)} %get-tuple-element.66), channel_id=1, source_target_pairs={{0,8},{1,9},{2,10},{3,11},{4,12},{5,13},{6,14},{7,15},{8,0},{9,1},... | collective-permute-start | bytes 344072 | tf_op jit(solution)/shard_map/ppermute | solution.py:643
  78.0 2.4 %collective-permute-start.11 = (bf16[8,7,8,128]{3,2,1,0:T(8,128)(2,1)S(1)}, bf16[8,7,8,128]{3,2,1,0:T(8,128)(2,1)S(1)}, u32[]{:S(2)}, u32[]{:S(2)}) collective-permute-start(bf16[8,7,8,128]{3,2,1,0:T(8,128)(2,1)S(1)} %get-tuple-element.67), channel_id=1, source_target_pairs={{0,16},{1,17},{2,18},{3,19},{4,20},{5,21},{6,22},{7,23},{8,24},{9,... | collective-permute-start | bytes 344072 | tf_op jit(solution)/shard_map/ppermute | solution.py:643
  80.4 0.2 collective-permute-start.12
  80.6 7.7 %collective-permute-done.10.refs_1_ = bf16[8,7,8,128]{3,2,1,0:T(8,128)(2,1)S(1)} collective-permute-done((bf16[8,7,8,128]{3,2,1,0:T(8,128)(2,1)S(1)}, bf16[8,7,8,128]{3,2,1,0:T(8,128)(2,1)S(1)}, u32[]{:S(2)}, u32[]{:S(2)}) %collective-permute-start.10) | collective-permute-done | bytes 114720 | tf_op jit(solution)/shard_map/ppermute | solution.py:643
  88.3 10.7 %collective-permute-done.11.refs_2_ = bf16[8,7,8,128]{3,2,1,0:T(8,128)(2,1)S(1)} collective-permute-done((bf16[8,7,8,128]{3,2,1,0:T(8,128)(2,1)S(1)}, bf16[8,7,8,128]{3,2,1,0:T(8,128)(2,1)S(1)}, u32[]{:S(2)}, u32[]{:S(2)}) %collective-permute-start.11) | collective-permute-done | bytes 114720 | tf_op jit(solution)/shard_map/ppermute | solution.py:643
  99.1 0.0 collective-permute-done.12.refs_3_
  99.1 0.1 collective-permute-start.13
  99.2 1.5 %collective-permute-start.14 = (bf16[4,7,8,128]{3,2,1,0:T(8,128)(2,1)S(1)}, bf16[4,7,8,128]{3,2,1,0:T(8,128)(2,1)S(1)}, u32[]{:S(2)}, u32[]{:S(2)}) collective-permute-start(bf16[4,7,8,128]{3,2,1,0:T(8,128)(2,1)S(1)} %get-tuple-element.71), channel_id=1, source_target_pairs={{0,2},{1,3},{2,0},{3,1},{4,6},{5,7},{6,4},{7,5},{8,10},{9,11},{10,... | collective-permute-start | bytes 172040 | tf_op jit(solution)/shard_map/ppermute | solution.py:643
  100.7 0.3 collective-permute-start.15
  101.0 1.5 %collective-permute-start.16 = (bf16[4,7,8,128]{3,2,1,0:T(8,128)(2,1)S(1)}, bf16[4,7,8,128]{3,2,1,0:T(8,128)(2,1)S(1)}, u32[]{:S(2)}, u32[]{:S(2)}) collective-permute-start(bf16[4,7,8,128]{3,2,1,0:T(8,128)(2,1)S(1)} %get-tuple-element.73), channel_id=1, source_target_pairs={{0,4},{1,5},{2,6},{3,7},{4,0},{5,1},{6,2},{7,3},{8,12},{9,13},{10,... | collective-permute-start | bytes 172040 | tf_op jit(solution)/shard_map/ppermute | solution.py:643
  102.5 0.2 collective-permute-start.17
  102.7 0.0 collective-permute-done.13.refs_1_
  102.7 2.4 %collective-permute-start.18 = (bf16[4,7,8,128]{3,2,1,0:T(8,128)(2,1)S(1)}, bf16[4,7,8,128]{3,2,1,0:T(8,128)(2,1)S(1)}, u32[]{:S(2)}, u32[]{:S(2)}) collective-permute-start(bf16[4,7,8,128]{3,2,1,0:T(8,128)(2,1)S(1)} %get-tuple-element.75), channel_id=1, source_target_pairs={{0,6},{1,7},{2,4},{3,5},{4,2},{5,3},{6,0},{7,1},{8,14},{9,15},{10,... | collective-permute-start | bytes 172040 | tf_op jit(solution)/shard_map/ppermute | solution.py:643
  105.1 0.0 collective-permute-done.14.refs_2_
  105.1 0.3 collective-permute-start.19
  105.4 0.0 collective-permute-done.15.refs_3_
  105.4 1.0 collective-permute-done.17.refs_5_
  106.4 2.4 %collective-permute-done.18.refs_6_ = bf16[4,7,8,128]{3,2,1,0:T(8,128)(2,1)S(1)} collective-permute-done((bf16[4,7,8,128]{3,2,1,0:T(8,128)(2,1)S(1)}, bf16[4,7,8,128]{3,2,1,0:T(8,128)(2,1)S(1)}, u32[]{:S(2)}, u32[]{:S(2)}) %collective-permute-start.18) | collective-permute-done | bytes 57376 | tf_op jit(solution)/shard_map/ppermute | solution.py:643
  108.9 1.1 collective-permute-done.19.refs_7_
  109.9 2.0 %receive.1 = (bf16[4,48,2304]{2,1,0:T(8,128)(2,1)}, f32[4,100]{1,0:T(4,128)}, f32[4,100]{1,0:T(4,128)}) custom-call(s32[8,128]{1,0:T(8,128)S(1)} %get-tuple-element.40.off_lanes_ref, bf16[16,2,8,8,128]{4,3,2,1,0:T(8,128)(2,1)S(1)} %bitcast.6, bf16[4,7,8,128]{3,2,1,0:T(8,128)(2,1)S(1)} %get-tuple-element.69.refs_0_, ...), custom_call_target="tpu_custom_call" | custom-call | tf_op jit(solution)/shard_map/receive/pallas_call | solution.py:748
  (3 shorter events, 0.0 us)
Async XLA Ops:
  7.0 60.3 %all-to-all-start = ((bf16[32,17,8,128]{3,2,1,0:T(8,128)(2,1)}), bf16[32,17,8,128]{3,2,1,0:T(8,128)(2,1)S(1)}, u32[]{:S(2)}, u32[]{:S(2)}) async-start(bf16[32,17,8,128]{3,2,1,0:T(8,128)(2,1)} %bitcast.4), calls=%async_computation | async-start | bytes 2228224 | tf_op jit(solution)/shard_map/all_to_all | solution.py:688
  14.4 22.9 %collective-permute-start = (bf16[8,11,8,128]{3,2,1,0:T(8,128)(2,1)S(1)}, bf16[8,11,8,128]{3,2,1,0:T(8,128)(2,1)S(1)}, u32[]{:S(2)}, u32[]{:S(2)}) collective-permute-start(bf16[8,11,8,128]{3,2,1,0:T(8,128)(2,1)S(1)} %bitcast.10), channel_id=1, source_target_pairs={{0,8},{1,9},{2,10},{3,11},{4,12},{5,13},{6,14},{7,15},{8,0},{9,1},... | collective-permute-start | bytes 540680 | tf_op jit(solution)/shard_map/ppermute | solution.py:643
  16.2 37.9 %collective-permute-start.1 = (bf16[8,11,8,128]{3,2,1,0:T(8,128)(2,1)S(1)}, bf16[8,11,8,128]{3,2,1,0:T(8,128)(2,1)S(1)}, u32[]{:S(2)}, u32[]{:S(2)}) collective-permute-start(bf16[8,11,8,128]{3,2,1,0:T(8,128)(2,1)S(1)} %bitcast.9), channel_id=1, source_target_pairs={{0,16},{1,17},{2,18},{3,19},{4,20},{5,21},{6,22},{7,23},{8,24},{9,... | collective-permute-start | bytes 540680 | tf_op jit(solution)/shard_map/ppermute | solution.py:643
  18.6 35.5 %collective-permute-start.2 = (bf16[8,11,8,128]{3,2,1,0:T(8,128)(2,1)S(1)}, bf16[8,11,8,128]{3,2,1,0:T(8,128)(2,1)S(1)}, u32[]{:S(2)}, u32[]{:S(2)}) collective-permute-start(bf16[8,11,8,128]{3,2,1,0:T(8,128)(2,1)S(1)} %bitcast.8), channel_id=1, source_target_pairs={{0,24},{1,25},{2,26},{3,27},{4,28},{5,29},{6,30},{7,31},{8,16},{9,... | collective-permute-start | bytes 540680 | tf_op jit(solution)/shard_map/ppermute | solution.py:643
  54.2 3.6 %collective-permute-start.3 = (bf16[4,11,8,128]{3,2,1,0:T(8,128)(2,1)S(1)}, bf16[4,11,8,128]{3,2,1,0:T(8,128)(2,1)S(1)}, u32[]{:S(2)}, u32[]{:S(2)}) collective-permute-start(bf16[4,11,8,128]{3,2,1,0:T(8,128)(2,1)S(1)} %get-tuple-element.46), channel_id=1, source_target_pairs={{0,1},{1,0},{2,3},{3,2},{4,5},{5,4},{6,7},{7,6},{8,9},{9,8},{10,11... | collective-permute-start | bytes 270344 | tf_op jit(solution)/shard_map/ppermute | solution.py:643
  54.3 6.0 %collective-permute-start.4 = (bf16[4,11,8,128]{3,2,1,0:T(8,128)(2,1)S(1)}, bf16[4,11,8,128]{3,2,1,0:T(8,128)(2,1)S(1)}, u32[]{:S(2)}, u32[]{:S(2)}) collective-permute-start(bf16[4,11,8,128]{3,2,1,0:T(8,128)(2,1)S(1)} %get-tuple-element.47), channel_id=1, source_target_pairs={{0,2},{1,3},{2,0},{3,1},{4,6},{5,7},{6,4},{7,5},{8,10},{9,11},{10,... | collective-permute-start | bytes 270344 | tf_op jit(solution)/shard_map/ppermute | solution.py:643
  55.8 5.0 %collective-permute-start.5 = (bf16[4,11,8,128]{3,2,1,0:T(8,128)(2,1)S(1)}, bf16[4,11,8,128]{3,2,1,0:T(8,128)(2,1)S(1)}, u32[]{:S(2)}, u32[]{:S(2)}) collective-permute-start(bf16[4,11,8,128]{3,2,1,0:T(8,128)(2,1)S(1)} %get-tuple-element.48), channel_id=1, source_target_pairs={{0,3},{1,2},{2,1},{3,0},{4,7},{5,6},{6,5},{7,4},{8,11},{9,10},{10,... | collective-permute-start | bytes 270344 | tf_op jit(solution)/shard_map/ppermute | solution.py:643
  56.1 5.3 %collective-permute-start.6 = (bf16[4,11,8,128]{3,2,1,0:T(8,128)(2,1)S(1)}, bf16[4,11,8,128]{3,2,1,0:T(8,128)(2,1)S(1)}, u32[]{:S(2)}, u32[]{:S(2)}) collective-permute-start(bf16[4,11,8,128]{3,2,1,0:T(8,128)(2,1)S(1)} %get-tuple-element.49), channel_id=1, source_target_pairs={{0,4},{1,5},{2,6},{3,7},{4,0},{5,1},{6,2},{7,3},{8,12},{9,13},{10,... | collective-permute-start | bytes 270344 | tf_op jit(solution)/shard_map/ppermute | solution.py:643
  57.6 4.9 %collective-permute-start.7 = (bf16[4,11,8,128]{3,2,1,0:T(8,128)(2,1)S(1)}, bf16[4,11,8,128]{3,2,1,0:T(8,128)(2,1)S(1)}, u32[]{:S(2)}, u32[]{:S(2)}) collective-permute-start(bf16[4,11,8,128]{3,2,1,0:T(8,128)(2,1)S(1)} %get-tuple-element.50), channel_id=1, source_target_pairs={{0,5},{1,4},{2,7},{3,6},{4,1},{5,0},{6,3},{7,2},{8,13},{9,12},{10,... | collective-permute-start | bytes 270344 | tf_op jit(solution)/shard_map/ppermute | solution.py:643
  57.8 8.4 %collective-permute-start.8 = (bf16[4,11,8,128]{3,2,1,0:T(8,128)(2,1)S(1)}, bf16[4,11,8,128]{3,2,1,0:T(8,128)(2,1)S(1)}, u32[]{:S(2)}, u32[]{:S(2)}) collective-permute-start(bf16[4,11,8,128]{3,2,1,0:T(8,128)(2,1)S(1)} %get-tuple-element.51), channel_id=1, source_target_pairs={{0,6},{1,7},{2,4},{3,5},{4,2},{5,3},{6,0},{7,1},{8,14},{9,15},{10,... | collective-permute-start | bytes 270344 | tf_op jit(solution)/shard_map/ppermute | solution.py:643
  60.2 7.1 %collective-permute-start.9 = (bf16[4,11,8,128]{3,2,1,0:T(8,128)(2,1)S(1)}, bf16[4,11,8,128]{3,2,1,0:T(8,128)(2,1)S(1)}, u32[]{:S(2)}, u32[]{:S(2)}) collective-permute-start(bf16[4,11,8,128]{3,2,1,0:T(8,128)(2,1)S(1)} %get-tuple-element.52), channel_id=1, source_target_pairs={{0,7},{1,6},{2,5},{3,4},{4,3},{5,2},{6,1},{7,0},{8,15},{9,14},{10,... | collective-permute-start | bytes 270344 | tf_op jit(solution)/shard_map/ppermute | solution.py:643
  71.1 38.8 %all-to-all-start.1 = ((bf16[32,8,8,128]{3,2,1,0:T(8,128)(2,1)}), bf16[32,8,8,128]{3,2,1,0:T(8,128)(2,1)S(1)}, u32[]{:S(2)}, u32[]{:S(2)}) async-start(bf16[32,8,8,128]{3,2,1,0:T(8,128)(2,1)} %second.1), calls=%async_computation.1 | async-start | bytes 1048576 | tf_op jit(solution)/shard_map/all_to_all | solution.py:736
  76.1 12.2 %collective-permute-start.10 = (bf16[8,7,8,128]{3,2,1,0:T(8,128)(2,1)S(1)}, bf16[8,7,8,128]{3,2,1,0:T(8,128)(2,1)S(1)}, u32[]{:S(2)}, u32[]{:S(2)}) collective-permute-start(bf16[8,7,8,128]{3,2,1,0:T(8,128)(2,1)S(1)} %get-tuple-element.66), channel_id=1, source_target_pairs={{0,8},{1,9},{2,10},{3,11},{4,12},{5,13},{6,14},{7,15},{8,0},{9,1},... | collective-permute-start | bytes 344072 | tf_op jit(solution)/shard_map/ppermute | solution.py:643
  78.0 21.1 %collective-permute-start.11 = (bf16[8,7,8,128]{3,2,1,0:T(8,128)(2,1)S(1)}, bf16[8,7,8,128]{3,2,1,0:T(8,128)(2,1)S(1)}, u32[]{:S(2)}, u32[]{:S(2)}) collective-permute-start(bf16[8,7,8,128]{3,2,1,0:T(8,128)(2,1)S(1)} %get-tuple-element.67), channel_id=1, source_target_pairs={{0,16},{1,17},{2,18},{3,19},{4,20},{5,21},{6,22},{7,23},{8,24},{9,... | collective-permute-start | bytes 344072 | tf_op jit(solution)/shard_map/ppermute | solution.py:643
  80.4 18.7 %collective-permute-start.12 = (bf16[8,7,8,128]{3,2,1,0:T(8,128)(2,1)S(1)}, bf16[8,7,8,128]{3,2,1,0:T(8,128)(2,1)S(1)}, u32[]{:S(2)}, u32[]{:S(2)}) collective-permute-start(bf16[8,7,8,128]{3,2,1,0:T(8,128)(2,1)S(1)} %get-tuple-element.68), channel_id=1, source_target_pairs={{0,24},{1,25},{2,26},{3,27},{4,28},{5,29},{6,30},{7,31},{8,16},{9,... | collective-permute-start | bytes 344072 | tf_op jit(solution)/shard_map/ppermute | solution.py:643
  99.1 3.6 %collective-permute-start.13 = (bf16[4,7,8,128]{3,2,1,0:T(8,128)(2,1)S(1)}, bf16[4,7,8,128]{3,2,1,0:T(8,128)(2,1)S(1)}, u32[]{:S(2)}, u32[]{:S(2)}) collective-permute-start(bf16[4,7,8,128]{3,2,1,0:T(8,128)(2,1)S(1)} %get-tuple-element.70), channel_id=1, source_target_pairs={{0,1},{1,0},{2,3},{3,2},{4,5},{5,4},{6,7},{7,6},{8,9},{9,8},{10,11... | collective-permute-start | bytes 172040 | tf_op jit(solution)/shard_map/ppermute | solution.py:643
  99.2 6.0 %collective-permute-start.14 = (bf16[4,7,8,128]{3,2,1,0:T(8,128)(2,1)S(1)}, bf16[4,7,8,128]{3,2,1,0:T(8,128)(2,1)S(1)}, u32[]{:S(2)}, u32[]{:S(2)}) collective-permute-start(bf16[4,7,8,128]{3,2,1,0:T(8,128)(2,1)S(1)} %get-tuple-element.71), channel_id=1, source_target_pairs={{0,2},{1,3},{2,0},{3,1},{4,6},{5,7},{6,4},{7,5},{8,10},{9,11},{10,... | collective-permute-start | bytes 172040 | tf_op jit(solution)/shard_map/ppermute | solution.py:643
  100.7 4.7 %collective-permute-start.15 = (bf16[4,7,8,128]{3,2,1,0:T(8,128)(2,1)S(1)}, bf16[4,7,8,128]{3,2,1,0:T(8,128)(2,1)S(1)}, u32[]{:S(2)}, u32[]{:S(2)}) collective-permute-start(bf16[4,7,8,128]{3,2,1,0:T(8,128)(2,1)S(1)} %get-tuple-element.72), channel_id=1, source_target_pairs={{0,3},{1,2},{2,1},{3,0},{4,7},{5,6},{6,5},{7,4},{8,11},{9,10},{10,... | collective-permute-start | bytes 172040 | tf_op jit(solution)/shard_map/ppermute | solution.py:643
  101.0 4.4 %collective-permute-start.16 = (bf16[4,7,8,128]{3,2,1,0:T(8,128)(2,1)S(1)}, bf16[4,7,8,128]{3,2,1,0:T(8,128)(2,1)S(1)}, u32[]{:S(2)}, u32[]{:S(2)}) collective-permute-start(bf16[4,7,8,128]{3,2,1,0:T(8,128)(2,1)S(1)} %get-tuple-element.73), channel_id=1, source_target_pairs={{0,4},{1,5},{2,6},{3,7},{4,0},{5,1},{6,2},{7,3},{8,12},{9,13},{10,... | collective-permute-start | bytes 172040 | tf_op jit(solution)/shard_map/ppermute | solution.py:643
  102.5 4.0 %collective-permute-start.17 = (bf16[4,7,8,128]{3,2,1,0:T(8,128)(2,1)S(1)}, bf16[4,7,8,128]{3,2,1,0:T(8,128)(2,1)S(1)}, u32[]{:S(2)}, u32[]{:S(2)}) collective-permute-start(bf16[4,7,8,128]{3,2,1,0:T(8,128)(2,1)S(1)} %get-tuple-element.74), channel_id=1, source_target_pairs={{0,5},{1,4},{2,7},{3,6},{4,1},{5,0},{6,3},{7,2},{8,13},{9,12},{10,... | collective-permute-start | bytes 172040 | tf_op jit(solution)/shard_map/ppermute | solution.py:643
  102.7 6.1 %collective-permute-start.18 = (bf16[4,7,8,128]{3,2,1,0:T(8,128)(2,1)S(1)}, bf16[4,7,8,128]{3,2,1,0:T(8,128)(2,1)S(1)}, u32[]{:S(2)}, u32[]{:S(2)}) collective-permute-start(bf16[4,7,8,128]{3,2,1,0:T(8,128)(2,1)S(1)} %get-tuple-element.75), channel_id=1, source_target_pairs={{0,6},{1,7},{2,4},{3,5},{4,2},{5,3},{6,0},{7,1},{8,14},{9,15},{10,... | collective-permute-start | bytes 172040 | tf_op jit(solution)/shard_map/ppermute | solution.py:643
  105.1 4.8 %collective-permute-start.19 = (bf16[4,7,8,128]{3,2,1,0:T(8,128)(2,1)S(1)}, bf16[4,7,8,128]{3,2,1,0:T(8,128)(2,1)S(1)}, u32[]{:S(2)}, u32[]{:S(2)}) collective-permute-start(bf16[4,7,8,128]{3,2,1,0:T(8,128)(2,1)S(1)} %get-tuple-element.76), channel_id=1, source_target_pairs={{0,7},{1,6},{2,5},{3,4},{4,3},{5,2},{6,1},{7,0},{8,15},{9,14},{10,... | collective-permute-start | bytes 172040 | tf_op jit(solution)/shard_map/ppermute | solution.py:643

commit v6 on v5

--- a/solution.py
+++ b/solution.py
@@ -335,24 +335,28 @@
     dims,
     off_rows_ref,
     psi_ref,
-    pot_ref,
+    cross_ref,
     kin_ref,
     kern_ref,
     mult_ref,
     patt_ref,
-    cross_hbm,
+    pot_hbm,
+    last_hbm,
+    out_hbm,
     out_ref,
     result_ref,
-    cross_ref,
+    pot_ref,
+    last_ref,
     sems,
+    out_sems,
 ):
     fn_count, edge, plane_len, classes, shares, chunk, reach = dims
-    copies = fetch([(cross_hbm.at[k], cross_ref.at[k]) for k in range(cross_ref.shape[0])], sems)
+    copies = fetch(((pot_hbm, pot_ref), (last_hbm, last_ref)), sems)
+    stacks = [cross_ref.at[k] for k in range(cross_ref.shape[0])] + [last_ref.at[0]]
     rows = fn_count * edge
     tiles = plane_len // LANES // shares
     chunks = plane_len // chunk
     psi = psi_ref[...].reshape(rows, plane_len)
-    pot = pot_ref[...].reshape(rows, plane_len)
     off_rows = off_rows_ref[...]
     shape = (classes, 2 * SUBLANES, LANES)
     select = class_select(iota(shape, 0), off_rows, fn_count, edge, classes)
@@ -362,30 +366,43 @@
     small = [coefficient_rows(ref[...], patt, off_rows, fn_count)[None] for ref in (mult_ref, kern_ref)]
     upper = iota(shape, 1) < fn_count
     led = dot(kin_ref[...], psi)
+    late = 2 * EARLY_PAIRS
+    rest = [
+        dot(deep, psi[:, (share * tiles + late) * LANES : (share + 1) * tiles * LANES]).reshape(
+            classes, SUBLANES, -1
+        )
+        for share in range(shares)
+    ]
+    copies[0].wait()
+    pot = pot_ref[...].reshape(rows, plane_len)
     for j in range(chunks):
-        if j < len(copies):
-            copies[j].wait()
+        if j == len(stacks) - 1:
+            copies[1].wait()
         lo, hi = max(0, j - reach), min(chunks, j + reach + 1)
         here = slice(j * chunk, (j + 1) * chunk)
         acc = dot(
             psi[:, lo * chunk : hi * chunk],
-            cross_ref[j % cross_ref.shape[0], (lo - j + reach) * chunk : (hi - j + reach) * chunk],
+            stacks[j % len(stacks)][(lo - j + reach) * chunk : (hi - j + reach) * chunk, :],
         )
         acc = acc + led[:, here]
         acc = acc + pot[:, here].astype(jnp.float32) * psi[:, here].astype(jnp.float32)
         result_ref[:, here] = acc.astype(jnp.bfloat16)
-    ordered = dot(select, result_ref[...]).reshape(classes, 2, SUBLANES, plane_len)
-    late = 2 * EARLY_PAIRS
+    leaving = []
     for share in range(shares):
-        first, last = share * tiles * LANES, (share + 1) * tiles * LANES
+        first, last = 0, tiles * LANES
+        ordered = dot(select, result_ref[:, share * last : (share + 1) * last])
+        ordered = ordered.reshape(classes, 2, SUBLANES, last)
         for t in range(tiles):
             at = slice(first + t * LANES, first + (t + 1) * LANES)
             out_ref[:, share, t] = ordered[:, 0, :, at].astype(jnp.bfloat16)
-        rest = dot(deep, psi[:, first + late * LANES : last]).reshape(classes, SUBLANES, -1)
         made = pair_units(ordered[:, 1, :, first:last], tiles, upper, small[0])
-        made += pair_units(rest, tiles - late, upper, small[1])
+        made += pair_units(rest[share], tiles - late, upper, small[1])
         for v, piece in enumerate(made):
             out_ref[:, share, tiles + v] = piece
+        leaving.append(pltpu.make_async_copy(out_ref.at[:, share], out_hbm.at[:, share], out_sems.at[share]))
+        leaving[-1].start()
+    for copy in leaving:
+        copy.wait()
 
 
 def turn_kernel(*refs):
@@ -502,7 +519,14 @@
     full = devices * SUBLANES
     planes = devices * Q // classes
     pairs = (tiles + 1) // 2
-    stacked, _ = grid_rows(psi_all, h_ref, tiles, fn_count, range(tiles))
+    stacked, both = grid_rows(psi_all, h_ref, tiles, fn_count, range(tiles))
+    upper = iota((devices // 2, SUBLANES, LANES), 1) < fn_count
+    dense_rows = []
+    for t in range(tiles):
+        two = both[t].reshape(devices // 2, 2, SUBLANES, LANES)
+        two = jnp.where(upper, two[:, 0], pltpu.roll(two[:, 1], fn_count, axis=1))
+        dense_rows.append(two.reshape(full // 2, LANES).astype(jnp.bfloat16))
+    psi_rows = jnp.concatenate([stacked[0], jnp.concatenate(dense_rows, axis=1)], axis=0)
     gap = gap_ref[...]
     half_row = jnp.bitwise_and(iota((full, full), 0) // fn_count, 1)
     low = same_plane(gap, planes, half_row, fn_count)
@@ -520,15 +544,19 @@
 
     sums = []
     for part in range(3):
-        low_gram = jnp.where(low[part], dot_nt(stacked[0], stacked[part]), 0.0)
-        top_gram = dot_nt(stacked[1], stacked[part])
-        top_gram = jnp.where(top[part] & (half_row == 0), top_gram, 0.0)
-        total = (low_gram + top_gram).reshape(devices, SUBLANES, full)
-        sums.append(total + pltpu.roll(total, fn_count, axis=1))
+        gram = dot_nt(psi_rows, stacked[part])
+        low_gram = jnp.where(low[part], gram[:full], 0.0).reshape(devices, SUBLANES, full)
+        deep = gram[full:].reshape(devices // 2, SUBLANES, full)
+        other = pltpu.roll(deep, fn_count, axis=1)
+        upper = iota(deep.shape, 1) < fn_count
+        deep = jnp.stack([jnp.where(upper, deep, other), jnp.where(upper, other, deep)], axis=1)
+        deep = jnp.where(top[part], deep.reshape(full, full), 0.0).reshape(devices, SUBLANES, full)
+        sums.append(low_gram + pltpu.roll(low_gram, fn_count, axis=1) + deep)
     first = sums[0] + pltpu.roll(sums[0], full - fn_count, axis=2)
     third = sums[2] + pltpu.roll(sums[2], fn_count, axis=2)
     lanes_half = jnp.bitwise_and(iota((devices, SUBLANES, full), 2) // fn_count, 1)
     bands = sums[1] + jnp.where(lanes_half == 0, first, third)
+    upper = iota((devices, SUBLANES, LANES), 1) < fn_count
     bands = jnp.where(upper, bands[:, :, :LANES], bands[:, :, LANES:])
     bands = bands * (1.0 / float(edge**3))
     out_ref[:, tiles - EARLY_TILES + pairs] = bands.astype(jnp.bfloat16)
@@ -644,8 +672,7 @@
 
     axes = ("brick", "sub")
     size = psi.size
-    kinetic, cross = jnp.asarray(kinetic), jnp.asarray(cross)
-    carried = (psi, potential, kinetic, kernel, multipliers, pattern)
+    carried = (psi, cross[:-1], kinetic, kernel, multipliers, pattern)
     results = pl.pallas_call(
         functools.partial(
             pack_kernel, (fn_count, edge, plane_len, classes, shares, groups, sub_count, len(carried))
@@ -662,7 +689,7 @@
         compiler_params=params,
         cost_estimate=cost(512 * size, 4 * size),
         name="pack",
-    )(offsets, *(in_hbm(x) for x in carried))
+    )(offsets, *(in_hbm(jnp.asarray(x)) for x in carried))
     packed, kept = results[:groups], results[groups:-2]
     off_rows, off_lanes = results[-2:]
     packed = [x.reshape(near, early, SUBLANES, LANES) for x in packed]
@@ -674,17 +701,20 @@
     applied = pl.pallas_call(
         functools.partial(apply_kernel, (fn_count, edge, plane_len, classes, shares, chunk, reach)),
         out_shape=block(classes, shares, units),
-        in_specs=[vmem] * (1 + len(kept)) + [hbm],
-        out_specs=vmem,
+        in_specs=[vmem] * (1 + len(kept)) + [hbm] * 2,
+        out_specs=hbm,
         scratch_shapes=[
+            pltpu.VMEM((classes, shares, units, SUBLANES, LANES), jnp.bfloat16),
             pltpu.VMEM((fn_count * edge, plane_len), jnp.bfloat16),
-            pltpu.VMEM(cross.shape, jnp.bfloat16),
-            pltpu.SemaphoreType.DMA((cross.shape[0],)),
+            pltpu.VMEM(potential.shape, potential.dtype),
+            pltpu.VMEM(cross[-1:].shape, jnp.bfloat16),
+            pltpu.SemaphoreType.DMA((2,)),
+            pltpu.SemaphoreType.DMA((shares,)),
         ],
         compiler_params=params,
         cost_estimate=cost(4608 * size, 8 * size),
         name="apply",
-    )(off_rows, *kept, in_hbm(cross))
+    )(off_rows, *kept, in_hbm(potential), in_hbm(jnp.asarray(cross[-1:])))
     held = lax.all_to_all(applied.reshape(devices, units, SUBLANES, LANES), axes, 0, 0, tiled=True)
 
     turned = pl.pallas_call(

time: 112 us -> 112 us (level)
  no operation moved by 1% of the time
where the time goes in v6:
time: 112 us
  waiting for transfers between devices  64.7 us (58%)
  starting transfers between devices  34.2 us (31%)
  Pallas kernels  12.1 us (11%)
    ppermute x20, waiting for transfers between devices, exchange(): return lax.ppermute(array, axes, [(i, i ^ bits) for i in range(devices)])  64.7 us
    ppermute x20, starting transfers between devices, exchange(): return lax.ppermute(array, axes, [(i, i ^ bits) for i in range(devices)])  21.9 us
    all_to_all x1, starting transfers between devices, transposed_shards(): lax.all_to_all(applied.reshape(devices, units, SUBLANES, LANES), axes, 0,...  7.34 us
    all_to_all x1, starting transfers between devices, transposed_shards(): back = lax.all_to_all(made, axes, 0, 0, tiled=True)  4.99 us
    pallas_call x1, Pallas kernels, transposed_shards(): pl.pallas_call(functools.partial(apply_kernel, (fn_count, edge, plane_len...  4.45 us
    pallas_call x1, Pallas kernels, transposed_shards(): pl.pallas_call(functools.partial(second_kernel, (fn_count, edge, classes)...  2.67 us
  transfers between devices with their start and end apart: 22, of which 11 were waited for; matrix products, arithmetic and copies ran while one was open for 0% of the time, Pallas kernels for 0%

profile of v6, /device:TPU:0, one launch (start us, length us, event | category | flops | bytes accessed | tf_op | source)
XLA Modules:
  0.0 111.8 jit_solution(16906001459481867747)
XLA Ops:
  0.6 1.9 %pack.1 = (bf16[4,2,11,8,128]{4,3,2,1,0:T(8,128)(2,1)S(1)}, bf16[4,2,11,8,128]{4,3,2,1,0:T(8,128)(2,1)S(1)}, bf16[4,2,11,8,128]{4,3,2,1,0:T(8,128)(2,1)S(1)}, bf...) custom-call(s32[4]{0:T(128)} %offs_hbm.1, ...), custom_call_target="tpu_custom_call" | custom-call | flops 226492416 | bytes 1769472 | tf_op jit(solution)/shard_map/pack/pallas_call | solution.py:676
  2.5 4.5 %apply.1 = bf16[16,2,17,8,128]{4,3,2,1,0:T(8,128)(2,1)} custom-call(s32[8,128]{1,0:T(8,128)S(1)} %get-tuple-element.53.off_rows_ref, bf16[4,48,2304]{2,1,0:T(8,128)(2,1)S(1)} %get-tuple-element.54.psi_ref, bf16[2,1792,256]{2,1,0:T(8,128)(2,1)S(1)} %get-tuple-element.55.cross_ref, bf16[192,192]{1,0:T(8,128)(2,1)S(1)} %get-tuple-element.56.kin_ref, ...), custom_call_target="tpu_custom_call" | custom-call | flops 2038431744 | bytes 3538944 | tf_op jit(solution)/shard_map/apply/pallas_call | solution.py:701
  7.0 7.3 %all-to-all-start = ((bf16[32,17,8,128]{3,2,1,0:T(8,128)(2,1)}), bf16[32,17,8,128]{3,2,1,0:T(8,128)(2,1)S(1)}, u32[]{:S(2)}, u32[]{:S(2)}) async-start(bf16[32,17,8,128]{3,2,1,0:T(8,128)(2,1)} %bitcast.4), calls=%async_computation | async-start | bytes 2228224 | tf_op jit(solution)/shard_map/all_to_all | solution.py:718
  14.3 1.8 %collective-permute-start = (bf16[8,11,8,128]{3,2,1,0:T(8,128)(2,1)S(1)}, bf16[8,11,8,128]{3,2,1,0:T(8,128)(2,1)S(1)}, u32[]{:S(2)}, u32[]{:S(2)}) collective-permute-start(bf16[8,11,8,128]{3,2,1,0:T(8,128)(2,1)S(1)} %bitcast.10), channel_id=1, source_target_pairs={{0,8},{1,9},{2,10},{3,11},{4,12},{5,13},{6,14},{7,15},{8,0},{9,1},... | collective-permute-start | bytes 540680 | tf_op jit(solution)/shard_map/ppermute | solution.py:671
  16.1 2.4 %collective-permute-start.1 = (bf16[8,11,8,128]{3,2,1,0:T(8,128)(2,1)S(1)}, bf16[8,11,8,128]{3,2,1,0:T(8,128)(2,1)S(1)}, u32[]{:S(2)}, u32[]{:S(2)}) collective-permute-start(bf16[8,11,8,128]{3,2,1,0:T(8,128)(2,1)S(1)} %bitcast.9), channel_id=1, source_target_pairs={{0,16},{1,17},{2,18},{3,19},{4,20},{5,21},{6,22},{7,23},{8,24},{9,... | collective-permute-start | bytes 540680 | tf_op jit(solution)/shard_map/ppermute | solution.py:671
  18.5 0.2 collective-permute-start.2
  18.7 18.4 %collective-permute-done.refs_1_ = bf16[8,11,8,128]{3,2,1,0:T(8,128)(2,1)S(1)} collective-permute-done((bf16[8,11,8,128]{3,2,1,0:T(8,128)(2,1)S(1)}, bf16[8,11,8,128]{3,2,1,0:T(8,128)(2,1)S(1)}, u32[]{:S(2)}, u32[]{:S(2)}) %collective-permute-start) | collective-permute-done | bytes 180256 | tf_op jit(solution)/shard_map/ppermute | solution.py:671
  37.2 16.9 %collective-permute-done.1.refs_2_ = bf16[8,11,8,128]{3,2,1,0:T(8,128)(2,1)S(1)} collective-permute-done((bf16[8,11,8,128]{3,2,1,0:T(8,128)(2,1)S(1)}, bf16[8,11,8,128]{3,2,1,0:T(8,128)(2,1)S(1)}, u32[]{:S(2)}, u32[]{:S(2)}) %collective-permute-start.1) | collective-permute-done | bytes 180256 | tf_op jit(solution)/shard_map/ppermute | solution.py:671
  54.1 0.0 collective-permute-done.2.refs_3_
  54.1 0.1 turn.1
  54.1 0.1 collective-permute-start.3
  54.2 1.6 %collective-permute-start.4 = (bf16[4,11,8,128]{3,2,1,0:T(8,128)(2,1)S(1)}, bf16[4,11,8,128]{3,2,1,0:T(8,128)(2,1)S(1)}, u32[]{:S(2)}, u32[]{:S(2)}) collective-permute-start(bf16[4,11,8,128]{3,2,1,0:T(8,128)(2,1)S(1)} %get-tuple-element.47), channel_id=1, source_target_pairs={{0,2},{1,3},{2,0},{3,1},{4,6},{5,7},{6,4},{7,5},{8,10},{9,11},{10,... | collective-permute-start | bytes 270344 | tf_op jit(solution)/shard_map/ppermute | solution.py:671
  55.8 0.3 collective-permute-start.5
  56.0 1.5 %collective-permute-start.6 = (bf16[4,11,8,128]{3,2,1,0:T(8,128)(2,1)S(1)}, bf16[4,11,8,128]{3,2,1,0:T(8,128)(2,1)S(1)}, u32[]{:S(2)}, u32[]{:S(2)}) collective-permute-start(bf16[4,11,8,128]{3,2,1,0:T(8,128)(2,1)S(1)} %get-tuple-element.49), channel_id=1, source_target_pairs={{0,4},{1,5},{2,6},{3,7},{4,0},{5,1},{6,2},{7,3},{8,12},{9,13},{10,... | collective-permute-start | bytes 270344 | tf_op jit(solution)/shard_map/ppermute | solution.py:671
  57.5 0.2 collective-permute-start.7
  57.8 0.0 collective-permute-done.3.refs_1_
  57.8 2.4 %collective-permute-start.8 = (bf16[4,11,8,128]{3,2,1,0:T(8,128)(2,1)S(1)}, bf16[4,11,8,128]{3,2,1,0:T(8,128)(2,1)S(1)}, u32[]{:S(2)}, u32[]{:S(2)}) collective-permute-start(bf16[4,11,8,128]{3,2,1,0:T(8,128)(2,1)S(1)} %get-tuple-element.51), channel_id=1, source_target_pairs={{0,6},{1,7},{2,4},{3,5},{4,2},{5,3},{6,0},{7,1},{8,14},{9,15},{10,... | collective-permute-start | bytes 270344 | tf_op jit(solution)/shard_map/ppermute | solution.py:671
  60.2 0.0 collective-permute-done.4.refs_2_
  60.2 0.6 collective-permute-start.9
  60.8 0.0 collective-permute-done.5.refs_3_
  60.8 0.6 collective-permute-done.6.refs_4_
  61.4 1.1 collective-permute-done.7.refs_5_
  62.5 3.7 %collective-permute-done.8.refs_6_ = bf16[4,11,8,128]{3,2,1,0:T(8,128)(2,1)S(1)} collective-permute-done((bf16[4,11,8,128]{3,2,1,0:T(8,128)(2,1)S(1)}, bf16[4,11,8,128]{3,2,1,0:T(8,128)(2,1)S(1)}, u32[]{:S(2)}, u32[]{:S(2)}) %collective-permute-start.8) | collective-permute-done | bytes 90144 | tf_op jit(solution)/shard_map/ppermute | solution.py:671
  66.2 1.0 collective-permute-done.9.refs_7_
  67.2 0.0 all-to-all-done.refs_8_.h_ref
  67.2 1.0 first.1
  68.3 2.7 %second.1 = bf16[32,8,8,128]{3,2,1,0:T(8,128)(2,1)} custom-call(bf16[32,11,8,128]{3,2,1,0:T(8,128)(2,1)S(1)} %get-tuple-element.60.psi_all, bf16[32,17,8,128]{3,2,1,0:T(8,128)(2,1)S(1)} %all-to-all-done.refs_8_.h_ref, bf16[256,768]{1,0:T(8,128)(2,1)S(1)} %get-tuple-element.61.low_ref, f32[256,256]{1,0:T(8,128)S(1)} %get-tuple-element.62.plus_ref, ...), custom_call_target="tpu_custom_call" | custom-call | flops 905969664 | bytes 1769472 | tf_op jit(solution)/shard_map/second/pallas_call | solution.py:757
  71.0 5.0 %all-to-all-start.1 = ((bf16[32,8,8,128]{3,2,1,0:T(8,128)(2,1)}), bf16[32,8,8,128]{3,2,1,0:T(8,128)(2,1)S(1)}, u32[]{:S(2)}, u32[]{:S(2)}) async-start(bf16[32,8,8,128]{3,2,1,0:T(8,128)(2,1)} %second.1), calls=%async_computation.1 | async-start | bytes 1048576 | tf_op jit(solution)/shard_map/all_to_all | solution.py:766
  75.9 1.8 %collective-permute-start.10 = (bf16[8,7,8,128]{3,2,1,0:T(8,128)(2,1)S(1)}, bf16[8,7,8,128]{3,2,1,0:T(8,128)(2,1)S(1)}, u32[]{:S(2)}, u32[]{:S(2)}) collective-permute-start(bf16[8,7,8,128]{3,2,1,0:T(8,128)(2,1)S(1)} %get-tuple-element.66), channel_id=1, source_target_pairs={{0,8},{1,9},{2,10},{3,11},{4,12},{5,13},{6,14},{7,15},{8,0},{9,1},... | collective-permute-start | bytes 344072 | tf_op jit(solution)/shard_map/ppermute | solution.py:671
  77.8 2.4 %collective-permute-start.11 = (bf16[8,7,8,128]{3,2,1,0:T(8,128)(2,1)S(1)}, bf16[8,7,8,128]{3,2,1,0:T(8,128)(2,1)S(1)}, u32[]{:S(2)}, u32[]{:S(2)}) collective-permute-start(bf16[8,7,8,128]{3,2,1,0:T(8,128)(2,1)S(1)} %get-tuple-element.67), channel_id=1, source_target_pairs={{0,16},{1,17},{2,18},{3,19},{4,20},{5,21},{6,22},{7,23},{8,24},{9,... | collective-permute-start | bytes 344072 | tf_op jit(solution)/shard_map/ppermute | solution.py:671
  80.2 0.2 collective-permute-start.12
  80.4 7.7 %collective-permute-done.10.refs_1_ = bf16[8,7,8,128]{3,2,1,0:T(8,128)(2,1)S(1)} collective-permute-done((bf16[8,7,8,128]{3,2,1,0:T(8,128)(2,1)S(1)}, bf16[8,7,8,128]{3,2,1,0:T(8,128)(2,1)S(1)}, u32[]{:S(2)}, u32[]{:S(2)}) %collective-permute-start.10) | collective-permute-done | bytes 114720 | tf_op jit(solution)/shard_map/ppermute | solution.py:671
  88.1 10.7 %collective-permute-done.11.refs_2_ = bf16[8,7,8,128]{3,2,1,0:T(8,128)(2,1)S(1)} collective-permute-done((bf16[8,7,8,128]{3,2,1,0:T(8,128)(2,1)S(1)}, bf16[8,7,8,128]{3,2,1,0:T(8,128)(2,1)S(1)}, u32[]{:S(2)}, u32[]{:S(2)}) %collective-permute-start.11) | collective-permute-done | bytes 114720 | tf_op jit(solution)/shard_map/ppermute | solution.py:671
  98.9 0.0 collective-permute-done.12.refs_3_
  98.9 0.1 collective-permute-start.13
  99.0 1.5 %collective-permute-start.14 = (bf16[4,7,8,128]{3,2,1,0:T(8,128)(2,1)S(1)}, bf16[4,7,8,128]{3,2,1,0:T(8,128)(2,1)S(1)}, u32[]{:S(2)}, u32[]{:S(2)}) collective-permute-start(bf16[4,7,8,128]{3,2,1,0:T(8,128)(2,1)S(1)} %get-tuple-element.71), channel_id=1, source_target_pairs={{0,2},{1,3},{2,0},{3,1},{4,6},{5,7},{6,4},{7,5},{8,10},{9,11},{10,... | collective-permute-start | bytes 172040 | tf_op jit(solution)/shard_map/ppermute | solution.py:671
  100.5 0.3 collective-permute-start.15
  100.8 1.5 %collective-permute-start.16 = (bf16[4,7,8,128]{3,2,1,0:T(8,128)(2,1)S(1)}, bf16[4,7,8,128]{3,2,1,0:T(8,128)(2,1)S(1)}, u32[]{:S(2)}, u32[]{:S(2)}) collective-permute-start(bf16[4,7,8,128]{3,2,1,0:T(8,128)(2,1)S(1)} %get-tuple-element.73), channel_id=1, source_target_pairs={{0,4},{1,5},{2,6},{3,7},{4,0},{5,1},{6,2},{7,3},{8,12},{9,13},{10,... | collective-permute-start | bytes 172040 | tf_op jit(solution)/shard_map/ppermute | solution.py:671
  102.3 0.2 collective-permute-start.17
  102.5 0.0 collective-permute-done.13.refs_1_
  102.5 2.4 %collective-permute-start.18 = (bf16[4,7,8,128]{3,2,1,0:T(8,128)(2,1)S(1)}, bf16[4,7,8,128]{3,2,1,0:T(8,128)(2,1)S(1)}, u32[]{:S(2)}, u32[]{:S(2)}) collective-permute-start(bf16[4,7,8,128]{3,2,1,0:T(8,128)(2,1)S(1)} %get-tuple-element.75), channel_id=1, source_target_pairs={{0,6},{1,7},{2,4},{3,5},{4,2},{5,3},{6,0},{7,1},{8,14},{9,15},{10,... | collective-permute-start | bytes 172040 | tf_op jit(solution)/shard_map/ppermute | solution.py:671
  104.9 0.0 collective-permute-done.14.refs_2_
  104.9 0.3 collective-permute-start.19
  105.2 0.0 collective-permute-done.16.refs_4_
  105.2 1.0 collective-permute-done.17.refs_5_
  106.3 2.4 %collective-permute-done.18.refs_6_ = bf16[4,7,8,128]{3,2,1,0:T(8,128)(2,1)S(1)} collective-permute-done((bf16[4,7,8,128]{3,2,1,0:T(8,128)(2,1)S(1)}, bf16[4,7,8,128]{3,2,1,0:T(8,128)(2,1)S(1)}, u32[]{:S(2)}, u32[]{:S(2)}) %collective-permute-start.18) | collective-permute-done | bytes 57376 | tf_op jit(solution)/shard_map/ppermute | solution.py:671
  108.7 1.1 collective-permute-done.19.refs_7_
  109.7 2.0 %receive.1 = (bf16[4,48,2304]{2,1,0:T(8,128)(2,1)}, f32[4,100]{1,0:T(4,128)}, f32[4,100]{1,0:T(4,128)}) custom-call(s32[8,128]{1,0:T(8,128)S(1)} %get-tuple-element.40.off_lanes_ref, bf16[16,2,8,8,128]{4,3,2,1,0:T(8,128)(2,1)S(1)} %bitcast.6, bf16[4,7,8,128]{3,2,1,0:T(8,128)(2,1)S(1)} %get-tuple-element.69.refs_0_, ...), custom_call_target="tpu_custom_call" | custom-call | tf_op jit(solution)/shard_map/receive/pallas_call | solution.py:778
  (3 shorter events, 0.0 us)
Async XLA Ops:
  7.0 60.3 %all-to-all-start = ((bf16[32,17,8,128]{3,2,1,0:T(8,128)(2,1)}), bf16[32,17,8,128]{3,2,1,0:T(8,128)(2,1)S(1)}, u32[]{:S(2)}, u32[]{:S(2)}) async-start(bf16[32,17,8,128]{3,2,1,0:T(8,128)(2,1)} %bitcast.4), calls=%async_computation | async-start | bytes 2228224 | tf_op jit(solution)/shard_map/all_to_all | solution.py:718
  14.3 22.9 %collective-permute-start = (bf16[8,11,8,128]{3,2,1,0:T(8,128)(2,1)S(1)}, bf16[8,11,8,128]{3,2,1,0:T(8,128)(2,1)S(1)}, u32[]{:S(2)}, u32[]{:S(2)}) collective-permute-start(bf16[8,11,8,128]{3,2,1,0:T(8,128)(2,1)S(1)} %bitcast.10), channel_id=1, source_target_pairs={{0,8},{1,9},{2,10},{3,11},{4,12},{5,13},{6,14},{7,15},{8,0},{9,1},... | collective-permute-start | bytes 540680 | tf_op jit(solution)/shard_map/ppermute | solution.py:671
  16.1 37.9 %collective-permute-start.1 = (bf16[8,11,8,128]{3,2,1,0:T(8,128)(2,1)S(1)}, bf16[8,11,8,128]{3,2,1,0:T(8,128)(2,1)S(1)}, u32[]{:S(2)}, u32[]{:S(2)}) collective-permute-start(bf16[8,11,8,128]{3,2,1,0:T(8,128)(2,1)S(1)} %bitcast.9), channel_id=1, source_target_pairs={{0,16},{1,17},{2,18},{3,19},{4,20},{5,21},{6,22},{7,23},{8,24},{9,... | collective-permute-start | bytes 540680 | tf_op jit(solution)/shard_map/ppermute | solution.py:671
  18.5 35.5 %collective-permute-start.2 = (bf16[8,11,8,128]{3,2,1,0:T(8,128)(2,1)S(1)}, bf16[8,11,8,128]{3,2,1,0:T(8,128)(2,1)S(1)}, u32[]{:S(2)}, u32[]{:S(2)}) collective-permute-start(bf16[8,11,8,128]{3,2,1,0:T(8,128)(2,1)S(1)} %bitcast.8), channel_id=1, source_target_pairs={{0,24},{1,25},{2,26},{3,27},{4,28},{5,29},{6,30},{7,31},{8,16},{9,... | collective-permute-start | bytes 540680 | tf_op jit(solution)/shard_map/ppermute | solution.py:671
  54.1 3.6 %collective-permute-start.3 = (bf16[4,11,8,128]{3,2,1,0:T(8,128)(2,1)S(1)}, bf16[4,11,8,128]{3,2,1,0:T(8,128)(2,1)S(1)}, u32[]{:S(2)}, u32[]{:S(2)}) collective-permute-start(bf16[4,11,8,128]{3,2,1,0:T(8,128)(2,1)S(1)} %get-tuple-element.46), channel_id=1, source_target_pairs={{0,1},{1,0},{2,3},{3,2},{4,5},{5,4},{6,7},{7,6},{8,9},{9,8},{10,11... | collective-permute-start | bytes 270344 | tf_op jit(solution)/shard_map/ppermute | solution.py:671
  54.2 6.0 %collective-permute-start.4 = (bf16[4,11,8,128]{3,2,1,0:T(8,128)(2,1)S(1)}, bf16[4,11,8,128]{3,2,1,0:T(8,128)(2,1)S(1)}, u32[]{:S(2)}, u32[]{:S(2)}) collective-permute-start(bf16[4,11,8,128]{3,2,1,0:T(8,128)(2,1)S(1)} %get-tuple-element.47), channel_id=1, source_target_pairs={{0,2},{1,3},{2,0},{3,1},{4,6},{5,7},{6,4},{7,5},{8,10},{9,11},{10,... | collective-permute-start | bytes 270344 | tf_op jit(solution)/shard_map/ppermute | solution.py:671
  55.8 5.0 %collective-permute-start.5 = (bf16[4,11,8,128]{3,2,1,0:T(8,128)(2,1)S(1)}, bf16[4,11,8,128]{3,2,1,0:T(8,128)(2,1)S(1)}, u32[]{:S(2)}, u32[]{:S(2)}) collective-permute-start(bf16[4,11,8,128]{3,2,1,0:T(8,128)(2,1)S(1)} %get-tuple-element.48), channel_id=1, source_target_pairs={{0,3},{1,2},{2,1},{3,0},{4,7},{5,6},{6,5},{7,4},{8,11},{9,10},{10,... | collective-permute-start | bytes 270344 | tf_op jit(solution)/shard_map/ppermute | solution.py:671
  56.0 5.3 %collective-permute-start.6 = (bf16[4,11,8,128]{3,2,1,0:T(8,128)(2,1)S(1)}, bf16[4,11,8,128]{3,2,1,0:T(8,128)(2,1)S(1)}, u32[]{:S(2)}, u32[]{:S(2)}) collective-permute-start(bf16[4,11,8,128]{3,2,1,0:T(8,128)(2,1)S(1)} %get-tuple-element.49), channel_id=1, source_target_pairs={{0,4},{1,5},{2,6},{3,7},{4,0},{5,1},{6,2},{7,3},{8,12},{9,13},{10,... | collective-permute-start | bytes 270344 | tf_op jit(solution)/shard_map/ppermute | solution.py:671
  57.5 4.9 %collective-permute-start.7 = (bf16[4,11,8,128]{3,2,1,0:T(8,128)(2,1)S(1)}, bf16[4,11,8,128]{3,2,1,0:T(8,128)(2,1)S(1)}, u32[]{:S(2)}, u32[]{:S(2)}) collective-permute-start(bf16[4,11,8,128]{3,2,1,0:T(8,128)(2,1)S(1)} %get-tuple-element.50), channel_id=1, source_target_pairs={{0,5},{1,4},{2,7},{3,6},{4,1},{5,0},{6,3},{7,2},{8,13},{9,12},{10,... | collective-permute-start | bytes 270344 | tf_op jit(solution)/shard_map/ppermute | solution.py:671
  57.8 8.4 %collective-permute-start.8 = (bf16[4,11,8,128]{3,2,1,0:T(8,128)(2,1)S(1)}, bf16[4,11,8,128]{3,2,1,0:T(8,128)(2,1)S(1)}, u32[]{:S(2)}, u32[]{:S(2)}) collective-permute-start(bf16[4,11,8,128]{3,2,1,0:T(8,128)(2,1)S(1)} %get-tuple-element.51), channel_id=1, source_target_pairs={{0,6},{1,7},{2,4},{3,5},{4,2},{5,3},{6,0},{7,1},{8,14},{9,15},{10,... | collective-permute-start | bytes 270344 | tf_op jit(solution)/shard_map/ppermute | solution.py:671
  60.2 7.1 %collective-permute-start.9 = (bf16[4,11,8,128]{3,2,1,0:T(8,128)(2,1)S(1)}, bf16[4,11,8,128]{3,2,1,0:T(8,128)(2,1)S(1)}, u32[]{:S(2)}, u32[]{:S(2)}) collective-permute-start(bf16[4,11,8,128]{3,2,1,0:T(8,128)(2,1)S(1)} %get-tuple-element.52), channel_id=1, source_target_pairs={{0,7},{1,6},{2,5},{3,4},{4,3},{5,2},{6,1},{7,0},{8,15},{9,14},{10,... | collective-permute-start | bytes 270344 | tf_op jit(solution)/shard_map/ppermute | solution.py:671
  71.0 38.8 %all-to-all-start.1 = ((bf16[32,8,8,128]{3,2,1,0:T(8,128)(2,1)}), bf16[32,8,8,128]{3,2,1,0:T(8,128)(2,1)S(1)}, u32[]{:S(2)}, u32[]{:S(2)}) async-start(bf16[32,8,8,128]{3,2,1,0:T(8,128)(2,1)} %second.1), calls=%async_computation.1 | async-start | bytes 1048576 | tf_op jit(solution)/shard_map/all_to_all | solution.py:766
  75.9 12.2 %collective-permute-start.10 = (bf16[8,7,8,128]{3,2,1,0:T(8,128)(2,1)S(1)}, bf16[8,7,8,128]{3,2,1,0:T(8,128)(2,1)S(1)}, u32[]{:S(2)}, u32[]{:S(2)}) collective-permute-start(bf16[8,7,8,128]{3,2,1,0:T(8,128)(2,1)S(1)} %get-tuple-element.66), channel_id=1, source_target_pairs={{0,8},{1,9},{2,10},{3,11},{4,12},{5,13},{6,14},{7,15},{8,0},{9,1},... | collective-permute-start | bytes 344072 | tf_op jit(solution)/shard_map/ppermute | solution.py:671
  77.8 21.1 %collective-permute-start.11 = (bf16[8,7,8,128]{3,2,1,0:T(8,128)(2,1)S(1)}, bf16[8,7,8,128]{3,2,1,0:T(8,128)(2,1)S(1)}, u32[]{:S(2)}, u32[]{:S(2)}) collective-permute-start(bf16[8,7,8,128]{3,2,1,0:T(8,128)(2,1)S(1)} %get-tuple-element.67), channel_id=1, source_target_pairs={{0,16},{1,17},{2,18},{3,19},{4,20},{5,21},{6,22},{7,23},{8,24},{9,... | collective-permute-start | bytes 344072 | tf_op jit(solution)/shard_map/ppermute | solution.py:671
  80.2 18.7 %collective-permute-start.12 = (bf16[8,7,8,128]{3,2,1,0:T(8,128)(2,1)S(1)}, bf16[8,7,8,128]{3,2,1,0:T(8,128)(2,1)S(1)}, u32[]{:S(2)}, u32[]{:S(2)}) collective-permute-start(bf16[8,7,8,128]{3,2,1,0:T(8,128)(2,1)S(1)} %get-tuple-element.68), channel_id=1, source_target_pairs={{0,24},{1,25},{2,26},{3,27},{4,28},{5,29},{6,30},{7,31},{8,16},{9,... | collective-permute-start | bytes 344072 | tf_op jit(solution)/shard_map/ppermute | solution.py:671
  98.9 3.6 %collective-permute-start.13 = (bf16[4,7,8,128]{3,2,1,0:T(8,128)(2,1)S(1)}, bf16[4,7,8,128]{3,2,1,0:T(8,128)(2,1)S(1)}, u32[]{:S(2)}, u32[]{:S(2)}) collective-permute-start(bf16[4,7,8,128]{3,2,1,0:T(8,128)(2,1)S(1)} %get-tuple-element.70), channel_id=1, source_target_pairs={{0,1},{1,0},{2,3},{3,2},{4,5},{5,4},{6,7},{7,6},{8,9},{9,8},{10,11... | collective-permute-start | bytes 172040 | tf_op jit(solution)/shard_map/ppermute | solution.py:671
  99.0 6.0 %collective-permute-start.14 = (bf16[4,7,8,128]{3,2,1,0:T(8,128)(2,1)S(1)}, bf16[4,7,8,128]{3,2,1,0:T(8,128)(2,1)S(1)}, u32[]{:S(2)}, u32[]{:S(2)}) collective-permute-start(bf16[4,7,8,128]{3,2,1,0:T(8,128)(2,1)S(1)} %get-tuple-element.71), channel_id=1, source_target_pairs={{0,2},{1,3},{2,0},{3,1},{4,6},{5,7},{6,4},{7,5},{8,10},{9,11},{10,... | collective-permute-start | bytes 172040 | tf_op jit(solution)/shard_map/ppermute | solution.py:671
  100.5 4.7 %collective-permute-start.15 = (bf16[4,7,8,128]{3,2,1,0:T(8,128)(2,1)S(1)}, bf16[4,7,8,128]{3,2,1,0:T(8,128)(2,1)S(1)}, u32[]{:S(2)}, u32[]{:S(2)}) collective-permute-start(bf16[4,7,8,128]{3,2,1,0:T(8,128)(2,1)S(1)} %get-tuple-element.72), channel_id=1, source_target_pairs={{0,3},{1,2},{2,1},{3,0},{4,7},{5,6},{6,5},{7,4},{8,11},{9,10},{10,... | collective-permute-start | bytes 172040 | tf_op jit(solution)/shard_map/ppermute | solution.py:671
  100.8 4.4 %collective-permute-start.16 = (bf16[4,7,8,128]{3,2,1,0:T(8,128)(2,1)S(1)}, bf16[4,7,8,128]{3,2,1,0:T(8,128)(2,1)S(1)}, u32[]{:S(2)}, u32[]{:S(2)}) collective-permute-start(bf16[4,7,8,128]{3,2,1,0:T(8,128)(2,1)S(1)} %get-tuple-element.73), channel_id=1, source_target_pairs={{0,4},{1,5},{2,6},{3,7},{4,0},{5,1},{6,2},{7,3},{8,12},{9,13},{10,... | collective-permute-start | bytes 172040 | tf_op jit(solution)/shard_map/ppermute | solution.py:671
  102.3 4.0 %collective-permute-start.17 = (bf16[4,7,8,128]{3,2,1,0:T(8,128)(2,1)S(1)}, bf16[4,7,8,128]{3,2,1,0:T(8,128)(2,1)S(1)}, u32[]{:S(2)}, u32[]{:S(2)}) collective-permute-start(bf16[4,7,8,128]{3,2,1,0:T(8,128)(2,1)S(1)} %get-tuple-element.74), channel_id=1, source_target_pairs={{0,5},{1,4},{2,7},{3,6},{4,1},{5,0},{6,3},{7,2},{8,13},{9,12},{10,... | collective-permute-start | bytes 172040 | tf_op jit(solution)/shard_map/ppermute | solution.py:671
  102.5 6.1 %collective-permute-start.18 = (bf16[4,7,8,128]{3,2,1,0:T(8,128)(2,1)S(1)}, bf16[4,7,8,128]{3,2,1,0:T(8,128)(2,1)S(1)}, u32[]{:S(2)}, u32[]{:S(2)}) collective-permute-start(bf16[4,7,8,128]{3,2,1,0:T(8,128)(2,1)S(1)} %get-tuple-element.75), channel_id=1, source_target_pairs={{0,6},{1,7},{2,4},{3,5},{4,2},{5,3},{6,0},{7,1},{8,14},{9,15},{10,... | collective-permute-start | bytes 172040 | tf_op jit(solution)/shard_map/ppermute | solution.py:671
  104.9 4.8 %collective-permute-start.19 = (bf16[4,7,8,128]{3,2,1,0:T(8,128)(2,1)S(1)}, bf16[4,7,8,128]{3,2,1,0:T(8,128)(2,1)S(1)}, u32[]{:S(2)}, u32[]{:S(2)}) collective-permute-start(bf16[4,7,8,128]{3,2,1,0:T(8,128)(2,1)S(1)} %get-tuple-element.76), channel_id=1, source_target_pairs={{0,7},{1,6},{2,5},{3,4},{4,3},{5,2},{6,1},{7,0},{8,15},{9,14},{10,... | collective-permute-start | bytes 172040 | tf_op jit(solution)/shard_map/ppermute | solution.py:671

commit v7 on v6

--- a/solution.py
+++ b/solution.py
@@ -168,7 +168,7 @@
 
 
 EARLY_PAIRS = 2
-EARLY_TILES = 7
+EARLY_TILES = 8
 SUBLANES = 8
 LANES = 128
 
@@ -670,6 +670,12 @@
     def exchange(array, bits):
         return lax.ppermute(array, axes, [(i, i ^ bits) for i in range(devices)])
 
+    def within(blocks):
+        moved = {}
+        for n in range(len(blocks) - 1, 0, -1):
+            moved[n] = exchange(blocks[n], n)
+        return [blocks[0]] + [moved[n] for n in range(1, len(blocks))]
+
     axes = ("brick", "sub")
     size = psi.size
     carried = (psi, cross[:-1], kinetic, kernel, multipliers, pattern)
@@ -726,7 +732,7 @@
         cost_estimate=cost(0, 4 * size),
         name="turn",
     )(*arrived)
-    gathered = [x if n == 0 else exchange(x, n) for n, x in enumerate(turned)]
+    gathered = within(turned)
 
     full = devices * SUBLANES
     results = pl.pallas_call(
@@ -774,7 +780,7 @@
         cost_estimate=cost(0, 4 * size),
         name="spread",
     )(*returned)
-    homed = [x if n == 0 else exchange(x, n) for n, x in enumerate(spread)]
+    homed = within(spread)
     return pl.pallas_call(
         functools.partial(
             receive_kernel, (fn_count, edge, plane_len, classes, shares, band_reach, sub_count, near)

time: 112 us -> 112 us (level)
  no operation moved by 1% of the time
where the time goes in v7:
time: 112 us
  waiting for transfers between devices  64.9 us (58%)
  starting transfers between devices  34.2 us (31%)
  Pallas kernels  12.1 us (11%)
    ppermute x20, waiting for transfers between devices, exchange(): return lax.ppermute(array, axes, [(i, i ^ bits) for i in range(devices)])  64.9 us
    ppermute x20, starting transfers between devices, exchange(): return lax.ppermute(array, axes, [(i, i ^ bits) for i in range(devices)])  21.9 us
    all_to_all x1, starting transfers between devices, transposed_shards(): lax.all_to_all(applied.reshape(devices, units, SUBLANES, LANES), axes, 0,...  7.34 us
    all_to_all x1, starting transfers between devices, transposed_shards(): back = lax.all_to_all(made, axes, 0, 0, tiled=True)  4.98 us
    pallas_call x1, Pallas kernels, transposed_shards(): pl.pallas_call(functools.partial(apply_kernel, (fn_count, edge, plane_len...  4.45 us
    pallas_call x1, Pallas kernels, transposed_shards(): pl.pallas_call(functools.partial(second_kernel, (fn_count, edge, classes)...  2.63 us
  transfers between devices with their start and end apart: 22, of which 11 were waited for; matrix products, arithmetic and copies ran while one was open for 0% of the time, Pallas kernels for 0%

profile of v7, /device:TPU:0, one launch (start us, length us, event | category | flops | bytes accessed | tf_op | source)
XLA Modules:
  0.0 111.9 jit_solution(15315526797513263452)
XLA Ops:
  0.6 1.9 %pack.1 = (bf16[4,2,11,8,128]{4,3,2,1,0:T(8,128)(2,1)S(1)}, bf16[4,2,11,8,128]{4,3,2,1,0:T(8,128)(2,1)S(1)}, bf16[4,2,11,8,128]{4,3,2,1,0:T(8,128)(2,1)S(1)}, bf...) custom-call(s32[4]{0:T(128)} %offs_hbm.1, ...), custom_call_target="tpu_custom_call" | custom-call | flops 226492416 | bytes 1769472 | tf_op jit(solution)/shard_map/pack/pallas_call | solution.py:682
  2.5 4.5 %apply.1 = bf16[16,2,17,8,128]{4,3,2,1,0:T(8,128)(2,1)} custom-call(s32[8,128]{1,0:T(8,128)S(1)} %get-tuple-element.53.off_rows_ref, bf16[4,48,2304]{2,1,0:T(8,128)(2,1)S(1)} %get-tuple-element.54.psi_ref, bf16[2,1792,256]{2,1,0:T(8,128)(2,1)S(1)} %get-tuple-element.55.cross_ref, bf16[192,192]{1,0:T(8,128)(2,1)S(1)} %get-tuple-element.56.kin_ref, ...), custom_call_target="tpu_custom_call" | custom-call | flops 2038431744 | bytes 3538944 | tf_op jit(solution)/shard_map/apply/pallas_call | solution.py:707
  7.0 7.3 %all-to-all-start = ((bf16[32,17,8,128]{3,2,1,0:T(8,128)(2,1)}), bf16[32,17,8,128]{3,2,1,0:T(8,128)(2,1)S(1)}, u32[]{:S(2)}, u32[]{:S(2)}) async-start(bf16[32,17,8,128]{3,2,1,0:T(8,128)(2,1)} %bitcast.4), calls=%async_computation | async-start | bytes 2228224 | tf_op jit(solution)/shard_map/all_to_all | solution.py:724
  14.3 1.8 %collective-permute-start = (bf16[8,11,8,128]{3,2,1,0:T(8,128)(2,1)S(1)}, bf16[8,11,8,128]{3,2,1,0:T(8,128)(2,1)S(1)}, u32[]{:S(2)}, u32[]{:S(2)}) collective-permute-start(bf16[8,11,8,128]{3,2,1,0:T(8,128)(2,1)S(1)} %bitcast.10), channel_id=1, source_target_pairs={{0,8},{1,9},{2,10},{3,11},{4,12},{5,13},{6,14},{7,15},{8,0},{9,1},... | collective-permute-start | bytes 540680 | tf_op jit(solution)/shard_map/ppermute | solution.py:671
  16.1 2.4 %collective-permute-start.1 = (bf16[8,11,8,128]{3,2,1,0:T(8,128)(2,1)S(1)}, bf16[8,11,8,128]{3,2,1,0:T(8,128)(2,1)S(1)}, u32[]{:S(2)}, u32[]{:S(2)}) collective-permute-start(bf16[8,11,8,128]{3,2,1,0:T(8,128)(2,1)S(1)} %bitcast.9), channel_id=1, source_target_pairs={{0,16},{1,17},{2,18},{3,19},{4,20},{5,21},{6,22},{7,23},{8,24},{9,... | collective-permute-start | bytes 540680 | tf_op jit(solution)/shard_map/ppermute | solution.py:671
  18.5 0.2 collective-permute-start.2
  18.7 18.4 %collective-permute-done.refs_1_ = bf16[8,11,8,128]{3,2,1,0:T(8,128)(2,1)S(1)} collective-permute-done((bf16[8,11,8,128]{3,2,1,0:T(8,128)(2,1)S(1)}, bf16[8,11,8,128]{3,2,1,0:T(8,128)(2,1)S(1)}, u32[]{:S(2)}, u32[]{:S(2)}) %collective-permute-start) | collective-permute-done | bytes 180256 | tf_op jit(solution)/shard_map/ppermute | solution.py:671
  37.2 16.9 %collective-permute-done.1.refs_2_ = bf16[8,11,8,128]{3,2,1,0:T(8,128)(2,1)S(1)} collective-permute-done((bf16[8,11,8,128]{3,2,1,0:T(8,128)(2,1)S(1)}, bf16[8,11,8,128]{3,2,1,0:T(8,128)(2,1)S(1)}, u32[]{:S(2)}, u32[]{:S(2)}) %collective-permute-start.1) | collective-permute-done | bytes 180256 | tf_op jit(solution)/shard_map/ppermute | solution.py:671
  54.1 0.0 collective-permute-done.2.refs_3_
  54.1 0.1 turn.1
  54.1 0.1 collective-permute-start.3
  54.2 1.6 %collective-permute-start.4 = (bf16[4,11,8,128]{3,2,1,0:T(8,128)(2,1)S(1)}, bf16[4,11,8,128]{3,2,1,0:T(8,128)(2,1)S(1)}, u32[]{:S(2)}, u32[]{:S(2)}) collective-permute-start(bf16[4,11,8,128]{3,2,1,0:T(8,128)(2,1)S(1)} %get-tuple-element.47), channel_id=1, source_target_pairs={{0,2},{1,3},{2,0},{3,1},{4,6},{5,7},{6,4},{7,5},{8,10},{9,11},{10,... | collective-permute-start | bytes 270344 | tf_op jit(solution)/shard_map/ppermute | solution.py:671
  55.8 0.3 collective-permute-start.5
  56.0 1.5 %collective-permute-start.6 = (bf16[4,11,8,128]{3,2,1,0:T(8,128)(2,1)S(1)}, bf16[4,11,8,128]{3,2,1,0:T(8,128)(2,1)S(1)}, u32[]{:S(2)}, u32[]{:S(2)}) collective-permute-start(bf16[4,11,8,128]{3,2,1,0:T(8,128)(2,1)S(1)} %get-tuple-element.49), channel_id=1, source_target_pairs={{0,4},{1,5},{2,6},{3,7},{4,0},{5,1},{6,2},{7,3},{8,12},{9,13},{10,... | collective-permute-start | bytes 270344 | tf_op jit(solution)/shard_map/ppermute | solution.py:671
  57.5 0.2 collective-permute-start.7
  57.8 0.0 collective-permute-done.3.refs_1_
  57.8 2.4 %collective-permute-start.8 = (bf16[4,11,8,128]{3,2,1,0:T(8,128)(2,1)S(1)}, bf16[4,11,8,128]{3,2,1,0:T(8,128)(2,1)S(1)}, u32[]{:S(2)}, u32[]{:S(2)}) collective-permute-start(bf16[4,11,8,128]{3,2,1,0:T(8,128)(2,1)S(1)} %get-tuple-element.51), channel_id=1, source_target_pairs={{0,6},{1,7},{2,4},{3,5},{4,2},{5,3},{6,0},{7,1},{8,14},{9,15},{10,... | collective-permute-start | bytes 270344 | tf_op jit(solution)/shard_map/ppermute | solution.py:671
  60.2 0.0 collective-permute-done.4.refs_2_
  60.2 0.6 collective-permute-start.9
  60.8 0.0 collective-permute-done.5.refs_3_
  60.8 0.6 collective-permute-done.6.refs_4_
  61.4 1.1 collective-permute-done.7.refs_5_
  62.5 3.7 %collective-permute-done.8.refs_6_ = bf16[4,11,8,128]{3,2,1,0:T(8,128)(2,1)S(1)} collective-permute-done((bf16[4,11,8,128]{3,2,1,0:T(8,128)(2,1)S(1)}, bf16[4,11,8,128]{3,2,1,0:T(8,128)(2,1)S(1)}, u32[]{:S(2)}, u32[]{:S(2)}) %collective-permute-start.8) | collective-permute-done | bytes 90144 | tf_op jit(solution)/shard_map/ppermute | solution.py:671
  66.2 1.0 collective-permute-done.9.refs_7_
  67.2 0.0 all-to-all-done.refs_8_.h_ref
  67.2 1.1 first.1
  68.3 2.6 %second.1 = bf16[32,7,8,128]{3,2,1,0:T(8,128)(2,1)} custom-call(bf16[32,11,8,128]{3,2,1,0:T(8,128)(2,1)S(1)} %get-tuple-element.60.psi_all, bf16[32,17,8,128]{3,2,1,0:T(8,128)(2,1)S(1)} %all-to-all-done.refs_8_.h_ref, bf16[256,768]{1,0:T(8,128)(2,1)S(1)} %get-tuple-element.61.low_ref, f32[256,256]{1,0:T(8,128)S(1)} %get-tuple-element.62.plus_ref, ...), custom_call_target="tpu_custom_call" | custom-call | flops 905969664 | bytes 1769472 | tf_op jit(solution)/shard_map/second/pallas_call | solution.py:763
  70.9 5.0 %all-to-all-start.1 = ((bf16[32,7,8,128]{3,2,1,0:T(8,128)(2,1)}), bf16[32,7,8,128]{3,2,1,0:T(8,128)(2,1)S(1)}, u32[]{:S(2)}, u32[]{:S(2)}) async-start(bf16[32,7,8,128]{3,2,1,0:T(8,128)(2,1)} %second.1), calls=%async_computation.1 | async-start | bytes 917504 | tf_op jit(solution)/shard_map/all_to_all | solution.py:772
  75.9 1.8 %collective-permute-start.10 = (bf16[8,8,8,128]{3,2,1,0:T(8,128)(2,1)S(1)}, bf16[8,8,8,128]{3,2,1,0:T(8,128)(2,1)S(1)}, u32[]{:S(2)}, u32[]{:S(2)}) collective-permute-start(bf16[8,8,8,128]{3,2,1,0:T(8,128)(2,1)S(1)} %get-tuple-element.66), channel_id=1, source_target_pairs={{0,8},{1,9},{2,10},{3,11},{4,12},{5,13},{6,14},{7,15},{8,0},{9,1},... | collective-permute-start | bytes 393224 | tf_op jit(solution)/shard_map/ppermute | solution.py:671
  77.8 2.4 %collective-permute-start.11 = (bf16[8,8,8,128]{3,2,1,0:T(8,128)(2,1)S(1)}, bf16[8,8,8,128]{3,2,1,0:T(8,128)(2,1)S(1)}, u32[]{:S(2)}, u32[]{:S(2)}) collective-permute-start(bf16[8,8,8,128]{3,2,1,0:T(8,128)(2,1)S(1)} %get-tuple-element.67), channel_id=1, source_target_pairs={{0,16},{1,17},{2,18},{3,19},{4,20},{5,21},{6,22},{7,23},{8,24},{9,... | collective-permute-start | bytes 393224 | tf_op jit(solution)/shard_map/ppermute | solution.py:671
  80.2 0.2 collective-permute-start.12
  80.4 7.7 %collective-permute-done.10.refs_1_ = bf16[8,8,8,128]{3,2,1,0:T(8,128)(2,1)S(1)} collective-permute-done((bf16[8,8,8,128]{3,2,1,0:T(8,128)(2,1)S(1)}, bf16[8,8,8,128]{3,2,1,0:T(8,128)(2,1)S(1)}, u32[]{:S(2)}, u32[]{:S(2)}) %collective-permute-start.10) | collective-permute-done | bytes 131104 | tf_op jit(solution)/shard_map/ppermute | solution.py:671
  88.1 10.4 %collective-permute-done.11.refs_2_ = bf16[8,8,8,128]{3,2,1,0:T(8,128)(2,1)S(1)} collective-permute-done((bf16[8,8,8,128]{3,2,1,0:T(8,128)(2,1)S(1)}, bf16[8,8,8,128]{3,2,1,0:T(8,128)(2,1)S(1)}, u32[]{:S(2)}, u32[]{:S(2)}) %collective-permute-start.11) | collective-permute-done | bytes 131104 | tf_op jit(solution)/shard_map/ppermute | solution.py:671
  98.5 0.0 collective-permute-done.12.refs_3_
  98.5 0.1 collective-permute-start.13
  98.6 1.5 %collective-permute-start.14 = (bf16[4,8,8,128]{3,2,1,0:T(8,128)(2,1)S(1)}, bf16[4,8,8,128]{3,2,1,0:T(8,128)(2,1)S(1)}, u32[]{:S(2)}, u32[]{:S(2)}) collective-permute-start(bf16[4,8,8,128]{3,2,1,0:T(8,128)(2,1)S(1)} %get-tuple-element.71), channel_id=1, source_target_pairs={{0,2},{1,3},{2,0},{3,1},{4,6},{5,7},{6,4},{7,5},{8,10},{9,11},{10,... | collective-permute-start | bytes 196616 | tf_op jit(solution)/shard_map/ppermute | solution.py:671
  100.2 0.3 collective-permute-start.15
  100.5 1.5 %collective-permute-start.16 = (bf16[4,8,8,128]{3,2,1,0:T(8,128)(2,1)S(1)}, bf16[4,8,8,128]{3,2,1,0:T(8,128)(2,1)S(1)}, u32[]{:S(2)}, u32[]{:S(2)}) collective-permute-start(bf16[4,8,8,128]{3,2,1,0:T(8,128)(2,1)S(1)} %get-tuple-element.73), channel_id=1, source_target_pairs={{0,4},{1,5},{2,6},{3,7},{4,0},{5,1},{6,2},{7,3},{8,12},{9,13},{10,... | collective-permute-start | bytes 196616 | tf_op jit(solution)/shard_map/ppermute | solution.py:671
  101.9 0.2 collective-permute-start.17
  102.2 0.0 collective-permute-done.13.refs_1_
  102.2 2.4 %collective-permute-start.18 = (bf16[4,8,8,128]{3,2,1,0:T(8,128)(2,1)S(1)}, bf16[4,8,8,128]{3,2,1,0:T(8,128)(2,1)S(1)}, u32[]{:S(2)}, u32[]{:S(2)}) collective-permute-start(bf16[4,8,8,128]{3,2,1,0:T(8,128)(2,1)S(1)} %get-tuple-element.75), channel_id=1, source_target_pairs={{0,6},{1,7},{2,4},{3,5},{4,2},{5,3},{6,0},{7,1},{8,14},{9,15},{10,... | collective-permute-start | bytes 196616 | tf_op jit(solution)/shard_map/ppermute | solution.py:671
  104.6 0.0 collective-permute-done.14.refs_2_
  104.6 0.3 collective-permute-start.19
  104.9 1.2 %collective-permute-done.17.refs_5_ = bf16[4,8,8,128]{3,2,1,0:T(8,128)(2,1)S(1)} collective-permute-done((bf16[4,8,8,128]{3,2,1,0:T(8,128)(2,1)S(1)}, bf16[4,8,8,128]{3,2,1,0:T(8,128)(2,1)S(1)}, u32[]{:S(2)}, u32[]{:S(2)}) %collective-permute-start.17) | collective-permute-done | bytes 65568 | tf_op jit(solution)/shard_map/ppermute | solution.py:671
  106.1 2.8 %collective-permute-done.18.refs_6_ = bf16[4,8,8,128]{3,2,1,0:T(8,128)(2,1)S(1)} collective-permute-done((bf16[4,8,8,128]{3,2,1,0:T(8,128)(2,1)S(1)}, bf16[4,8,8,128]{3,2,1,0:T(8,128)(2,1)S(1)}, u32[]{:S(2)}, u32[]{:S(2)}) %collective-permute-start.18) | collective-permute-done | bytes 65568 | tf_op jit(solution)/shard_map/ppermute | solution.py:671
  108.8 1.0 collective-permute-done.19.refs_7_
  109.9 0.0 all-to-all-done.1
  109.9 2.0 %receive.1 = (bf16[4,48,2304]{2,1,0:T(8,128)(2,1)}, f32[4,100]{1,0:T(4,128)}, f32[4,100]{1,0:T(4,128)}) custom-call(s32[8,128]{1,0:T(8,128)S(1)} %get-tuple-element.40.off_lanes_ref, bf16[16,2,7,8,128]{4,3,2,1,0:T(8,128)(2,1)S(1)} %bitcast.6, bf16[4,8,8,128]{3,2,1,0:T(8,128)(2,1)S(1)} %get-tuple-element.69.refs_0_, ...), custom_call_target="tpu_custom_call" | custom-call | tf_op jit(solution)/shard_map/receive/pallas_call | solution.py:784
  (3 shorter events, 0.0 us)
Async XLA Ops:
  7.0 60.3 %all-to-all-start = ((bf16[32,17,8,128]{3,2,1,0:T(8,128)(2,1)}), bf16[32,17,8,128]{3,2,1,0:T(8,128)(2,1)S(1)}, u32[]{:S(2)}, u32[]{:S(2)}) async-start(bf16[32,17,8,128]{3,2,1,0:T(8,128)(2,1)} %bitcast.4), calls=%async_computation | async-start | bytes 2228224 | tf_op jit(solution)/shard_map/all_to_all | solution.py:724
  14.3 22.9 %collective-permute-start = (bf16[8,11,8,128]{3,2,1,0:T(8,128)(2,1)S(1)}, bf16[8,11,8,128]{3,2,1,0:T(8,128)(2,1)S(1)}, u32[]{:S(2)}, u32[]{:S(2)}) collective-permute-start(bf16[8,11,8,128]{3,2,1,0:T(8,128)(2,1)S(1)} %bitcast.10), channel_id=1, source_target_pairs={{0,8},{1,9},{2,10},{3,11},{4,12},{5,13},{6,14},{7,15},{8,0},{9,1},... | collective-permute-start | bytes 540680 | tf_op jit(solution)/shard_map/ppermute | solution.py:671
  16.1 37.9 %collective-permute-start.1 = (bf16[8,11,8,128]{3,2,1,0:T(8,128)(2,1)S(1)}, bf16[8,11,8,128]{3,2,1,0:T(8,128)(2,1)S(1)}, u32[]{:S(2)}, u32[]{:S(2)}) collective-permute-start(bf16[8,11,8,128]{3,2,1,0:T(8,128)(2,1)S(1)} %bitcast.9), channel_id=1, source_target_pairs={{0,16},{1,17},{2,18},{3,19},{4,20},{5,21},{6,22},{7,23},{8,24},{9,... | collective-permute-start | bytes 540680 | tf_op jit(solution)/shard_map/ppermute | solution.py:671
  18.5 35.5 %collective-permute-start.2 = (bf16[8,11,8,128]{3,2,1,0:T(8,128)(2,1)S(1)}, bf16[8,11,8,128]{3,2,1,0:T(8,128)(2,1)S(1)}, u32[]{:S(2)}, u32[]{:S(2)}) collective-permute-start(bf16[8,11,8,128]{3,2,1,0:T(8,128)(2,1)S(1)} %bitcast.8), channel_id=1, source_target_pairs={{0,24},{1,25},{2,26},{3,27},{4,28},{5,29},{6,30},{7,31},{8,16},{9,... | collective-permute-start | bytes 540680 | tf_op jit(solution)/shard_map/ppermute | solution.py:671
  54.1 3.6 %collective-permute-start.3 = (bf16[4,11,8,128]{3,2,1,0:T(8,128)(2,1)S(1)}, bf16[4,11,8,128]{3,2,1,0:T(8,128)(2,1)S(1)}, u32[]{:S(2)}, u32[]{:S(2)}) collective-permute-start(bf16[4,11,8,128]{3,2,1,0:T(8,128)(2,1)S(1)} %get-tuple-element.46), channel_id=1, source_target_pairs={{0,1},{1,0},{2,3},{3,2},{4,5},{5,4},{6,7},{7,6},{8,9},{9,8},{10,11... | collective-permute-start | bytes 270344 | tf_op jit(solution)/shard_map/ppermute | solution.py:671
  54.2 6.0 %collective-permute-start.4 = (bf16[4,11,8,128]{3,2,1,0:T(8,128)(2,1)S(1)}, bf16[4,11,8,128]{3,2,1,0:T(8,128)(2,1)S(1)}, u32[]{:S(2)}, u32[]{:S(2)}) collective-permute-start(bf16[4,11,8,128]{3,2,1,0:T(8,128)(2,1)S(1)} %get-tuple-element.47), channel_id=1, source_target_pairs={{0,2},{1,3},{2,0},{3,1},{4,6},{5,7},{6,4},{7,5},{8,10},{9,11},{10,... | collective-permute-start | bytes 270344 | tf_op jit(solution)/shard_map/ppermute | solution.py:671
  55.8 5.0 %collective-permute-start.5 = (bf16[4,11,8,128]{3,2,1,0:T(8,128)(2,1)S(1)}, bf16[4,11,8,128]{3,2,1,0:T(8,128)(2,1)S(1)}, u32[]{:S(2)}, u32[]{:S(2)}) collective-permute-start(bf16[4,11,8,128]{3,2,1,0:T(8,128)(2,1)S(1)} %get-tuple-element.48), channel_id=1, source_target_pairs={{0,3},{1,2},{2,1},{3,0},{4,7},{5,6},{6,5},{7,4},{8,11},{9,10},{10,... | collective-permute-start | bytes 270344 | tf_op jit(solution)/shard_map/ppermute | solution.py:671
  56.0 5.3 %collective-permute-start.6 = (bf16[4,11,8,128]{3,2,1,0:T(8,128)(2,1)S(1)}, bf16[4,11,8,128]{3,2,1,0:T(8,128)(2,1)S(1)}, u32[]{:S(2)}, u32[]{:S(2)}) collective-permute-start(bf16[4,11,8,128]{3,2,1,0:T(8,128)(2,1)S(1)} %get-tuple-element.49), channel_id=1, source_target_pairs={{0,4},{1,5},{2,6},{3,7},{4,0},{5,1},{6,2},{7,3},{8,12},{9,13},{10,... | collective-permute-start | bytes 270344 | tf_op jit(solution)/shard_map/ppermute | solution.py:671
  57.5 4.9 %collective-permute-start.7 = (bf16[4,11,8,128]{3,2,1,0:T(8,128)(2,1)S(1)}, bf16[4,11,8,128]{3,2,1,0:T(8,128)(2,1)S(1)}, u32[]{:S(2)}, u32[]{:S(2)}) collective-permute-start(bf16[4,11,8,128]{3,2,1,0:T(8,128)(2,1)S(1)} %get-tuple-element.50), channel_id=1, source_target_pairs={{0,5},{1,4},{2,7},{3,6},{4,1},{5,0},{6,3},{7,2},{8,13},{9,12},{10,... | collective-permute-start | bytes 270344 | tf_op jit(solution)/shard_map/ppermute | solution.py:671
  57.8 8.4 %collective-permute-start.8 = (bf16[4,11,8,128]{3,2,1,0:T(8,128)(2,1)S(1)}, bf16[4,11,8,128]{3,2,1,0:T(8,128)(2,1)S(1)}, u32[]{:S(2)}, u32[]{:S(2)}) collective-permute-start(bf16[4,11,8,128]{3,2,1,0:T(8,128)(2,1)S(1)} %get-tuple-element.51), channel_id=1, source_target_pairs={{0,6},{1,7},{2,4},{3,5},{4,2},{5,3},{6,0},{7,1},{8,14},{9,15},{10,... | collective-permute-start | bytes 270344 | tf_op jit(solution)/shard_map/ppermute | solution.py:671
  60.2 7.1 %collective-permute-start.9 = (bf16[4,11,8,128]{3,2,1,0:T(8,128)(2,1)S(1)}, bf16[4,11,8,128]{3,2,1,0:T(8,128)(2,1)S(1)}, u32[]{:S(2)}, u32[]{:S(2)}) collective-permute-start(bf16[4,11,8,128]{3,2,1,0:T(8,128)(2,1)S(1)} %get-tuple-element.52), channel_id=1, source_target_pairs={{0,7},{1,6},{2,5},{3,4},{4,3},{5,2},{6,1},{7,0},{8,15},{9,14},{10,... | collective-permute-start | bytes 270344 | tf_op jit(solution)/shard_map/ppermute | solution.py:671
  70.9 38.9 %all-to-all-start.1 = ((bf16[32,7,8,128]{3,2,1,0:T(8,128)(2,1)}), bf16[32,7,8,128]{3,2,1,0:T(8,128)(2,1)S(1)}, u32[]{:S(2)}, u32[]{:S(2)}) async-start(bf16[32,7,8,128]{3,2,1,0:T(8,128)(2,1)} %second.1), calls=%async_computation.1 | async-start | bytes 917504 | tf_op jit(solution)/shard_map/all_to_all | solution.py:772
  75.9 12.1 %collective-permute-start.10 = (bf16[8,8,8,128]{3,2,1,0:T(8,128)(2,1)S(1)}, bf16[8,8,8,128]{3,2,1,0:T(8,128)(2,1)S(1)}, u32[]{:S(2)}, u32[]{:S(2)}) collective-permute-start(bf16[8,8,8,128]{3,2,1,0:T(8,128)(2,1)S(1)} %get-tuple-element.66), channel_id=1, source_target_pairs={{0,8},{1,9},{2,10},{3,11},{4,12},{5,13},{6,14},{7,15},{8,0},{9,1},... | collective-permute-start | bytes 393224 | tf_op jit(solution)/shard_map/ppermute | solution.py:671
  77.8 20.7 %collective-permute-start.11 = (bf16[8,8,8,128]{3,2,1,0:T(8,128)(2,1)S(1)}, bf16[8,8,8,128]{3,2,1,0:T(8,128)(2,1)S(1)}, u32[]{:S(2)}, u32[]{:S(2)}) collective-permute-start(bf16[8,8,8,128]{3,2,1,0:T(8,128)(2,1)S(1)} %get-tuple-element.67), channel_id=1, source_target_pairs={{0,16},{1,17},{2,18},{3,19},{4,20},{5,21},{6,22},{7,23},{8,24},{9,... | collective-permute-start | bytes 393224 | tf_op jit(solution)/shard_map/ppermute | solution.py:671
  80.2 18.3 %collective-permute-start.12 = (bf16[8,8,8,128]{3,2,1,0:T(8,128)(2,1)S(1)}, bf16[8,8,8,128]{3,2,1,0:T(8,128)(2,1)S(1)}, u32[]{:S(2)}, u32[]{:S(2)}) collective-permute-start(bf16[8,8,8,128]{3,2,1,0:T(8,128)(2,1)S(1)} %get-tuple-element.68), channel_id=1, source_target_pairs={{0,24},{1,25},{2,26},{3,27},{4,28},{5,29},{6,30},{7,31},{8,16},{9,... | collective-permute-start | bytes 393224 | tf_op jit(solution)/shard_map/ppermute | solution.py:671
  98.5 3.6 %collective-permute-start.13 = (bf16[4,8,8,128]{3,2,1,0:T(8,128)(2,1)S(1)}, bf16[4,8,8,128]{3,2,1,0:T(8,128)(2,1)S(1)}, u32[]{:S(2)}, u32[]{:S(2)}) collective-permute-start(bf16[4,8,8,128]{3,2,1,0:T(8,128)(2,1)S(1)} %get-tuple-element.70), channel_id=1, source_target_pairs={{0,1},{1,0},{2,3},{3,2},{4,5},{5,4},{6,7},{7,6},{8,9},{9,8},{10,11... | collective-permute-start | bytes 196616 | tf_op jit(solution)/shard_map/ppermute | solution.py:671
  98.6 6.0 %collective-permute-start.14 = (bf16[4,8,8,128]{3,2,1,0:T(8,128)(2,1)S(1)}, bf16[4,8,8,128]{3,2,1,0:T(8,128)(2,1)S(1)}, u32[]{:S(2)}, u32[]{:S(2)}) collective-permute-start(bf16[4,8,8,128]{3,2,1,0:T(8,128)(2,1)S(1)} %get-tuple-element.71), channel_id=1, source_target_pairs={{0,2},{1,3},{2,0},{3,1},{4,6},{5,7},{6,4},{7,5},{8,10},{9,11},{10,... | collective-permute-start | bytes 196616 | tf_op jit(solution)/shard_map/ppermute | solution.py:671
  100.2 4.7 %collective-permute-start.15 = (bf16[4,8,8,128]{3,2,1,0:T(8,128)(2,1)S(1)}, bf16[4,8,8,128]{3,2,1,0:T(8,128)(2,1)S(1)}, u32[]{:S(2)}, u32[]{:S(2)}) collective-permute-start(bf16[4,8,8,128]{3,2,1,0:T(8,128)(2,1)S(1)} %get-tuple-element.72), channel_id=1, source_target_pairs={{0,3},{1,2},{2,1},{3,0},{4,7},{5,6},{6,5},{7,4},{8,11},{9,10},{10,... | collective-permute-start | bytes 196616 | tf_op jit(solution)/shard_map/ppermute | solution.py:671
  100.5 4.4 %collective-permute-start.16 = (bf16[4,8,8,128]{3,2,1,0:T(8,128)(2,1)S(1)}, bf16[4,8,8,128]{3,2,1,0:T(8,128)(2,1)S(1)}, u32[]{:S(2)}, u32[]{:S(2)}) collective-permute-start(bf16[4,8,8,128]{3,2,1,0:T(8,128)(2,1)S(1)} %get-tuple-element.73), channel_id=1, source_target_pairs={{0,4},{1,5},{2,6},{3,7},{4,0},{5,1},{6,2},{7,3},{8,12},{9,13},{10,... | collective-permute-start | bytes 196616 | tf_op jit(solution)/shard_map/ppermute | solution.py:671
  101.9 4.1 %collective-permute-start.17 = (bf16[4,8,8,128]{3,2,1,0:T(8,128)(2,1)S(1)}, bf16[4,8,8,128]{3,2,1,0:T(8,128)(2,1)S(1)}, u32[]{:S(2)}, u32[]{:S(2)}) collective-permute-start(bf16[4,8,8,128]{3,2,1,0:T(8,128)(2,1)S(1)} %get-tuple-element.74), channel_id=1, source_target_pairs={{0,5},{1,4},{2,7},{3,6},{4,1},{5,0},{6,3},{7,2},{8,13},{9,12},{10,... | collective-permute-start | bytes 196616 | tf_op jit(solution)/shard_map/ppermute | solution.py:671
  102.2 6.7 %collective-permute-start.18 = (bf16[4,8,8,128]{3,2,1,0:T(8,128)(2,1)S(1)}, bf16[4,8,8,128]{3,2,1,0:T(8,128)(2,1)S(1)}, u32[]{:S(2)}, u32[]{:S(2)}) collective-permute-start(bf16[4,8,8,128]{3,2,1,0:T(8,128)(2,1)S(1)} %get-tuple-element.75), channel_id=1, source_target_pairs={{0,6},{1,7},{2,4},{3,5},{4,2},{5,3},{6,0},{7,1},{8,14},{9,15},{10,... | collective-permute-start | bytes 196616 | tf_op jit(solution)/shard_map/ppermute | solution.py:671
  104.6 5.3 %collective-permute-start.19 = (bf16[4,8,8,128]{3,2,1,0:T(8,128)(2,1)S(1)}, bf16[4,8,8,128]{3,2,1,0:T(8,128)(2,1)S(1)}, u32[]{:S(2)}, u32[]{:S(2)}) collective-permute-start(bf16[4,8,8,128]{3,2,1,0:T(8,128)(2,1)S(1)} %get-tuple-element.76), channel_id=1, source_target_pairs={{0,7},{1,6},{2,5},{3,4},{4,3},{5,2},{6,1},{7,0},{8,15},{9,14},{10,... | collective-permute-start | bytes 196616 | tf_op jit(solution)/shard_map/ppermute | solution.py:671
